TPU v7x, 32 devices: a whole 2x2x4 slice. The times are simulated.
32 devices in a mesh: groups: 2 (over x), space: 4 (over y, core), pair: 4 (over z).
Axes of the slice: x: 2, y: 2, z: 4, core: 2. Of those that a mesh axis runs over, the one named last changes fastest.
Arguments:
- source_feats: bfloat16 [8, 64, 128, 256], P(('groups', 'pair'), 'space'), parts along dimension 0, may hold values from -46.1 to 46.1
- edit_feats: bfloat16 [8, 64, 128, 256], P(('groups', 'pair'), 'space'), parts along dimension 0, may hold values from -60 to 60
- conv_weight: bfloat16 [128, 289], replicated, may hold values from -0.375 to 0.375
- conv_bias: float32 [128], replicated, may hold values from -3 to 3
- head_weight: float32 [128], replicated, may hold values from -4 to 4
- comp_first: int32 [32], P('groups'), parts along dimension 0, may hold values from 0 to 3
- comp_second: int32 [32], P('groups'), parts along dimension 0, may hold values from 0 to 3
- comp_win: int32 [32], P('groups'), parts along dimension 0, may hold values 0 or 1
Outputs:
- grad_source: bfloat16 [8, 64, 128, 256], P(('groups', 'pair'), 'space'), parts along dimension 0
- grad_edit: bfloat16 [8, 64, 128, 256], P(('groups', 'pair'), 'space'), parts along dimension 0
- grad_conv: float32 [256, 289], P('groups'), parts along dimension 0
- grad_bias: float32 [256], P('groups'), parts along dimension 0
- grad_head: float32 [256], P('groups'), parts along dimension 0
- loss_mean: float32 [2], P('groups'), parts along dimension 0
There are 2 independent parts, one for each index of `groups`. A program takes and returns all parts, laid end to end along the dimension named above; an argument that names none is the same for every part. Nothing has to cross between parts.
All inputs are finite; a program needn't handle non-finite values.
Results may differ from a plain program's by a relative error of at most 0.0076.
Values may be sent and summed in bfloat16 or wider, within the bound.
No kernel may reach another device: no remote copies, remote signals or barrier semaphores. Data moves between devices by JAX's collectives and lax.ppermute only.
A program may use at most 64 MiB of HBM per device.

v0:
```python
import math

import jax
import jax.numpy as jnp
from jax import lax
from jax.sharding import PartitionSpec as P

RADIUS = 8


def extended(block, sides, width):
    for axis, dim in sides:
        count = lax.axis_size(axis)
        forward = [(i, i + 1) for i in range(count - 1)]
        backward = [(target, source) for source, target in forward]
        low = lax.ppermute(
            lax.slice_in_dim(block, block.shape[dim] - width, None, axis=dim), axis, forward
        )
        high = lax.ppermute(lax.slice_in_dim(block, 0, width, axis=dim), axis, backward)
        block = jnp.concatenate([low, block, high], axis=dim)
    return block


def band_table(columns, span_len):
    full_len = columns + span_len - 1
    padded_ids = jnp.arange(full_len, dtype=jnp.int32)[None, :, None]
    column_ids = jnp.arange(columns, dtype=jnp.int32)[None, None, :]
    shift_ids = jnp.arange(span_len, dtype=jnp.int32)[:, None, None]
    return (padded_ids == column_ids + shift_ids).astype(jnp.float32)


def correlate(source, edit_pad, inv_root):
    pairs_here, rows_here, columns = source.shape[:3]
    span_len = edit_pad.shape[1] - rows_here + 1
    table = band_table(columns, span_len)

    def one_shift(carry, offset):
        window = lax.dynamic_slice_in_dim(edit_pad, offset, rows_here, 1)
        matrix = jnp.einsum("pyjc,pyxc->pyjx", window, source, preferred_element_type=jnp.float32)
        banded = jnp.sum(matrix[:, :, None, :, :] * table[None, None], axis=3)
        block = (banded * inv_root).astype(jnp.bfloat16)
        carry = lax.dynamic_update_slice_in_dim(carry, block, offset * span_len, 2)
        return (carry, None)

    init = jnp.zeros((pairs_here, rows_here, span_len * span_len, columns), jnp.bfloat16)
    result, ignored = lax.scan(one_shift, init, jnp.arange(span_len, dtype=jnp.int32))
    return result


def correlate_back(corr_grad, source, edit_pad):
    pairs_here, rows_here, disp_len, columns = corr_grad.shape
    span_len = math.isqrt(disp_len)
    full_len = columns + span_len - 1
    channels = source.shape[-1]
    table = band_table(columns, span_len)

    def one_shift(totals, offset):
        edit_total, source_total = totals
        block = lax.dynamic_slice_in_dim(corr_grad, offset * span_len, span_len, 2).astype(
            jnp.float32
        )
        matrix = jnp.sum(block[:, :, :, None, :] * table[None, None], axis=2).astype(jnp.bfloat16)
        contrib = jnp.einsum("pyjx,pyxc->pyjc", matrix, source, preferred_element_type=jnp.float32)
        current = lax.dynamic_slice_in_dim(edit_total, offset, rows_here, 1)
        edit_total = lax.dynamic_update_slice_in_dim(edit_total, current + contrib, offset, 1)
        window = lax.dynamic_slice_in_dim(edit_pad, offset, rows_here, 1)
        source_total = source_total + jnp.einsum(
            "pyjx,pyjc->pyxc", matrix, window, preferred_element_type=jnp.float32
        )
        return ((edit_total, source_total), None)

    edit_rows_count = rows_here + span_len - 1
    edit_init = jnp.zeros((pairs_here, edit_rows_count, full_len, channels), jnp.float32)
    source_init = jnp.zeros((pairs_here, rows_here, columns, channels), jnp.float32)
    (edit_total, source_total), ignored = lax.scan(
        one_shift, (edit_init, source_init), jnp.arange(span_len, dtype=jnp.int32)
    )
    return (edit_total, source_total)


def local(
    source_feats, edit_feats, conv_weight, conv_bias, head_weight, comp_first, comp_second, comp_win
):
    pairs_here, rows_here, columns, channels = source_feats.shape
    inv_root = channels ** (-0.5)
    edit_rows = extended(edit_feats, (("space", 1),), RADIUS)
    edit_pad = jnp.pad(edit_rows, ((0, 0), (0, 0), (RADIUS, RADIUS), (0, 0)))
    correlation = correlate(source_feats, edit_pad, inv_root)
    preact = (
        jnp.einsum("kd,pydx->pykx", conv_weight, correlation, preferred_element_type=jnp.float32)
        + conv_bias[None, None, :, None]
    )
    gating = jax.nn.sigmoid(preact)
    hidden_act = preact * gating
    pixels = rows_here * lax.axis_size("space") * columns
    partial_value = jnp.sum(hidden_act * head_weight[None, None, :, None], axis=(1, 2, 3)) / pixels
    pair_start = lax.axis_index("pair") * pairs_here
    total_pairs = pairs_here * lax.axis_size("pair")
    own_scores = lax.psum(partial_value, "space")
    scores = lax.all_gather(own_scores, "pair", axis=0, tiled=True)
    pair_ids = jnp.arange(total_pairs, dtype=jnp.int32)
    first_hot = (comp_first[:, None] == pair_ids[None, :]).astype(jnp.float32)
    second_hot = (comp_second[:, None] == pair_ids[None, :]).astype(jnp.float32)
    margin = jnp.sum((first_hot - second_hot) * scores[None, :], axis=1)
    win_sign = 2.0 * comp_win.astype(jnp.float32) - 1.0
    loss_mean = jnp.reshape(jnp.mean(jax.nn.softplus(-win_sign * margin)), (1,))
    margin_grad = -win_sign * jax.nn.sigmoid(-win_sign * margin)
    score_grad = jnp.sum(margin_grad[:, None] * (first_hot - second_hot), axis=0)
    own_grad = lax.dynamic_slice_in_dim(score_grad, pair_start, pairs_here, 0)
    silu_slope = gating * (1.0 + preact * (1.0 - gating))
    pre_grad = own_grad[:, None, None, None] * head_weight[None, None, :, None] * silu_slope
    pre_rounded = pre_grad.astype(jnp.bfloat16)
    bias_grad = jnp.sum(pre_grad, axis=(0, 1, 3)) / pixels
    head_grad = jnp.sum(own_grad[:, None, None, None] * hidden_act, axis=(0, 1, 3)) / pixels
    conv_grad = (
        jnp.einsum("pykx,pydx->kd", pre_rounded, correlation, preferred_element_type=jnp.float32)
        / pixels
    )
    corr_grad = jnp.einsum(
        "kd,pykx->pydx", conv_weight, pre_rounded, preferred_element_type=jnp.float32
    ).astype(jnp.bfloat16)
    edit_total, source_total = correlate_back(corr_grad, source_feats, edit_pad)
    middle = edit_total[:, :, RADIUS : RADIUS + columns]
    rim_terms = jnp.concatenate((middle[:, :RADIUS], middle[:, RADIUS + rows_here :]), axis=1)
    arrived = extended(rim_terms.astype(jnp.bfloat16), (("space", 1),), RADIUS).astype(
        rim_terms.dtype
    )
    edit_sum = middle[:, RADIUS : RADIUS + rows_here]
    edit_sum = edit_sum.at[:, :RADIUS].add(arrived[:, :RADIUS])
    edit_sum = edit_sum.at[:, rows_here - RADIUS :].add(arrived[:, 3 * RADIUS :])
    conv_total, bias_total, head_total = lax.psum(
        (conv_grad, bias_grad, head_grad), ("space", "pair")
    )
    return (
        (source_total * inv_root).astype(jnp.bfloat16),
        (edit_sum * inv_root).astype(jnp.bfloat16),
        conv_total,
        bias_total,
        head_total,
        loss_mean,
    )


def solution(mesh):
    in_specs = (
        P(("groups", "pair"), "space", None, None),
        P(("groups", "pair"), "space", None, None),
        P(),
        P(),
        P(),
        P("groups"),
        P("groups"),
        P("groups"),
    )
    out_specs = (
        P(("groups", "pair"), "space", None, None),
        P(("groups", "pair"), "space", None, None),
        P("groups", None),
        P("groups"),
        P("groups"),
        P("groups"),
    )
    return jax.shard_map(local, mesh=mesh, in_specs=in_specs, out_specs=out_specs, check_vma=False)
```

profile of v0, /device:TPU:0, one launch (start us, length us, event | category | flops | bytes accessed | tf_op | source)
XLA Modules:
  0.0 483.7 jit_solution(8210158073045697157)
XLA Ops:
  13.7 3.3 collective-permute-done.1
  19.9 160.9 %while.26 = (s32[]{:T(128)}, bf16[1,16,289,128]{3,2,1,0:T(8,128)(2,1)}, s32[17]{0:T(128)S(1)}, bf16[1,32,144,256]{3,2,1,0:T(8,128)(2,1)S(1)}, bf16[1,16,128,256]...) while((s32[]{:T(128)}, ...), condition=%wide.region_2.3_spmd.clone, body=%wide.region_0.2_spmd.clone.sunk | while | flops 161683456 | bytes 7590617 | solution.py:46
  23.6 3.3 multiply_reduce_fusion.8
  33.1 3.3 multiply_reduce_fusion.8
  42.6 3.3 multiply_reduce_fusion.8
  52.1 3.3 multiply_reduce_fusion.8
  61.6 3.3 multiply_reduce_fusion.8
  71.1 3.3 multiply_reduce_fusion.8
  80.6 3.3 multiply_reduce_fusion.8
  90.0 3.3 multiply_reduce_fusion.8
  99.5 3.3 multiply_reduce_fusion.8
  109.0 3.3 multiply_reduce_fusion.8
  118.4 3.3 multiply_reduce_fusion.8
  127.9 3.3 multiply_reduce_fusion.8
  137.3 3.3 multiply_reduce_fusion.8
  146.8 3.3 multiply_reduce_fusion.8
  156.2 3.3 multiply_reduce_fusion.8
  165.7 3.3 multiply_reduce_fusion.8
  175.2 3.3 multiply_reduce_fusion.8
  180.9 3.6 multiply_reduce_fusion.3
  185.1 13.9 %psum.28 = f32[1]{0:T(128)} all-reduce(f32[1]{0:T(128)} %bitcast.4), channel_id=1, replica_groups=mesh['groups'=2,'space'=4,'pair'=4] {'space'}, use_global_device_ids=true, to_apply=%region_4.5 | all-reduce | flops 1 | bytes 8 | tf_op jit(solution)/shard_map/psum | solution.py:99
  200.5 11.9 %all-reduce.1 = f32[4]{0:T(128)S(1)} all-reduce(f32[4]{0:T(128)S(1)} %dynamic-update-slice.6), channel_id=1, replica_groups=mesh['groups'=2,'space'=4,'pair'=4] {'pair'}, use_global_device_ids=true, to_apply=%add.1 | all-reduce | flops 4 | bytes 32
  225.4 199.0 %while.27 = (s32[]{:T(128)}, f32[1,32,144,256]{3,2,1,0:T(8,128)}, f32[1,16,128,256]{3,2,1,0:T(8,128)}, s32[17]{0:T(128)S(1)}, bf16[1,16,289,128]{3,2,1,0:T(8,128...) while((s32[]{:T(128)}, f32[1,32,144,256]{3,2,1,0:T(8,128)}, ...), condition=%wide.region_9.10_spmd.clone, body=%wide.region_7.9_spmd.clone.sunk | while | flops 314021888 | bytes 70300512 | solution.py:75
  434.4 32.5 %all-reduce.2 = (f32[128]{0:T(128)}, f32[128]{0:T(128)}) all-reduce(f32[128]{0:T(128)S(1)} %get-tuple-element.194, f32[128]{0:T(128)S(1)} %get-tuple-element.193), channel_id=1, replica_groups=mesh['groups'=2,'space'=4,'pair'=4] {'space','pair'}, use_global_device_ids=true, to_apply=%region_12.13 | all-reduce | flops 256 | bytes 2048 | tf_op jit(solution)/shard_map/psum | solution.py:131
  (383 shorter events, 255.7 us)
Async XLA Ops:
  7.2 173.7 %copy-start = (bf16[128,289]{0,1:T(8,128)(2,1)S(1)}, bf16[128,289]{0,1:T(8,128)(2,1)}, u32[]{:S(2)}) copy-start(bf16[128,289]{0,1:T(8,128)(2,1)} %param.18) | copy-start | bytes 221956
  7.2 5.1 %copy-start.14 = (u32[32]{0:T(128)S(1)}, u32[32]{0:T(128)}, u32[]{:S(2)}) copy-start(u32[32]{0:T(128)} %constant.127) | copy-start | bytes 388
  7.2 466.9 %all-reduce.5.cloned.1.call-start = ((), (), s32[]{:S(2)}) async-start(), calls=%async_computation | async-start | bytes 303104 | tf_op jit(solution)/shard_map/psum | solution.py:131
  8.5 4.3 collective-permute-start
  10.9 6.0 %collective-permute-start.1 = (bf16[1,8,128,256]{3,2,1,0:T(8,128)(2,1)S(1)}, bf16[1,8,128,256]{3,2,1,0:T(8,128)(2,1)}, u32[]{:S(2)}, u32[]{:S(2)}) collective-permute-start(bf16[1,8,128,256]{3,2,1,0:T(8,128)(2,1)S(1)} %get-tuple-element.188), channel_id=1, source_target_pairs={{4,0},{8,4},{12,8},{5,1},{9,5},{13,9},{6,2},{10,6},{14,10},{7,3},{... | collective-permute-start | bytes 1572872 | tf_op jit(solution)/shard_map/ppermute | solution.py:19
  12.9 7.0 %copy-start.1 = (bf16[1,16,128,256]{3,2,1,0:T(8,128)(2,1)S(1)}, bf16[1,16,128,256]{3,2,1,0:T(8,128)(2,1)}, u32[]{:S(2)}) copy-start(bf16[1,16,128,256]{3,2,1,0:T(8,128)(2,1)} %param.16) | copy-start | bytes 3145732
  19.9 161.0 %copy-start.12 = (f32[128]{0:T(128)S(1)}, f32[128]{0:T(128)}, u32[]{:S(2)}) copy-start(f32[128]{0:T(128)} %param.19) | copy-start | bytes 1540
  19.9 161.0 %copy-start.13 = (f32[128]{0:T(128)S(1)}, f32[128]{0:T(128)}, u32[]{:S(2)}) copy-start(f32[128]{0:T(128)} %param.20) | copy-start | bytes 1540
  180.9 31.5 %copy-start.9 = (s32[16]{0:T(128)S(1)}, s32[16]{0:T(128)}, u32[]{:S(2)}) copy-start(s32[16]{0:T(128)} %param.22) | copy-start | bytes 196
  180.9 31.5 %copy-start.10 = (s32[16]{0:T(128)S(1)}, s32[16]{0:T(128)}, u32[]{:S(2)}) copy-start(s32[16]{0:T(128)} %param.21) | copy-start | bytes 196
  180.9 31.6 %copy-start.11 = (s32[16]{0:T(128)S(1)}, s32[16]{0:T(128)}, u32[]{:S(2)}) copy-start(s32[16]{0:T(128)} %param.23) | copy-start | bytes 196
  240.3 2.7 copy-start.4
  252.0 2.7 copy-start.4
  263.7 2.7 copy-start.4
  275.4 2.7 copy-start.4
  287.1 2.7 copy-start.4
  298.9 2.7 copy-start.4
  310.6 2.7 copy-start.4
  334.0 2.7 copy-start.4
  345.7 2.7 copy-start.4
  357.4 2.7 copy-start.4
  427.1 42.4 %collective-permute-start.2 = (bf16[1,8,128,256]{3,2,1,0:T(8,128)(2,1)}, bf16[1,8,128,256]{3,2,1,0:T(8,128)(2,1)}, u32[]{:S(2)}, u32[]{:S(2)}) collective-permute-start(bf16[1,8,128,256]{3,2,1,0:T(8,128)(2,1)} %get-tuple-element.185), channel_id=1, source_target_pairs={{0,4},{4,8},{8,12},{1,5},{5,9},{9,13},{2,6},{6,10},{10,14},{3,7},{... | collective-permute-start | bytes 1572872 | tf_op jit(solution)/shard_map/ppermute | solution.py:16
  429.1 40.3 %collective-permute-start.3 = (bf16[1,8,128,256]{3,2,1,0:T(8,128)(2,1)}, bf16[1,8,128,256]{3,2,1,0:T(8,128)(2,1)}, u32[]{:S(2)}, u32[]{:S(2)}) collective-permute-start(bf16[1,8,128,256]{3,2,1,0:T(8,128)(2,1)} %get-tuple-element.186), channel_id=1, source_target_pairs={{4,0},{8,4},{12,8},{5,1},{9,5},{13,9},{6,2},{10,6},{14,10},{7,3},{... | collective-permute-start | bytes 1572872 | tf_op jit(solution)/shard_map/ppermute | solution.py:19
  433.6 34.6 %copy-start.6 = (f32[1,16,128,256]{3,2,1,0:T(8,128)S(1)}, f32[1,16,128,256]{3,2,1,0:T(8,128)}, u32[]{:S(2)}) copy-start(f32[1,16,128,256]{3,2,1,0:T(8,128)} %get-tuple-element.106) | copy-start | bytes 6291460
  (60 other events, 120.7 us)
Sparse Core Ops, SparseCore 0:
  222.9 86.0 all-reduce.4
where the time goes:
time: 487 us; the launch traced here: 484 us
  local copies, waits for them, and re-layouts  138 us (28%)
  other arithmetic  127 us (26%)
  loops' own time  89.3 us (18%)
  blocking collectives  58.3 us (12%)
  matrix products  44.5 us (9%)
  between operations  16.8 us (3%)
  starting transfers between devices  7.08 us (1%)
    while x136, local copies, waits for them, and re-layouts  71.9 us
    reduce_sum x17, other arithmetic, one_shift(): banded = jnp.sum(matrix[:, :, None, :, :] * table[None, None], axis=3)  56.6 us
    another operation x1, loops' own time, correlate_back(): lax.scan(one_shift, (edit_init, source_init), jnp.arange(span_len, dtype=...  45 us
    another operation x1, loops' own time, correlate(): lax.scan(one_shift, init, jnp.arange(span_len, dtype=jnp.int32))  44.4 us
    psum x1, blocking collectives, local(): lax.psum((conv_grad, bias_grad, head_grad), ('space', 'pair'))  32.5 us
    dynamic_update_slice x17, local copies, waits for them, and re-layouts, one_shift(): carry = lax.dynamic_update_slice_in_dim(carry, block, offset * span_len, 2)  29.3 us
    reduce_sum x17, other arithmetic, one_shift(): jnp.sum(block[:, :, :, None, :] * table[None, None], axis=2)  25.2 us
    dynamic_slice x34, local copies, waits for them, and re-layouts, correlate(): lax.scan(one_shift, init, jnp.arange(span_len, dtype=jnp.int32))  19.8 us
  transfers between devices with their start and end apart: 5, of which 1 were waited for; matrix products, arithmetic and copies ran while one was open for 20% of the time, Pallas kernels for 0%

commit v1 on v0

v1 whole, which is shorter than its diff:
```python
import functools

import jax
import jax.numpy as jnp
from jax import lax
from jax.experimental import pallas as pl
from jax.experimental.pallas import tpu as pltpu
from jax.sharding import PartitionSpec as P

RADIUS = 8
SPAN = 2 * RADIUS + 1
GROUP = 16
WIN = GROUP + 2 * RADIUS
LANES = 128
PER = LANES // WIN
POS = 5
STAT = SPAN * SPAN
F32 = jnp.float32
BF16 = jnp.bfloat16
VMEM_LIMIT = 24 * 1024 * 1024


def nt(a, b):
    return lax.dot_general(a, b, (((1,), (1,)), ((), ())), preferred_element_type=F32)


def nn(a, b):
    return lax.dot_general(a, b, (((1,), (0,)), ((), ())), preferred_element_type=F32)


def tn(a, b):
    return lax.dot_general(a, b, (((0,), (0,)), ((), ())), preferred_element_type=F32)


def iota(shape, dim):
    return lax.broadcasted_iota(jnp.int32, shape, dim)


def mirror(size):
    row, col = iota((size, size), 0), iota((size, size), 1)
    return (col == (row ^ (GROUP - 1))).astype(F32).astype(BF16)


def spread_table(rows):
    row, lane = iota((rows, POS * LANES), 0), iota((rows, POS * LANES), 1)
    dy, t = lane // WIN, lane % WIN
    hit = (row == dy * SPAN + t) & (t < SPAN) & (dy < SPAN)
    return hit.astype(F32).astype(BF16)


def skew(values, shift):
    return pltpu.roll(values, shift, 2, stride=1, stride_axis=1)


def skew_wide(values, shift):
    parts = []
    for start in range(0, values.shape[-1], LANES):
        parts.append(skew(values[:, :, start : start + LANES], shift))
    return parts


def fill_columns(pad_ref, row, rows, cols):
    zero = jnp.zeros((rows, RADIUS, pad_ref.shape[2]), BF16)
    pad_ref[row : row + rows, 0:RADIUS] = zero
    pad_ref[row : row + rows, RADIUS + cols :] = zero


def fill_padded(pad_ref, row, block_ref):
    rows, cols = block_ref.shape[:2]
    fill_columns(pad_ref, row, rows, cols)
    pad_ref[row : row + rows, RADIUS : RADIUS + cols] = block_ref[...]


def fill_halos(pad_ref, low, high, across_ref, beyond_ref, parts):
    me = lax.axis_index("space")
    odd = lax.rem(me, 2) == 1
    cols = across_ref.shape[1]
    for row, edge, mine in ((low, 0, odd), (high, parts - 1, ~odd)):
        fill_columns(pad_ref, row, 8, cols)
        at = (slice(row, row + 8), slice(RADIUS, RADIUS + cols))

        @pl.when(me == edge)
        def _():
            pad_ref[at] = jnp.zeros(across_ref.shape, BF16)

        @pl.when((me != edge) & mine)
        def _():
            pad_ref[at] = across_ref[...]

        @pl.when((me != edge) & ~mine)
        def _():
            pad_ref[at] = beyond_ref[...]


def window(pad_ref, row, rows, g):
    block = pad_ref[row : row + rows, g * GROUP : g * GROUP + WIN, :]
    return block.reshape(rows * WIN, block.shape[2])


def correlate_set(lhs, pad_ref, row, g, inv_root, out_ref, y0, lane):
    ys = lhs.shape[0] // GROUP
    scores = nt(lhs, window(pad_ref, row, 8, g)) * inv_root
    scores = scores.reshape(ys, GROUP, 8 * WIN)
    for i, part in enumerate(skew_wide(scores, LANES - GROUP + 1)):
        at = lane + i * LANES
        out_ref[y0 : y0 + ys, g, :, at : at + LANES] = part.astype(BF16)


def inner_kernel(inv_root, source_ref, edit_ref, weight_ref, turned_ref, corr_ref, wide_ref, pad):
    rows, groups, _, chan = source_ref.shape
    fill_padded(pad, 0, edit_ref)
    table = spread_table(SPAN * SPAN)
    base = tn(weight_ref[...], table)
    for r in range(PER):
        wide_ref[r] = (base if r == 0 else pltpu.roll(base, r * WIN, 1)).astype(BF16)
    turn = mirror(rows * GROUP)

    def body(g, carry):
        block = source_ref[:, g].reshape(rows * GROUP, chan)
        lhs = nn(turn, block).astype(BF16)
        turned_ref[:, g] = lhs.reshape(rows, GROUP, chan)
        for s in range(rows // 8):
            correlate_set(lhs, pad, 8 * s, g, inv_root, corr_ref, 0, 2 * s * LANES)
        return carry

    for g in range(groups):
        body(g, 0)


def row_chunks(rim_lo, corr_ref, rim_hi, r, rows):
    pieces = []
    half = rows // 2
    for q in range(rows // PER):
        y = q * PER + r
        parts = []
        for c in range(q, q + POS):
            if c < 2:
                part = rim_lo[y, :, :, c * LANES : (c + 1) * LANES]
            elif c < 2 + rows // PER:
                part = corr_ref[y, :, :, (c - 2) * LANES : (c - 1) * LANES]
            else:
                at = c - 2 - rows // PER
                part = rim_hi[y - half, :, :, at * LANES : (at + 1) * LANES]
            parts.append(part.reshape(part.shape[0] * part.shape[1], LANES))
        pieces.append(jnp.concatenate(parts, axis=1))
    return jnp.concatenate(pieces, axis=0)


def outer_kernel(
    inv_root,
    pixels,
    parts,
    turned_ref,
    corr_ref,
    across_ref,
    beyond_ref,
    wide_ref,
    bias_ref,
    head_ref,
    *rest,
):
    gate_ref = rest[0]
    piece_refs = rest[1 : 1 + parts]
    pad, rim_lo, rim_hi, stage = rest[1 + parts :]
    rows, groups, _, chan = turned_ref.shape
    half = rows // 2
    fill_halos(pad, 0, 8, across_ref, beyond_ref, parts)

    def body(g, carry):
        lhs = turned_ref[:half, g].reshape(half * GROUP, chan)
        correlate_set(lhs, pad, 0, g, inv_root, rim_lo, 0, 0)
        lhs = turned_ref[half:, g].reshape(half * GROUP, chan)
        correlate_set(lhs, pad, 8, g, inv_root, rim_hi, 0, 0)
        return carry

    for g in range(groups):
        body(g, 0)

    bias, head = bias_ref[...], head_ref[...]
    kout = bias.shape[1]
    cols = groups * GROUP
    turn = mirror(cols)
    hidden = jnp.zeros((1, kout), F32)
    slopes = jnp.zeros((1, kout), F32)
    total = None
    for r in range(PER):
        corr = row_chunks(rim_lo, corr_ref, rim_hi, r, rows)
        value = nt(corr, wide_ref[r]) + bias
        gating = jax.nn.sigmoid(value)
        act = value * gating
        slope = gating * (1.0 + value * (1.0 - gating))
        hidden = hidden + jnp.sum(act, axis=0, keepdims=True)
        slopes = slopes + jnp.sum(slope, axis=0, keepdims=True)
        pre = (slope * head).astype(BF16)
        for q in range(rows // PER):
            gate_ref[q * PER + r] = nn(turn, pre[q * cols : (q + 1) * cols]).astype(BF16)
        grad = tn(pre, corr)
        if r:
            grad = pltpu.roll(grad, POS * LANES - r * WIN, 1)
        total = grad if total is None else total + grad
    share = stage.shape[0] // parts
    table = spread_table(stage.shape[0])
    first = total.astype(BF16)
    left = total - first.astype(F32)
    second = left.astype(BF16)
    third = (left - second.astype(F32)).astype(BF16)
    packed = nt(table, first) + nt(table, second) + nt(table, third)
    scale = 1.0 / pixels
    stage[...] = packed * scale
    stage[STAT : STAT + 1] = head * slopes * scale
    stage[STAT + 1 : STAT + 2] = hidden * scale
    score = jnp.sum(hidden * head, axis=1, keepdims=True) * scale
    me = lax.axis_index("space")
    for k in range(parts):
        start = pl.multiple_of(lax.rem(me + k, parts) * share, 8)
        piece_refs[k][:share] = stage[pl.ds(start, share), :]
        piece_refs[k][share:] = jnp.broadcast_to(score, (8, kout))


def back_chunks(gate_ref, wide_ref, r, rows, groups):
    quarter = rows // PER
    lhs = jnp.concatenate([gate_ref[q * PER + r] for q in range(quarter)], axis=0)
    out = []
    for pos in range(POS):
        grad = nn(lhs, wide_ref[r, :, pos * LANES : (pos + 1) * LANES])
        grad = skew(grad.reshape(quarter * groups, GROUP, LANES), 0)
        out.append(grad.astype(BF16).reshape(quarter, groups, GROUP, LANES))
    return out


def rim_kernel(gate_ref, wide_ref, source_ref, across_ref, beyond_ref, band_lo, band_hi, sums):
    rows, groups, _, chan = source_ref.shape
    half = rows // 2
    quarter = rows // PER
    zero = jnp.zeros((groups, GROUP, LANES), BF16)
    for r in range(PER):
        for q in range(quarter):
            y = q * PER + r
            for c in (0, 1, 6, 7):
                pos = c - q
                band, row = (band_lo, y) if c < 2 else (band_hi, y - half)
                if not 0 <= row < half:
                    continue
                at = (c if c < 2 else c - 6) * LANES
                if 0 <= pos < POS:
                    grad = nn(gate_ref[y], wide_ref[r, :, pos * LANES : (pos + 1) * LANES])
                    part = skew(grad.reshape(groups, GROUP, LANES), 0).astype(BF16)
                else:
                    part = zero
                band[row, :, :, at : at + LANES] = part
    sums[...] = jnp.zeros(sums.shape, F32)

    def body(g, carry):
        start = g * GROUP
        for i, band in enumerate((band_lo, band_hi)):
            lhs = band[:, g].reshape(half * GROUP, 2 * LANES)
            rhs = source_ref[i * half : (i + 1) * half, g].reshape(half * GROUP, chan)
            grad = tn(lhs, rhs).reshape(8, WIN, chan)
            sums[8 * i : 8 * i + 8, start : start + WIN, :] += grad
        return carry

    for g in range(groups):
        body(g, 0)
    cols = groups * GROUP
    odd = lax.rem(lax.axis_index("space"), 2)
    low = pl.multiple_of(8 * odd, 8)
    high = pl.multiple_of(8 - 8 * odd, 8)
    across_ref[...] = sums[pl.ds(high, 8), RADIUS : RADIUS + cols].astype(BF16)
    beyond_ref[...] = sums[pl.ds(low, 8), RADIUS : RADIUS + cols].astype(BF16)


def back_kernel(
    parts,
    gate_ref,
    wide_ref,
    source_ref,
    edit_ref,
    across_ref,
    beyond_ref,
    source_out,
    edit_out,
    pad,
    band,
    sums,
):
    rows, groups, _, chan = source_ref.shape
    half = rows // 2
    quarter = rows // PER
    fill_halos(pad, 0, 8 + rows, across_ref, beyond_ref, parts)
    fill_padded(pad, 8, edit_ref)
    zero = jnp.zeros((PER, groups, GROUP, LANES), BF16)
    for q, c in ((1, 0), (3, 2), (0, 5), (2, 7)):
        band[q * PER : (q + 1) * PER, :, :, c * LANES : (c + 1) * LANES] = zero
    for r in range(PER):
        for pos, part in enumerate(back_chunks(gate_ref, wide_ref, r, rows, groups)):
            for q in range(quarter):
                at = (q + pos) * LANES
                band[q * PER + r, :, :, at : at + LANES] = part[q]
    sums[...] = jnp.zeros(sums.shape, F32)

    def body(g, carry):
        start = g * GROUP
        rhs = source_ref[:, g].reshape(rows * GROUP, chan)
        for s in range(rows // 8):
            at = (2 + 2 * s) * LANES
            lhs = band[:, g, :, at : at + 2 * LANES].reshape(rows * GROUP, 2 * LANES)
            grad = tn(lhs, rhs).reshape(8, WIN, chan)
            sums[8 * s : 8 * s + 8, start : start + WIN, :] += grad
        for i in range(2):
            at = i * 2 * LANES
            lhs = band[i * half : (i + 1) * half, g, :, at : at + 6 * LANES]
            grad = nn(lhs.reshape(half * GROUP, 6 * LANES), window(pad, 8 * i, 24, g))
            source_out[i * half : (i + 1) * half, g] = grad.reshape(half, GROUP, chan)
        return carry

    for g in range(groups):
        body(g, 0)
    cols = groups * GROUP
    edit_out[...] = sums[:, RADIUS : RADIUS + cols]


def judge_kernel(pairs, comp_ref, *rest):
    piece_refs = rest[:pairs]
    total_ref, grad_ref, loss_ref = rest[pairs:]
    share = total_ref.shape[0]
    me = lax.axis_index("pair")
    first, second, win = comp_ref[0:1], comp_ref[1:2], comp_ref[2:3]
    hots, margin = [], jnp.zeros(first.shape, F32)
    for k in range(pairs):
        pid = lax.rem(me - k + pairs, pairs)
        hot = (first == pid).astype(F32) - (second == pid).astype(F32)
        score = piece_refs[k][share : share + 1, 0:1]
        margin = margin + hot * score
        hots.append(hot)
    sign = 2.0 * win.astype(F32) - 1.0
    loss = jnp.mean(jax.nn.softplus(-sign * margin), axis=1, keepdims=True)
    loss_ref[...] = jnp.broadcast_to(loss, loss_ref.shape)
    margin_grad = -sign * jax.nn.sigmoid(-sign * margin)
    total = jnp.zeros(total_ref.shape, F32)
    for k in range(pairs):
        grad = jnp.sum(margin_grad * hots[k], axis=1, keepdims=True)
        if k == 0:
            grad_ref[...] = jnp.broadcast_to(grad, grad_ref.shape)
        total = total + grad * piece_refs[k][:share]
    total_ref[...] = total


def gather_kernel(parts, *rest):
    piece_refs = rest[:parts]
    conv_ref, bias_ref, head_ref, stage = rest[parts:]
    share = piece_refs[0].shape[0]
    me = lax.axis_index("space")
    for k in range(parts):
        start = pl.multiple_of(lax.rem(me - k + parts, parts) * share, 8)
        stage[pl.ds(start, share), :] = piece_refs[k][...]
    conv_ref[...] = stage[: conv_ref.shape[0]]
    bias_ref[...] = stage[STAT : STAT + 1]
    head_ref[...] = stage[STAT + 1 : STAT + 2]


def finish_kernel(
    inv_root, parts, grad_ref, source_ref, edit_ref, across_ref, beyond_ref, source_out, edit_out
):
    scale = grad_ref[0:1, 0:1].reshape(1, 1, 1) * inv_root
    source_out[...] = (source_ref[...] * scale).astype(BF16)
    rows = edit_ref.shape[0]
    me = lax.axis_index("space")
    odd = lax.rem(me, 2) == 1
    for row, edge, mine in ((0, 0, odd), (rows - 8, parts - 1, ~odd)):
        own = edit_ref[row : row + 8]
        for picked, ref in ((mine, across_ref), (~mine, beyond_ref)):

            @pl.when((me != edge) & picked)
            def _():
                edit_out[row : row + 8] = ((own + ref[...].astype(F32)) * scale).astype(BF16)

        @pl.when(me == edge)
        def _():
            edit_out[row : row + 8] = (own * scale).astype(BF16)


def call(kernel, outs, scratch, flops, *args):
    nbytes = sum(a.size * a.dtype.itemsize for a in args)
    return pl.pallas_call(
        kernel,
        out_shape=outs,
        in_specs=[pl.BlockSpec(memory_space=pltpu.VMEM)] * len(args),
        scratch_shapes=scratch,
        compiler_params=pltpu.CompilerParams(vmem_limit_bytes=VMEM_LIMIT),
        cost_estimate=pl.CostEstimate(flops=flops, bytes_accessed=nbytes, transcendentals=0),
    )(*(pltpu.with_memory_space_constraint(a, pltpu.VMEM) for a in args))


def result(dims, dtype=F32):
    return jax.ShapeDtypeStruct(dims, dtype)


def shape(dims, dtype=F32):
    return pltpu.VMEM(dims, dtype)


def around(axis, step):
    count = lax.axis_size(axis)
    return [(i, (i + step) % count) for i in range(count)]


def local(
    source_feats, edit_feats, conv_weight, conv_bias, head_weight, comp_first, comp_second, comp_win
):
    _, rows, columns, chan = source_feats.shape
    kout, disp = conv_weight.shape
    inv_root = chan ** (-0.5)
    space, pairs = lax.axis_size("space"), lax.axis_size("pair")
    pixels = rows * space * columns
    groups = columns // GROUP
    wide_cols = columns + 2 * RADIUS
    share = -(-(disp + 2) // (8 * space)) * 8
    edit = edit_feats[0]
    source = source_feats.reshape(rows, groups, GROUP, chan)
    odd = lax.rem(lax.axis_index("space"), 2)
    to_across = [(i, i ^ 1 if i ^ 1 < space else i) for i in range(space)]
    to_beyond = [(i, b if 0 <= (b := i + 1 - 2 * ((i + 1) % 2)) < space else i) for i in range(space)]
    edge_rows = rows - RADIUS
    across = lax.dynamic_slice_in_dim(edit, edge_rows * (1 - odd), RADIUS, 0)
    beyond = lax.dynamic_slice_in_dim(edit, edge_rows * odd, RADIUS, 0)
    across = lax.ppermute(across, "space", to_across)
    beyond = lax.ppermute(beyond, "space", to_beyond)
    turned, corr, wide = call(
        functools.partial(inner_kernel, inv_root),
        (
            shape((rows, groups, GROUP, chan), BF16),
            shape((rows, groups, GROUP, rows * WIN), BF16),
            shape((PER, kout, POS * LANES), BF16),
        ),
        [pltpu.VMEM((rows, wide_cols, chan), BF16)],
        2 * 10**9,
        source,
        edit,
        conv_weight.T,
    )
    gate, *pieces = call(
        functools.partial(outer_kernel, inv_root, pixels, space),
        (shape((rows, columns, kout), BF16),) + (shape((share + 8, kout)),) * space,
        [
            pltpu.VMEM((2 * RADIUS, wide_cols, chan), BF16),
            pltpu.VMEM((rows // 2, groups, GROUP, 8 * WIN), BF16),
            pltpu.VMEM((rows // 2, groups, GROUP, 8 * WIN), BF16),
            pltpu.VMEM((share * space, kout), F32),
        ],
        2 * 10**9,
        turned,
        corr,
        across,
        beyond,
        wide,
        conv_bias[None],
        head_weight[None],
    )
    quarter = pieces[0]
    for k in range(1, space):
        quarter = quarter + lax.ppermute(pieces[k], "space", around("space", k))
    rim_across, rim_beyond = call(
        rim_kernel,
        (shape((RADIUS, columns, chan), BF16),) * 2,
        [
            pltpu.VMEM((rows // 2, groups, GROUP, 8 * WIN), BF16),
            pltpu.VMEM((rows // 2, groups, GROUP, 8 * WIN), BF16),
            pltpu.VMEM((2 * RADIUS, wide_cols, chan), F32),
        ],
        10**9,
        gate,
        wide,
        source,
    )
    from_across = lax.ppermute(rim_across, "space", to_across)
    from_beyond = lax.ppermute(rim_beyond, "space", to_beyond)
    source_sum, edit_sum = call(
        functools.partial(back_kernel, space),
        (shape((rows, groups, GROUP, chan)), shape((rows, columns, chan))),
        [
            pltpu.VMEM((rows + 2 * RADIUS, wide_cols, chan), BF16),
            pltpu.VMEM((rows, groups, GROUP, (rows + 2 * RADIUS) * WIN), BF16),
            pltpu.VMEM((rows, wide_cols, chan), F32),
        ],
        4 * 10**9,
        gate,
        wide,
        source,
        edit,
        across,
        beyond,
    )
    others = [quarter] + [lax.ppermute(quarter, "pair", around("pair", k)) for k in range(1, pairs)]
    comps = jnp.stack([comp_first, comp_second, comp_win])
    total, score_grad, loss = call(
        functools.partial(judge_kernel, pairs),
        (shape((share, kout)), shape((8, LANES)), shape((1, LANES))),
        [],
        10**6,
        comps,
        *others,
    )
    gathered = [total] + [lax.ppermute(total, "space", around("space", k)) for k in range(1, space)]
    source_grad, edit_grad = call(
        functools.partial(finish_kernel, inv_root, space),
        (result((rows, columns, chan), BF16),) * 2,
        [],
        10**7,
        score_grad,
        source_sum.reshape(rows, columns, chan),
        edit_sum,
        from_across,
        from_beyond,
    )
    conv_grad, bias_grad, head_grad = call(
        functools.partial(gather_kernel, space),
        (result((disp, kout)), result((1, kout)), result((1, kout))),
        [pltpu.VMEM((share * space, kout), F32)],
        10**6,
        *gathered,
    )
    return (
        source_grad[None],
        edit_grad[None],
        conv_grad.T,
        bias_grad[0],
        head_grad[0],
        loss[0, :1],
    )


def solution(mesh):
    in_specs = (
        P(("groups", "pair"), "space", None, None),
        P(("groups", "pair"), "space", None, None),
        P(),
        P(),
        P(),
        P("groups"),
        P("groups"),
        P("groups"),
    )
    out_specs = (
        P(("groups", "pair"), "space", None, None),
        P(("groups", "pair"), "space", None, None),
        P("groups", None),
        P("groups"),
        P("groups"),
        P("groups"),
    )
    return jax.shard_map(local, mesh=mesh, in_specs=in_specs, out_specs=out_specs, check_vma=False)
```

time: 487 us -> 41.9 us (0.09)
  local copies, waits for them, and re-layouts: 138 us -> 2.36 us
  other arithmetic: 127 us -> 0.03 us
  loops' own time: 89.3 us -> 0 us
  blocking collectives: 58.3 us -> 0 us
  matrix products: 44.5 us -> 0 us
  between operations: 16.8 us -> 0.85 us
  starting transfers between devices: 7.08 us -> 21.2 us
  Pallas kernels: 0 us -> 13.5 us
    another operation x2 -> x0, loops' own time: 89.3 us -> none  [the longest x1 45 us: correlate_back(): lax.scan(one_shift, (edit_init, source_init), jnp.arange(span_len, dtype=...]
    reduce_sum x38 -> x0, other arithmetic: 85 us -> none  [the longest x17 56.6 us: one_shift(): banded = jnp.sum(matrix[:, :, None, :, :] * table[None, None], axis=3)]
    while x136 -> x0, local copies, waits for them, and re-layouts: 71.9 us -> none
    psum x2 -> x0, blocking collectives: 46.4 us -> none  [the longest x1 32.5 us: local(): lax.psum((conv_grad, bias_grad, head_grad), ('space', 'pair'))]
    dot_general x54 -> x0, matrix products: 44.5 us -> none  [the longest x17 15 us: one_shift(): jnp.einsum('pyjx,pyjc->pyxc', matrix, window, preferred_element_type=jnp....]
    dynamic_update_slice x17 -> x0, local copies, waits for them, and re-layouts: 29.3 us -> none  [one_shift(): carry = lax.dynamic_update_slice_in_dim(carry, block, offset * span_len, 2)]
    mul x18 -> x0, other arithmetic: 19.1 us -> none  [the longest x17 18.5 us: one_shift(): block[:, :, :, None, :] * table[None, None]]
    dynamic_slice x35 -> x1, local copies, waits for them, and re-layouts: 20.4 us -> 1.43 us  [local(): beyond = lax.dynamic_slice_in_dim(edit, edge_rows * odd, RADIUS, 0)]
  transfers between devices with their start and end apart: 5 -> 13, of which waited for: 1 -> 5; matrix products, arithmetic and copies ran while one was open for 20% -> 0% of each run, Pallas kernels for 0% -> 18%
where the time goes in v1:
time: 41.9 us; the launch traced here: 41.7 us
  starting transfers between devices  21.2 us (51%)
  Pallas kernels  13.5 us (32%)
  waiting for transfers between devices  3.79 us (9%)
  local copies, waits for them, and re-layouts  2.36 us (6%)
  between operations  0.85 us (2%)
    pallas_call x7, Pallas kernels, call(): pl.pallas_call(kernel, out_shape=outs, in_specs=[pl.BlockSpec(memory_spac...  13.5 us
    ppermute x3, starting transfers between devices, local(): quarter = quarter + lax.ppermute(pieces[k], 'space', around('space', k))  9.58 us
    ppermute x3, starting transfers between devices, local(): lax.ppermute(quarter, 'pair', around('pair', k))  6.07 us
    ppermute x3, starting transfers between devices, local(): lax.ppermute(total, 'space', around('space', k))  3.62 us
    ppermute x3, waiting for transfers between devices, local(): lax.ppermute(quarter, 'pair', around('pair', k))  2.91 us
    dynamic_slice x1, local copies, waits for them, and re-layouts, local(): beyond = lax.dynamic_slice_in_dim(edit, edge_rows * odd, RADIUS, 0)  1.43 us
    unnamed x18, local copies, waits for them, and re-layouts  0.92 us
    ppermute x3, waiting for transfers between devices, local(): quarter = quarter + lax.ppermute(pieces[k], 'space', around('space', k))  0.86 us
  transfers between devices with their start and end apart: 13, of which 5 were waited for; matrix products, arithmetic and copies ran while one was open for 0% of the time, Pallas kernels for 18%

profile of v1, /device:TPU:0, one launch (start us, length us, event | category | flops | bytes accessed | tf_op | source)
XLA Modules:
  0.0 41.7 jit_solution(15159178409529266564)
XLA Ops:
  0.7 1.4 %dynamic-slice_bitcast_fusion = (bf16[8,128,256]{2,1,0:T(8,128)(2,1)S(1)}, bf16[8,128,256]{2,1,0:T(8,128)(2,1)S(1)}) fusion(bf16[1,16,128,256]{3,2,1,0:T(8,128)(2,1)} %param.9, s32[]{:T(128)S(6)} %select_n.7, s32[]{:T(128)S(6)} %select_n.6), kind=kLoop, calls=%fused_computation | loop fusion | bytes 2097160 | tf_op jit(solution)/shard_map/dynamic_slice | solution.py:425
  2.1 0.5 %collective-permute-start = (bf16[8,128,256]{2,1,0:T(8,128)(2,1)S(1)}, bf16[8,128,256]{2,1,0:T(8,128)(2,1)S(1)}, u32[]{:S(2)}, u32[]{:S(2)}) collective-permute-start(bf16[8,128,256]{2,1,0:T(8,128)(2,1)S(1)} %get-tuple-element.47), channel_id=1, source_target_pairs={{0,4},{4,0},{8,12},{12,8},{1,5},{5,1},{9,13},{13,9},{2,6},{6,2},{1... | collective-permute-start | bytes 1572872 | tf_op jit(solution)/shard_map/ppermute | solution.py:426
  2.6 0.7 %collective-permute-start.1 = (bf16[8,128,256]{2,1,0:T(8,128)(2,1)S(1)}, bf16[8,128,256]{2,1,0:T(8,128)(2,1)S(1)}, u32[]{:S(2)}, u32[]{:S(2)}) collective-permute-start(bf16[8,128,256]{2,1,0:T(8,128)(2,1)S(1)} %get-tuple-element.46), channel_id=1, source_target_pairs={{0,0},{4,8},{8,4},{12,12},{1,1},{5,9},{9,5},{13,13},{2,2},{6,10},{... | collective-permute-start | bytes 1572872 | tf_op jit(solution)/shard_map/ppermute | solution.py:427
  3.3 0.9 %copy-done.2 = bf16[128,289]{0,1:T(8,128)(2,1)S(1)} copy-done((bf16[128,289]{0,1:T(8,128)(2,1)S(1)}, bf16[128,289]{0,1:T(8,128)(2,1)}, u32[]{:S(2)}) %copy-start.2) | copy-done | bytes 74008
  4.2 2.1 %shard_map.127 = (bf16[16,8,16,256]{3,2,1,0:T(8,128)(2,1)S(1)}, bf16[16,8,16,512]{3,2,1,0:T(8,128)(2,1)S(1)}, bf16[4,128,640]{2,1,0:T(8,128)(2,1)S(1)}) custom-call(bf16[16,8,16,256]{3,2,1,0:T(8,128)(2,1)S(1)} %bitcast.23, bf16[16,128,256]{2,1,0:T(8,128)(2,1)S(1)} %bitcast.21, bf16[289,128]{1,0:T(8,128)(2,1)S(1)} %bitcast.26), custom_call_target="tpu_custom_call" | custom-call | flops 2000000000 | bytes 2171136 | tf_op jit(solution)/shard_map/pallas_call | solution.py:384
  6.4 4.0 %shard_map.128 = (bf16[16,128,128]{2,1,0:T(8,128)(2,1)S(1)}, f32[88,128]{1,0:T(8,128)S(1)}, f32[88,128]{1,0:T(8,128)S(1)}, f32[88,128]{1,0:T(8,128)S(1)}, f32[88,128]{1,0:T(8,128)S(1)}) custom-call(bf16[16,8,16,256]{3,2,1,0:T(8,128)(2,1)S(1)} %get-tuple-element.26.turned_ref, bf16[16,8,16,512]{3,2,1,0:T(8,128)(2,1)S(1)} %get-tuple-element.27.corr_ref, ...), custom_call_target="tpu_custom_call" | custom-call | flops 2000000000 | bytes 4850688 | tf_op jit(solution)/shard_map/pallas_call | solution.py:384
  10.4 2.7 %collective-permute-start.4 = (f32[88,128]{1,0:T(8,128)S(1)}, f32[88,128]{1,0:T(8,128)S(1)}, u32[]{:S(2)}, u32[]{:S(2)}) collective-permute-start(f32[88,128]{1,0:T(8,128)S(1)} %get-tuple-element.32), channel_id=1, source_target_pairs={{0,12},{4,0},{8,4},{12,8},{1,13},{5,1},{9,5},{13,9},{2,14},{6,2},{... | collective-permute-start | bytes 135176 | tf_op jit(solution)/shard_map/ppermute | solution.py:461
  13.1 6.7 %collective-permute-start.3 = (f32[88,128]{1,0:T(8,128)S(1)}, f32[88,128]{1,0:T(8,128)S(1)}, u32[]{:S(2)}, u32[]{:S(2)}) collective-permute-start(f32[88,128]{1,0:T(8,128)S(1)} %get-tuple-element.31), channel_id=1, source_target_pairs={{0,8},{4,12},{8,0},{12,4},{1,9},{5,13},{9,1},{13,5},{2,10},{6,14},... | collective-permute-start | bytes 135176 | tf_op jit(solution)/shard_map/ppermute | solution.py:461
  19.8 0.2 collective-permute-start.2
  20.0 1.6 %shard_map.131 = (bf16[8,128,256]{2,1,0:T(8,128)(2,1)S(1)}, bf16[8,128,256]{2,1,0:T(8,128)(2,1)S(1)}) custom-call(bf16[16,128,128]{2,1,0:T(8,128)(2,1)S(1)} %get-tuple-element.34.gate_ref, bf16[4,128,640]{2,1,0:T(8,128)(2,1)S(1)} %get-tuple-element.28.wide_ref, bf16[16,8,16,256]{3,2,1,0:T(8,128)(2,1)S(1)} %bitcast.24), custom_call_target="tpu_custom_call" | custom-call | flops 1000000000 | bytes 2228224 | tf_op jit(solution)/shard_map/pallas_call | solution.py:384
  21.7 0.7 %collective-permute-start.9 = (bf16[8,128,256]{2,1,0:T(8,128)(2,1)S(1)}, bf16[8,128,256]{2,1,0:T(8,128)(2,1)S(1)}, u32[]{:S(2)}, u32[]{:S(2)}) collective-permute-start(bf16[8,128,256]{2,1,0:T(8,128)(2,1)S(1)} %get-tuple-element.38), channel_id=1, source_target_pairs={{0,0},{4,8},{8,4},{12,12},{1,1},{5,9},{9,5},{13,13},{2,2},{6,10},{... | collective-permute-start | bytes 1572872 | tf_op jit(solution)/shard_map/ppermute | solution.py:476
  22.5 0.7 %collective-permute-done.2 = f32[88,128]{1,0:T(8,128)S(1)} collective-permute-done((f32[88,128]{1,0:T(8,128)S(1)}, f32[88,128]{1,0:T(8,128)S(1)}, u32[]{:S(2)}, u32[]{:S(2)}) %collective-permute-start.2) | collective-permute-done | bytes 45088 | tf_op jit(solution)/shard_map/ppermute | solution.py:461
  23.3 2.1 %collective-permute-start.5 = (f32[88,128]{1,0:T(8,128)S(1)}, f32[88,128]{1,0:T(8,128)S(1)}, u32[]{:S(2)}, u32[]{:S(2)}) collective-permute-start(f32[88,128]{1,0:T(8,128)S(1)} %add_add_fusion.rest_0_), channel_id=1, source_target_pairs={{0,1},{1,2},{2,3},{3,0},{4,5},{5,6},{6,7},{7,4},{8,9},{9,10},{10,1... | collective-permute-start | bytes 135176 | tf_op jit(solution)/shard_map/ppermute | solution.py:493
  25.4 2.6 %collective-permute-start.6 = (f32[88,128]{1,0:T(8,128)S(1)}, f32[88,128]{1,0:T(8,128)S(1)}, u32[]{:S(2)}, u32[]{:S(2)}) collective-permute-start(f32[88,128]{1,0:T(8,128)S(1)} %add_add_fusion.rest_0_), channel_id=1, source_target_pairs={{0,2},{1,3},{2,0},{3,1},{4,6},{5,7},{6,4},{7,5},{8,10},{9,11},{10,... | collective-permute-start | bytes 135176 | tf_op jit(solution)/shard_map/ppermute | solution.py:493
  28.0 1.3 %collective-permute-start.7 = (f32[88,128]{1,0:T(8,128)S(1)}, f32[88,128]{1,0:T(8,128)S(1)}, u32[]{:S(2)}, u32[]{:S(2)}) collective-permute-start(f32[88,128]{1,0:T(8,128)S(1)} %add_add_fusion.rest_0_), channel_id=1, source_target_pairs={{0,3},{1,0},{2,1},{3,2},{4,7},{5,4},{6,5},{7,6},{8,11},{9,8},{10,9... | collective-permute-start | bytes 135176 | tf_op jit(solution)/shard_map/ppermute | solution.py:493
  29.5 0.9 %collective-permute-done.6.rest_2_ = f32[88,128]{1,0:T(8,128)S(1)} collective-permute-done((f32[88,128]{1,0:T(8,128)S(1)}, f32[88,128]{1,0:T(8,128)S(1)}, u32[]{:S(2)}, u32[]{:S(2)}) %collective-permute-start.6) | collective-permute-done | bytes 45088 | tf_op jit(solution)/shard_map/ppermute | solution.py:493
  30.4 1.9 %collective-permute-done.7.rest_3_ = f32[88,128]{1,0:T(8,128)S(1)} collective-permute-done((f32[88,128]{1,0:T(8,128)S(1)}, f32[88,128]{1,0:T(8,128)S(1)}, u32[]{:S(2)}, u32[]{:S(2)}) %collective-permute-start.7) | collective-permute-done | bytes 45088 | tf_op jit(solution)/shard_map/ppermute | solution.py:493
  32.3 0.2 shard_map.129
  32.5 0.8 %collective-permute-start.10 = (f32[80,128]{1,0:T(8,128)S(1)}, f32[80,128]{1,0:T(8,128)S(1)}, u32[]{:S(2)}, u32[]{:S(2)}) collective-permute-start(f32[80,128]{1,0:T(8,128)S(1)} %get-tuple-element.41.rest_0_), channel_id=1, source_target_pairs={{0,4},{4,8},{8,12},{12,0},{1,5},{5,9},{9,13},{13,1},{2,6},{6,10},{... | collective-permute-start | bytes 122888 | tf_op jit(solution)/shard_map/ppermute | solution.py:503
  33.3 1.4 %collective-permute-start.11 = (f32[80,128]{1,0:T(8,128)S(1)}, f32[80,128]{1,0:T(8,128)S(1)}, u32[]{:S(2)}, u32[]{:S(2)}) collective-permute-start(f32[80,128]{1,0:T(8,128)S(1)} %get-tuple-element.41.rest_0_), channel_id=1, source_target_pairs={{0,8},{4,12},{8,0},{12,4},{1,9},{5,13},{9,1},{13,5},{2,10},{6,14},... | collective-permute-start | bytes 122888 | tf_op jit(solution)/shard_map/ppermute | solution.py:503
  34.7 1.4 %collective-permute-start.12 = (f32[80,128]{1,0:T(8,128)S(1)}, f32[80,128]{1,0:T(8,128)S(1)}, u32[]{:S(2)}, u32[]{:S(2)}) collective-permute-start(f32[80,128]{1,0:T(8,128)S(1)} %get-tuple-element.41.rest_0_), channel_id=1, source_target_pairs={{0,12},{4,0},{8,4},{12,8},{1,13},{5,1},{9,5},{13,9},{2,14},{6,2},{... | collective-permute-start | bytes 122888 | tf_op jit(solution)/shard_map/ppermute | solution.py:503
  36.1 3.0 %shard_map.130 = (f32[16,8,16,256]{3,2,1,0:T(8,128)S(1)}, f32[16,128,256]{2,1,0:T(8,128)S(1)}) custom-call(bf16[16,128,128]{2,1,0:T(8,128)(2,1)S(1)} %get-tuple-element.34.gate_ref, bf16[4,128,640]{2,1,0:T(8,128)(2,1)S(1)} %get-tuple-element.28.wide_ref, bf16[16,8,16,256]{3,2,1,0:T(8,128)(2,1)S(1)} %bitcast.25, bf16[16,128,256]{2,1,0:T(8,128)(2,1)S(1)} %bitcast.22, ...), custom_call_target="tpu_custom_call" | custom-call | flops 4000000000 | bytes 4325376 | tf_op jit(solution)/shard_map/pallas_call | solution.py:384
  39.1 0.7 %shard_map.133 = (f32[289,128]{1,0:T(8,128)}, f32[1,128]{1,0:T(1,128)}, f32[1,128]{1,0:T(1,128)}) custom-call(f32[80,128]{1,0:T(8,128)S(1)} %get-tuple-element.41.rest_0_, f32[80,128]{1,0:T(8,128)S(1)} %collective-permute-done.10.rest_1_, f32[80,128]{1,0:T(8,128)S(1)} %collective-permute-done.11.rest_2_, f32[80,128]{1,0:T(8,128)S(1)} %collective-permute-done.12.rest_3_), custom_call_target="tpu_custom_call" | custom-call | flops 1000000 | bytes 163840 | tf_op jit(solution)/shard_map/pallas_call | solution.py:384
  39.8 1.9 %shard_map.132 = (bf16[16,128,256]{2,1,0:T(8,128)(2,1)}, bf16[16,128,256]{2,1,0:T(8,128)(2,1)}) custom-call(f32[8,128]{1,0:T(8,128)S(1)} %get-tuple-element.33.grad_ref, f32[16,128,256]{2,1,0:T(8,128)S(1)} %bitcast.20, f32[16,128,256]{2,1,0:T(8,128)S(1)} %get-tuple-element.36.edit_ref, bf16[8,128,256]{2,1,0:T(8,128)(2,1)S(1)} %collective-permute-done.8.across_ref, ...), custom_call_target="tpu_custom_call" | custom-call | flops 10000000 | bytes 5246976 | tf_op jit(solution)/shard_map/pallas_call | solution.py:384
  (30 shorter events, 0.4 us)
Async XLA Ops:
  0.6 2.7 %copy-start = (bf16[1,16,128,256]{3,2,1,0:T(8,128)(2,1)S(1)}, bf16[1,16,128,256]{3,2,1,0:T(8,128)(2,1)}, u32[]{:S(2)}) copy-start(bf16[1,16,128,256]{3,2,1,0:T(8,128)(2,1)} %param.9) | copy-start | bytes 3145732
  0.6 2.7 %copy-start.1 = (bf16[1,16,128,256]{3,2,1,0:T(8,128)(2,1)S(1)}, bf16[1,16,128,256]{3,2,1,0:T(8,128)(2,1)}, u32[]{:S(2)}) copy-start(bf16[1,16,128,256]{3,2,1,0:T(8,128)(2,1)} %param.8) | copy-start | bytes 3145732
  2.1 4.2 %collective-permute-start = (bf16[8,128,256]{2,1,0:T(8,128)(2,1)S(1)}, bf16[8,128,256]{2,1,0:T(8,128)(2,1)S(1)}, u32[]{:S(2)}, u32[]{:S(2)}) collective-permute-start(bf16[8,128,256]{2,1,0:T(8,128)(2,1)S(1)} %get-tuple-element.47), channel_id=1, source_target_pairs={{0,4},{4,0},{8,12},{12,8},{1,5},{5,1},{9,13},{13,9},{2,6},{6,2},{1... | collective-permute-start | bytes 1572872 | tf_op jit(solution)/shard_map/ppermute | solution.py:426
  2.6 3.7 %collective-permute-start.1 = (bf16[8,128,256]{2,1,0:T(8,128)(2,1)S(1)}, bf16[8,128,256]{2,1,0:T(8,128)(2,1)S(1)}, u32[]{:S(2)}, u32[]{:S(2)}) collective-permute-start(bf16[8,128,256]{2,1,0:T(8,128)(2,1)S(1)} %get-tuple-element.46), channel_id=1, source_target_pairs={{0,0},{4,8},{8,4},{12,12},{1,1},{5,9},{9,5},{13,13},{2,2},{6,10},{... | collective-permute-start | bytes 1572872 | tf_op jit(solution)/shard_map/ppermute | solution.py:427
  3.3 0.9 %copy-start.2 = (bf16[128,289]{0,1:T(8,128)(2,1)S(1)}, bf16[128,289]{0,1:T(8,128)(2,1)}, u32[]{:S(2)}) copy-start(bf16[128,289]{0,1:T(8,128)(2,1)} %param.10) | copy-start | bytes 221956
  4.2 2.1 %copy-start.3 = (f32[128]{0:T(128)S(1)}, f32[128]{0:T(128)}, u32[]{:S(2)}) copy-start(f32[128]{0:T(128)} %param.11) | copy-start | bytes 1540
  4.2 2.1 %copy-start.4 = (f32[128]{0:T(128)S(1)}, f32[128]{0:T(128)}, u32[]{:S(2)}) copy-start(f32[128]{0:T(128)} %param.12) | copy-start | bytes 1540
  10.4 19.0 %copy-start.6 = (s32[16]{0:T(128)S(1)}, s32[16]{0:T(128)}, u32[]{:S(2)}) copy-start(s32[16]{0:T(128)} %param.15) | copy-start | bytes 196
  10.4 19.0 %copy-start.7 = (s32[16]{0:T(128)S(1)}, s32[16]{0:T(128)}, u32[]{:S(2)}) copy-start(s32[16]{0:T(128)} %param.14) | copy-start | bytes 196
  10.4 19.0 %copy-start.8 = (s32[16]{0:T(128)S(1)}, s32[16]{0:T(128)}, u32[]{:S(2)}) copy-start(s32[16]{0:T(128)} %param.13) | copy-start | bytes 196
  10.4 12.0 %collective-permute-start.4 = (f32[88,128]{1,0:T(8,128)S(1)}, f32[88,128]{1,0:T(8,128)S(1)}, u32[]{:S(2)}, u32[]{:S(2)}) collective-permute-start(f32[88,128]{1,0:T(8,128)S(1)} %get-tuple-element.32), channel_id=1, source_target_pairs={{0,12},{4,0},{8,4},{12,8},{1,13},{5,1},{9,5},{13,9},{2,14},{6,2},{... | collective-permute-start | bytes 135176 | tf_op jit(solution)/shard_map/ppermute | solution.py:461
  13.1 9.5 %collective-permute-start.3 = (f32[88,128]{1,0:T(8,128)S(1)}, f32[88,128]{1,0:T(8,128)S(1)}, u32[]{:S(2)}, u32[]{:S(2)}) collective-permute-start(f32[88,128]{1,0:T(8,128)S(1)} %get-tuple-element.31), channel_id=1, source_target_pairs={{0,8},{4,12},{8,0},{12,4},{1,9},{5,13},{9,1},{13,5},{2,10},{6,14},... | collective-permute-start | bytes 135176 | tf_op jit(solution)/shard_map/ppermute | solution.py:461
  19.8 3.5 %collective-permute-start.2 = (f32[88,128]{1,0:T(8,128)S(1)}, f32[88,128]{1,0:T(8,128)S(1)}, u32[]{:S(2)}, u32[]{:S(2)}) collective-permute-start(f32[88,128]{1,0:T(8,128)S(1)} %get-tuple-element.30), channel_id=1, source_target_pairs={{0,4},{4,8},{8,12},{12,0},{1,5},{5,9},{9,13},{13,1},{2,6},{6,10},{... | collective-permute-start | bytes 135176 | tf_op jit(solution)/shard_map/ppermute | solution.py:461
  21.6 18.2 %collective-permute-start.8 = (bf16[8,128,256]{2,1,0:T(8,128)(2,1)S(1)}, bf16[8,128,256]{2,1,0:T(8,128)(2,1)S(1)}, u32[]{:S(2)}, u32[]{:S(2)}) collective-permute-start(bf16[8,128,256]{2,1,0:T(8,128)(2,1)S(1)} %get-tuple-element.37), channel_id=1, source_target_pairs={{0,4},{4,0},{8,12},{12,8},{1,5},{5,1},{9,13},{13,9},{2,6},{6,2},{1... | collective-permute-start | bytes 1572872 | tf_op jit(solution)/shard_map/ppermute | solution.py:475
  21.7 18.1 %collective-permute-start.9 = (bf16[8,128,256]{2,1,0:T(8,128)(2,1)S(1)}, bf16[8,128,256]{2,1,0:T(8,128)(2,1)S(1)}, u32[]{:S(2)}, u32[]{:S(2)}) collective-permute-start(bf16[8,128,256]{2,1,0:T(8,128)(2,1)S(1)} %get-tuple-element.38), channel_id=1, source_target_pairs={{0,0},{4,8},{8,4},{12,12},{1,1},{5,9},{9,5},{13,13},{2,2},{6,10},{... | collective-permute-start | bytes 1572872 | tf_op jit(solution)/shard_map/ppermute | solution.py:476
  23.3 6.2 %collective-permute-start.5 = (f32[88,128]{1,0:T(8,128)S(1)}, f32[88,128]{1,0:T(8,128)S(1)}, u32[]{:S(2)}, u32[]{:S(2)}) collective-permute-start(f32[88,128]{1,0:T(8,128)S(1)} %add_add_fusion.rest_0_), channel_id=1, source_target_pairs={{0,1},{1,2},{2,3},{3,0},{4,5},{5,6},{6,7},{7,4},{8,9},{9,10},{10,1... | collective-permute-start | bytes 135176 | tf_op jit(solution)/shard_map/ppermute | solution.py:493
  25.4 4.9 %collective-permute-start.6 = (f32[88,128]{1,0:T(8,128)S(1)}, f32[88,128]{1,0:T(8,128)S(1)}, u32[]{:S(2)}, u32[]{:S(2)}) collective-permute-start(f32[88,128]{1,0:T(8,128)S(1)} %add_add_fusion.rest_0_), channel_id=1, source_target_pairs={{0,2},{1,3},{2,0},{3,1},{4,6},{5,7},{6,4},{7,5},{8,10},{9,11},{10,... | collective-permute-start | bytes 135176 | tf_op jit(solution)/shard_map/ppermute | solution.py:493
  28.0 4.3 %collective-permute-start.7 = (f32[88,128]{1,0:T(8,128)S(1)}, f32[88,128]{1,0:T(8,128)S(1)}, u32[]{:S(2)}, u32[]{:S(2)}) collective-permute-start(f32[88,128]{1,0:T(8,128)S(1)} %add_add_fusion.rest_0_), channel_id=1, source_target_pairs={{0,3},{1,0},{2,1},{3,2},{4,7},{5,4},{6,5},{7,6},{8,11},{9,8},{10,9... | collective-permute-start | bytes 135176 | tf_op jit(solution)/shard_map/ppermute | solution.py:493
  32.5 6.6 %copy-start.5 = (f32[1,128]{1,0:T(1,128)}, f32[1,128]{1,0:T(1,128)S(1)}, u32[]{:S(2)}) copy-start(f32[1,128]{1,0:T(1,128)S(1)} %get-tuple-element.45) | copy-start | bytes 1540
  32.5 6.6 %collective-permute-start.10 = (f32[80,128]{1,0:T(8,128)S(1)}, f32[80,128]{1,0:T(8,128)S(1)}, u32[]{:S(2)}, u32[]{:S(2)}) collective-permute-start(f32[80,128]{1,0:T(8,128)S(1)} %get-tuple-element.41.rest_0_), channel_id=1, source_target_pairs={{0,4},{4,8},{8,12},{12,0},{1,5},{5,9},{9,13},{13,1},{2,6},{6,10},{... | collective-permute-start | bytes 122888 | tf_op jit(solution)/shard_map/ppermute | solution.py:503
  33.3 5.8 %collective-permute-start.11 = (f32[80,128]{1,0:T(8,128)S(1)}, f32[80,128]{1,0:T(8,128)S(1)}, u32[]{:S(2)}, u32[]{:S(2)}) collective-permute-start(f32[80,128]{1,0:T(8,128)S(1)} %get-tuple-element.41.rest_0_), channel_id=1, source_target_pairs={{0,8},{4,12},{8,0},{12,4},{1,9},{5,13},{9,1},{13,5},{2,10},{6,14},... | collective-permute-start | bytes 122888 | tf_op jit(solution)/shard_map/ppermute | solution.py:503
  34.7 4.4 %collective-permute-start.12 = (f32[80,128]{1,0:T(8,128)S(1)}, f32[80,128]{1,0:T(8,128)S(1)}, u32[]{:S(2)}, u32[]{:S(2)}) collective-permute-start(f32[80,128]{1,0:T(8,128)S(1)} %get-tuple-element.41.rest_0_), channel_id=1, source_target_pairs={{0,12},{4,0},{8,4},{12,8},{1,13},{5,1},{9,5},{13,9},{2,14},{6,2},{... | collective-permute-start | bytes 122888 | tf_op jit(solution)/shard_map/ppermute | solution.py:503

commit v2 on v1

--- a/solution.py
+++ b/solution.py
@@ -71,48 +71,36 @@
     pad_ref[row : row + rows, RADIUS : RADIUS + cols] = block_ref[...]
 
 
-def fill_halos(pad_ref, low, high, across_ref, beyond_ref, parts):
-    me = lax.axis_index("space")
-    odd = lax.rem(me, 2) == 1
-    cols = across_ref.shape[1]
-    for row, edge, mine in ((low, 0, odd), (high, parts - 1, ~odd)):
-        fill_columns(pad_ref, row, 8, cols)
-        at = (slice(row, row + 8), slice(RADIUS, RADIUS + cols))
-
-        @pl.when(me == edge)
-        def _():
-            pad_ref[at] = jnp.zeros(across_ref.shape, BF16)
-
-        @pl.when((me != edge) & mine)
-        def _():
-            pad_ref[at] = across_ref[...]
-
-        @pl.when((me != edge) & ~mine)
-        def _():
-            pad_ref[at] = beyond_ref[...]
-
-
 def window(pad_ref, row, rows, g):
     block = pad_ref[row : row + rows, g * GROUP : g * GROUP + WIN, :]
     return block.reshape(rows * WIN, block.shape[2])
 
 
-def correlate_set(lhs, pad_ref, row, g, inv_root, out_ref, y0, lane):
+def correlate_set(lhs, pad_ref, row, g, inv_root, out_ref, spot, lane):
     ys = lhs.shape[0] // GROUP
     scores = nt(lhs, window(pad_ref, row, 8, g)) * inv_root
     scores = scores.reshape(ys, GROUP, 8 * WIN)
     for i, part in enumerate(skew_wide(scores, LANES - GROUP + 1)):
         at = lane + i * LANES
-        out_ref[y0 : y0 + ys, g, :, at : at + LANES] = part.astype(BF16)
-
-
-def inner_kernel(inv_root, source_ref, edit_ref, weight_ref, turned_ref, corr_ref, wide_ref, pad):
+        out_ref[spot, g, :, at : at + LANES] = part.astype(BF16)
+
+
+def inner_kernel(
+    inv_root,
+    source_ref,
+    edit_ref,
+    weight_ref,
+    turned_ref,
+    corr_ref,
+    wide_ref,
+    pad,
+    weight,
+    weight_sem,
+):
     rows, groups, _, chan = source_ref.shape
+    copy = pltpu.make_async_copy(weight_ref, weight, weight_sem)
+    copy.start()
     fill_padded(pad, 0, edit_ref)
-    table = spread_table(SPAN * SPAN)
-    base = tn(weight_ref[...], table)
-    for r in range(PER):
-        wide_ref[r] = (base if r == 0 else pltpu.roll(base, r * WIN, 1)).astype(BF16)
     turn = mirror(rows * GROUP)
 
     def body(g, carry):
@@ -120,14 +108,61 @@
         lhs = nn(turn, block).astype(BF16)
         turned_ref[:, g] = lhs.reshape(rows, GROUP, chan)
         for s in range(rows // 8):
-            correlate_set(lhs, pad, 8 * s, g, inv_root, corr_ref, 0, 2 * s * LANES)
+            correlate_set(lhs, pad, 8 * s, g, inv_root, corr_ref, slice(0, rows), 2 * s * LANES)
         return carry
 
     for g in range(groups):
         body(g, 0)
-
-
-def row_chunks(rim_lo, corr_ref, rim_hi, r, rows):
+    copy.wait()
+    base = tn(weight[...], spread_table(SPAN * SPAN))
+    for r in range(PER):
+        wide_ref[r] = (base if r == 0 else pltpu.roll(base, r * WIN, 1)).astype(BF16)
+
+
+def edge_spot(parts, kind):
+    me = lax.axis_index("space")
+    above = lax.rem(me, 2) ^ 1 if kind == 0 else lax.rem(me, 2)
+    inside = jnp.where(above == 1, me != parts - 1, me != 0)
+    return above, inside
+
+
+def fill_halo(pad_ref, row, halo_ref, inside):
+    cols = halo_ref.shape[1]
+    pad_ref[pl.ds(row, 8), RADIUS : RADIUS + cols] = jnp.where(
+        inside, halo_ref[...], jnp.zeros(halo_ref.shape, BF16)
+    )
+
+
+def rim_scores(inv_root, parts, kind, turned_ref, halo_ref, pad, rim_ref):
+    rows, groups, _, chan = turned_ref.shape
+    half = rows // 2
+    above, inside = edge_spot(parts, kind)
+    fill_columns(pad, 0, 8, groups * GROUP)
+    fill_halo(pad, 0, halo_ref, inside)
+    start = half * above
+    for g in range(groups):
+        lhs = turned_ref[pl.ds(start, half), g].reshape(half * GROUP, chan)
+        correlate_set(lhs, pad, 0, g, inv_root, rim_ref, slice(0, half), 0)
+    return above
+
+
+def across_kernel(inv_root, parts, turned_ref, halo_ref, rim_ref, pad):
+    rim_scores(inv_root, parts, 0, turned_ref, halo_ref, pad, rim_ref)
+
+
+def slice_kernel(edit_ref, across_ref, beyond_ref, sems):
+    rows = edit_ref.shape[0]
+    odd = lax.rem(lax.axis_index("space"), 2)
+    copies = []
+    for i, (start, ref) in enumerate(((odd, beyond_ref), (1 - odd, across_ref))):
+        block = edit_ref.at[pl.ds((rows - RADIUS) * start, RADIUS)]
+        copies.append(pltpu.make_async_copy(block, ref, sems.at[i]))
+        copies[i].start()
+    for copy in copies:
+        copy.wait()
+
+
+def row_chunks(rims, corr_ref, r, rows):
     pieces = []
     half = rows // 2
     for q in range(rows // PER):
@@ -135,12 +170,12 @@
         parts = []
         for c in range(q, q + POS):
             if c < 2:
-                part = rim_lo[y, :, :, c * LANES : (c + 1) * LANES]
+                part = rims[0, y, :, :, c * LANES : (c + 1) * LANES]
             elif c < 2 + rows // PER:
                 part = corr_ref[y, :, :, (c - 2) * LANES : (c - 1) * LANES]
             else:
                 at = c - 2 - rows // PER
-                part = rim_hi[y - half, :, :, at * LANES : (at + 1) * LANES]
+                part = rims[1, y - half, :, :, at * LANES : (at + 1) * LANES]
             parts.append(part.reshape(part.shape[0] * part.shape[1], LANES))
         pieces.append(jnp.concatenate(parts, axis=1))
     return jnp.concatenate(pieces, axis=0)
@@ -152,7 +187,7 @@
     parts,
     turned_ref,
     corr_ref,
-    across_ref,
+    rim_ref,
     beyond_ref,
     wide_ref,
     bias_ref,
@@ -161,21 +196,11 @@
 ):
     gate_ref = rest[0]
     piece_refs = rest[1 : 1 + parts]
-    pad, rim_lo, rim_hi, stage = rest[1 + parts :]
-    rows, groups, _, chan = turned_ref.shape
-    half = rows // 2
-    fill_halos(pad, 0, 8, across_ref, beyond_ref, parts)
-
-    def body(g, carry):
-        lhs = turned_ref[:half, g].reshape(half * GROUP, chan)
-        correlate_set(lhs, pad, 0, g, inv_root, rim_lo, 0, 0)
-        lhs = turned_ref[half:, g].reshape(half * GROUP, chan)
-        correlate_set(lhs, pad, 8, g, inv_root, rim_hi, 0, 0)
-        return carry
-
-    for g in range(groups):
-        body(g, 0)
-
+    pad, rims, stage = rest[1 + parts :]
+    rows, groups = turned_ref.shape[:2]
+    above, _ = edge_spot(parts, 1)
+    rims[1 - above] = rim_ref[...]
+    rim_scores(inv_root, parts, 1, turned_ref, beyond_ref, pad, rims.at[above])
     bias, head = bias_ref[...], head_ref[...]
     kout = bias.shape[1]
     cols = groups * GROUP
@@ -184,7 +209,7 @@
     slopes = jnp.zeros((1, kout), F32)
     total = None
     for r in range(PER):
-        corr = row_chunks(rim_lo, corr_ref, rim_hi, r, rows)
+        corr = row_chunks(rims, corr_ref, r, rows)
         value = nt(corr, wide_ref[r]) + bias
         gating = jax.nn.sigmoid(value)
         act = value * gating
@@ -286,8 +311,11 @@
     rows, groups, _, chan = source_ref.shape
     half = rows // 2
     quarter = rows // PER
-    fill_halos(pad, 0, 8 + rows, across_ref, beyond_ref, parts)
-    fill_padded(pad, 8, edit_ref)
+    for kind, ref in ((0, across_ref), (1, beyond_ref)):
+        above, inside = edge_spot(parts, kind)
+        fill_halo(pad, (8 + rows) * above, ref, inside)
+    fill_columns(pad, 0, 16 + rows, groups * GROUP)
+    pad[8 : 8 + rows, RADIUS : RADIUS + groups * GROUP] = edit_ref[...]
     zero = jnp.zeros((PER, groups, GROUP, LANES), BF16)
     for q, c in ((1, 0), (3, 2), (0, 5), (2, 7)):
         band[q * PER : (q + 1) * PER, :, :, c * LANES : (c + 1) * LANES] = zero
@@ -347,7 +375,8 @@
 
 def gather_kernel(parts, *rest):
     piece_refs = rest[:parts]
-    conv_ref, bias_ref, head_ref, stage = rest[parts:]
+    loss_ref, conv_ref, bias_ref, head_ref, loss_out, stage = rest[parts:]
+    loss_out[...] = loss_ref[...]
     share = piece_refs[0].shape[0]
     me = lax.axis_index("space")
     for k in range(parts):
@@ -364,31 +393,24 @@
     scale = grad_ref[0:1, 0:1].reshape(1, 1, 1) * inv_root
     source_out[...] = (source_ref[...] * scale).astype(BF16)
     rows = edit_ref.shape[0]
-    me = lax.axis_index("space")
-    odd = lax.rem(me, 2) == 1
-    for row, edge, mine in ((0, 0, odd), (rows - 8, parts - 1, ~odd)):
-        own = edit_ref[row : row + 8]
-        for picked, ref in ((mine, across_ref), (~mine, beyond_ref)):
-
-            @pl.when((me != edge) & picked)
-            def _():
-                edit_out[row : row + 8] = ((own + ref[...].astype(F32)) * scale).astype(BF16)
-
-        @pl.when(me == edge)
-        def _():
-            edit_out[row : row + 8] = (own * scale).astype(BF16)
-
-
-def call(kernel, outs, scratch, flops, *args):
+    for kind, ref in ((0, across_ref), (1, beyond_ref)):
+        above, inside = edge_spot(parts, kind)
+        at = pl.ds((rows - 8) * above, 8)
+        extra = jnp.where(inside, ref[...].astype(F32), 0.0)
+        edit_out[at] = ((edit_ref[at] + extra) * scale).astype(BF16)
+
+
+def call(kernel, outs, scratch, flops, *args, far=()):
     nbytes = sum(a.size * a.dtype.itemsize for a in args)
+    spaces = [pltpu.HBM if i in far else pltpu.VMEM for i in range(len(args))]
     return pl.pallas_call(
         kernel,
         out_shape=outs,
-        in_specs=[pl.BlockSpec(memory_space=pltpu.VMEM)] * len(args),
+        in_specs=[pl.BlockSpec(memory_space=space) for space in spaces],
         scratch_shapes=scratch,
         compiler_params=pltpu.CompilerParams(vmem_limit_bytes=VMEM_LIMIT),
         cost_estimate=pl.CostEstimate(flops=flops, bytes_accessed=nbytes, transcendentals=0),
-    )(*(pltpu.with_memory_space_constraint(a, pltpu.VMEM) for a in args))
+    )(*map(pltpu.with_memory_space_constraint, args, spaces))
 
 
 def result(dims, dtype=F32):
@@ -417,12 +439,16 @@
     share = -(-(disp + 2) // (8 * space)) * 8
     edit = edit_feats[0]
     source = source_feats.reshape(rows, groups, GROUP, chan)
-    odd = lax.rem(lax.axis_index("space"), 2)
     to_across = [(i, i ^ 1 if i ^ 1 < space else i) for i in range(space)]
     to_beyond = [(i, b if 0 <= (b := i + 1 - 2 * ((i + 1) % 2)) < space else i) for i in range(space)]
-    edge_rows = rows - RADIUS
-    across = lax.dynamic_slice_in_dim(edit, edge_rows * (1 - odd), RADIUS, 0)
-    beyond = lax.dynamic_slice_in_dim(edit, edge_rows * odd, RADIUS, 0)
+    across, beyond = call(
+        slice_kernel,
+        (shape((RADIUS, columns, chan), BF16),) * 2,
+        [pltpu.SemaphoreType.DMA((2,))],
+        10**4,
+        edit,
+        far=(0,),
+    )
     across = lax.ppermute(across, "space", to_across)
     beyond = lax.ppermute(beyond, "space", to_beyond)
     turned, corr, wide = call(
@@ -432,25 +458,37 @@
             shape((rows, groups, GROUP, rows * WIN), BF16),
             shape((PER, kout, POS * LANES), BF16),
         ),
-        [pltpu.VMEM((rows, wide_cols, chan), BF16)],
+        [
+            pltpu.VMEM((rows, wide_cols, chan), BF16),
+            pltpu.VMEM((disp, kout), BF16),
+            pltpu.SemaphoreType.DMA,
+        ],
         2 * 10**9,
         source,
         edit,
         conv_weight.T,
+        far=(2,),
+    )
+    (rim,) = call(
+        functools.partial(across_kernel, inv_root, space),
+        (shape((rows // 2, groups, GROUP, 8 * WIN), BF16),),
+        [pltpu.VMEM((RADIUS, wide_cols, chan), BF16)],
+        10**9,
+        turned,
+        across,
     )
     gate, *pieces = call(
         functools.partial(outer_kernel, inv_root, pixels, space),
         (shape((rows, columns, kout), BF16),) + (shape((share + 8, kout)),) * space,
         [
-            pltpu.VMEM((2 * RADIUS, wide_cols, chan), BF16),
-            pltpu.VMEM((rows // 2, groups, GROUP, 8 * WIN), BF16),
-            pltpu.VMEM((rows // 2, groups, GROUP, 8 * WIN), BF16),
+            pltpu.VMEM((RADIUS, wide_cols, chan), BF16),
+            pltpu.VMEM((2, rows // 2, groups, GROUP, 8 * WIN), BF16),
             pltpu.VMEM((share * space, kout), F32),
         ],
         2 * 10**9,
         turned,
         corr,
-        across,
+        rim,
         beyond,
         wide,
         conv_bias[None],
@@ -491,6 +529,7 @@
         beyond,
     )
     others = [quarter] + [lax.ppermute(quarter, "pair", around("pair", k)) for k in range(1, pairs)]
+    *others, source_sum, edit_sum = lax.optimization_barrier((*others, source_sum, edit_sum))
     comps = jnp.stack([comp_first, comp_second, comp_win])
     total, score_grad, loss = call(
         functools.partial(judge_kernel, pairs),
@@ -512,12 +551,14 @@
         from_across,
         from_beyond,
     )
-    conv_grad, bias_grad, head_grad = call(
+    *gathered, source_grad, edit_grad = lax.optimization_barrier((*gathered, source_grad, edit_grad))
+    conv_grad, bias_grad, head_grad, loss = call(
         functools.partial(gather_kernel, space),
-        (result((disp, kout)), result((1, kout)), result((1, kout))),
+        (result((disp, kout)), result((1, kout)), result((1, kout)), result((1, LANES))),
         [pltpu.VMEM((share * space, kout), F32)],
         10**6,
         *gathered,
+        loss,
     )
     return (
         source_grad[None],

time: 41.9 us -> 38.9 us (0.928)
  waiting for transfers between devices: 3.79 us -> 0.71 us
  starting transfers between devices: 21.2 us -> 18.7 us
  Pallas kernels: 13.5 us -> 15.3 us
  other arithmetic: 0.03 us -> 0.72 us
    ppermute x3, waiting for transfers between devices: 2.91 us -> 0.48 us  [local(): lax.ppermute(quarter, 'pair', around('pair', k))]
    ppermute x3, starting transfers between devices: 9.58 us -> 7.68 us  [local(): quarter = quarter + lax.ppermute(pieces[k], 'space', around('space', k))]
    pallas_call x7 -> x9, Pallas kernels: 13.5 us -> 15.3 us  [call(): pl.pallas_call(kernel, out_shape=outs, in_specs=[pl.BlockSpec(memory_spac...]
    unnamed x18 -> x12, local copies, waits for them, and re-layouts: 0.92 us -> 2.51 us
    dynamic_slice x1 -> x0, local copies, waits for them, and re-layouts: 1.43 us -> none  [local(): beyond = lax.dynamic_slice_in_dim(edit, edge_rows * odd, RADIUS, 0)]
    ppermute x3, waiting for transfers between devices: 0.86 us -> 0.01 us  [local(): quarter = quarter + lax.ppermute(pieces[k], 'space', around('space', k))]
    another operation x1, other arithmetic: 0.01 us -> 0.7 us  [local(): comps = jnp.stack([comp_first, comp_second, comp_win])]
    ppermute x3, starting transfers between devices: 6.07 us -> 5.59 us  [local(): lax.ppermute(quarter, 'pair', around('pair', k))]
  transfers between devices with their start and end apart: 13 -> 13, of which waited for: 5 -> 2; matrix products, arithmetic and copies ran while one was open for 0% -> 2% of each run, Pallas kernels for 18% -> 25%
where the time goes in v2:
time: 38.9 us; the launch traced here: 38.7 us
  starting transfers between devices  18.7 us (48%)
  Pallas kernels  15.3 us (39%)
  local copies, waits for them, and re-layouts  2.51 us (6%)
  between operations  0.8 us (2%)
  other arithmetic  0.72 us (2%)
  waiting for transfers between devices  0.71 us (2%)
    pallas_call x9, Pallas kernels, call(): pl.pallas_call(kernel, out_shape=outs, in_specs=[pl.BlockSpec(memory_spac...  15.3 us
    ppermute x3, starting transfers between devices, local(): quarter = quarter + lax.ppermute(pieces[k], 'space', around('space', k))  7.68 us
    ppermute x3, starting transfers between devices, local(): lax.ppermute(quarter, 'pair', around('pair', k))  5.59 us
    ppermute x3, starting transfers between devices, local(): lax.ppermute(total, 'space', around('space', k))  3.43 us
    unnamed x12, local copies, waits for them, and re-layouts  2.51 us
  transfers between devices with their start and end apart: 13, of which 2 were waited for; matrix products, arithmetic and copies ran while one was open for 2% of the time, Pallas kernels for 25%

profile of v2, /device:TPU:0, one launch (start us, length us, event | category | flops | bytes accessed | tf_op | source)
XLA Modules:
  0.0 38.7 jit_solution(3289241254461344015)
XLA Ops:
  0.6 1.2 %shard_map.128 = (bf16[8,128,256]{2,1,0:T(8,128)(2,1)S(1)}, bf16[8,128,256]{2,1,0:T(8,128)(2,1)S(1)}) custom-call(bf16[16,128,256]{2,1,0:T(8,128)(2,1)} %bitcast.17), custom_call_target="tpu_custom_call" | custom-call | flops 10000 | bytes 1048576 | tf_op jit(solution)/shard_map/pallas_call | solution.py:406
  1.9 0.5 %collective-permute-start = (bf16[8,128,256]{2,1,0:T(8,128)(2,1)S(1)}, bf16[8,128,256]{2,1,0:T(8,128)(2,1)S(1)}, u32[]{:S(2)}, u32[]{:S(2)}) collective-permute-start(bf16[8,128,256]{2,1,0:T(8,128)(2,1)S(1)} %get-tuple-element.43), channel_id=1, source_target_pairs={{0,4},{4,0},{8,12},{12,8},{1,5},{5,1},{9,13},{13,9},{2,6},{6,2},{1... | collective-permute-start | bytes 1572872 | tf_op jit(solution)/shard_map/ppermute | solution.py:452
  2.4 0.7 %collective-permute-start.1 = (bf16[8,128,256]{2,1,0:T(8,128)(2,1)S(1)}, bf16[8,128,256]{2,1,0:T(8,128)(2,1)S(1)}, u32[]{:S(2)}, u32[]{:S(2)}) collective-permute-start(bf16[8,128,256]{2,1,0:T(8,128)(2,1)S(1)} %get-tuple-element.44), channel_id=1, source_target_pairs={{0,0},{4,8},{8,4},{12,12},{1,1},{5,9},{9,5},{13,13},{2,2},{6,10},{... | collective-permute-start | bytes 1572872 | tf_op jit(solution)/shard_map/ppermute | solution.py:453
  3.1 0.7 %pad_add_fusion.comp_ref = s32[3,16]{1,0:T(4,128)S(1)} fusion(s32[1,16]{1,0:T(1,128)} %bitcast.25, s32[1,16]{1,0:T(1,128)} %bitcast.26, s32[1,16]{1,0:T(1,128)} %bitcast.27), kind=kLoop, calls=%fused_computation.1 | loop fusion | flops 96 | bytes 384 | tf_op jit(solution)/shard_map/stack | solution.py:533
  3.8 1.2 %copy-done = bf16[1,16,128,256]{3,2,1,0:T(8,128)(2,1)S(1)} copy-done((bf16[1,16,128,256]{3,2,1,0:T(8,128)(2,1)S(1)}, bf16[1,16,128,256]{3,2,1,0:T(8,128)(2,1)}, u32[]{:S(2)}) %copy-start) | copy-done | bytes 1048600
  5.0 1.2 %copy-done.2 = bf16[1,16,128,256]{3,2,1,0:T(8,128)(2,1)S(1)} copy-done((bf16[1,16,128,256]{3,2,1,0:T(8,128)(2,1)S(1)}, bf16[1,16,128,256]{3,2,1,0:T(8,128)(2,1)}, u32[]{:S(2)}) %copy-start.2) | copy-done | bytes 1048600
  6.2 2.4 %shard_map.127 = (bf16[16,8,16,256]{3,2,1,0:T(8,128)(2,1)S(1)}, bf16[16,8,16,512]{3,2,1,0:T(8,128)(2,1)S(1)}, bf16[4,128,640]{2,1,0:T(8,128)(2,1)S(1)}) custom-call(bf16[16,8,16,256]{3,2,1,0:T(8,128)(2,1)S(1)} %bitcast.20, bf16[16,128,256]{2,1,0:T(8,128)(2,1)S(1)} %bitcast.18, bf16[289,128]{1,0:T(8,128)(2,1)} %bitcast.31), custom_call_target="tpu_custom_call" | custom-call | flops 2000000000 | bytes 2171136 | tf_op jit(solution)/shard_map/pallas_call | solution.py:406
  8.6 0.6 %shard_map.129.rim_ref = bf16[8,8,16,256]{3,2,1,0:T(8,128)(2,1)S(1)} custom-call(bf16[16,8,16,256]{3,2,1,0:T(8,128)(2,1)S(1)} %get-tuple-element.41.turned_ref, bf16[8,128,256]{2,1,0:T(8,128)(2,1)S(1)} %collective-permute-done.halo_ref.across_ref), custom_call_target="tpu_custom_call" | custom-call | flops 1000000000 | bytes 1572864 | tf_op jit(solution)/shard_map/pallas_call | solution.py:406
  9.3 3.7 %shard_map.130 = (bf16[16,128,128]{2,1,0:T(8,128)(2,1)S(1)}, f32[88,128]{1,0:T(8,128)S(1)}, f32[88,128]{1,0:T(8,128)S(1)}, f32[88,128]{1,0:T(8,128)S(1)}, f32[88,128]{1,0:T(8,128)S(1)}) custom-call(bf16[16,8,16,256]{3,2,1,0:T(8,128)(2,1)S(1)} %get-tuple-element.41.turned_ref, bf16[16,8,16,512]{3,2,1,0:T(8,128)(2,1)S(1)} %get-tuple-element.42.corr_ref, ...), custom_call_target="tpu_custom_call" | custom-call | flops 2000000000 | bytes 4850688 | tf_op jit(solution)/shard_map/pallas_call | solution.py:406
  13.0 4.6 %collective-permute-start.2 = (f32[88,128]{1,0:T(8,128)S(1)}, f32[88,128]{1,0:T(8,128)S(1)}, u32[]{:S(2)}, u32[]{:S(2)}) collective-permute-start(f32[88,128]{1,0:T(8,128)S(1)} %get-tuple-element.47), channel_id=1, source_target_pairs={{0,4},{4,8},{8,12},{12,0},{1,5},{5,9},{9,13},{13,1},{2,6},{6,10},{... | collective-permute-start | bytes 135176 | tf_op jit(solution)/shard_map/ppermute | solution.py:499
  17.6 1.7 %collective-permute-start.3 = (f32[88,128]{1,0:T(8,128)S(1)}, f32[88,128]{1,0:T(8,128)S(1)}, u32[]{:S(2)}, u32[]{:S(2)}) collective-permute-start(f32[88,128]{1,0:T(8,128)S(1)} %get-tuple-element.48), channel_id=1, source_target_pairs={{0,8},{4,12},{8,0},{12,4},{1,9},{5,13},{9,1},{13,5},{2,10},{6,14},... | collective-permute-start | bytes 135176 | tf_op jit(solution)/shard_map/ppermute | solution.py:499
  19.3 1.4 %collective-permute-start.4 = (f32[88,128]{1,0:T(8,128)S(1)}, f32[88,128]{1,0:T(8,128)S(1)}, u32[]{:S(2)}, u32[]{:S(2)}) collective-permute-start(f32[88,128]{1,0:T(8,128)S(1)} %get-tuple-element.49), channel_id=1, source_target_pairs={{0,12},{4,0},{8,4},{12,8},{1,13},{5,1},{9,5},{13,9},{2,14},{6,2},{... | collective-permute-start | bytes 135176 | tf_op jit(solution)/shard_map/ppermute | solution.py:499
  20.7 1.6 %shard_map.133 = (bf16[8,128,256]{2,1,0:T(8,128)(2,1)S(1)}, bf16[8,128,256]{2,1,0:T(8,128)(2,1)S(1)}) custom-call(bf16[16,128,128]{2,1,0:T(8,128)(2,1)S(1)} %get-tuple-element.50.gate_ref, bf16[4,128,640]{2,1,0:T(8,128)(2,1)S(1)} %get-tuple-element.45.wide_ref, bf16[16,8,16,256]{3,2,1,0:T(8,128)(2,1)S(1)} %bitcast.21), custom_call_target="tpu_custom_call" | custom-call | flops 1000000000 | bytes 2228224 | tf_op jit(solution)/shard_map/pallas_call | solution.py:406
  22.4 0.7 %collective-permute-start.12 = (bf16[8,128,256]{2,1,0:T(8,128)(2,1)S(1)}, bf16[8,128,256]{2,1,0:T(8,128)(2,1)S(1)}, u32[]{:S(2)}, u32[]{:S(2)}) collective-permute-start(bf16[8,128,256]{2,1,0:T(8,128)(2,1)S(1)} %get-tuple-element.62), channel_id=1, source_target_pairs={{0,0},{4,8},{8,4},{12,12},{1,1},{5,9},{9,5},{13,13},{2,2},{6,10},{... | collective-permute-start | bytes 1572872 | tf_op jit(solution)/shard_map/ppermute | solution.py:514
  23.2 1.6 %collective-permute-start.5 = (f32[88,128]{1,0:T(8,128)S(1)}, f32[88,128]{1,0:T(8,128)S(1)}, u32[]{:S(2)}, u32[]{:S(2)}) collective-permute-start(f32[88,128]{1,0:T(8,128)S(1)} %add_add_fusion.rest_0_), channel_id=1, source_target_pairs={{0,1},{1,2},{2,3},{3,0},{4,5},{5,6},{6,7},{7,4},{8,9},{9,10},{10,1... | collective-permute-start | bytes 135176 | tf_op jit(solution)/shard_map/ppermute | solution.py:531
  24.8 2.6 %collective-permute-start.6 = (f32[88,128]{1,0:T(8,128)S(1)}, f32[88,128]{1,0:T(8,128)S(1)}, u32[]{:S(2)}, u32[]{:S(2)}) collective-permute-start(f32[88,128]{1,0:T(8,128)S(1)} %add_add_fusion.rest_0_), channel_id=1, source_target_pairs={{0,2},{1,3},{2,0},{3,1},{4,6},{5,7},{6,4},{7,5},{8,10},{9,11},{10,... | collective-permute-start | bytes 135176 | tf_op jit(solution)/shard_map/ppermute | solution.py:531
  27.4 1.4 %collective-permute-start.7 = (f32[88,128]{1,0:T(8,128)S(1)}, f32[88,128]{1,0:T(8,128)S(1)}, u32[]{:S(2)}, u32[]{:S(2)}) collective-permute-start(f32[88,128]{1,0:T(8,128)S(1)} %add_add_fusion.rest_0_), channel_id=1, source_target_pairs={{0,3},{1,0},{2,1},{3,2},{4,7},{5,4},{6,5},{7,6},{8,11},{9,8},{10,9... | collective-permute-start | bytes 135176 | tf_op jit(solution)/shard_map/ppermute | solution.py:531
  28.7 3.0 %shard_map.131 = (f32[16,8,16,256]{3,2,1,0:T(8,128)S(1)}, f32[16,128,256]{2,1,0:T(8,128)S(1)}) custom-call(bf16[16,128,128]{2,1,0:T(8,128)(2,1)S(1)} %get-tuple-element.50.gate_ref, bf16[4,128,640]{2,1,0:T(8,128)(2,1)S(1)} %get-tuple-element.45.wide_ref, bf16[16,8,16,256]{3,2,1,0:T(8,128)(2,1)S(1)} %bitcast.22, bf16[16,128,256]{2,1,0:T(8,128)(2,1)S(1)} %bitcast.19, ...), custom_call_target="tpu_custom_call" | custom-call | flops 4000000000 | bytes 4325376 | tf_op jit(solution)/shard_map/pallas_call | solution.py:406
  31.7 0.5 %collective-permute-done.7.rest_3_ = f32[88,128]{1,0:T(8,128)S(1)} collective-permute-done((f32[88,128]{1,0:T(8,128)S(1)}, f32[88,128]{1,0:T(8,128)S(1)}, u32[]{:S(2)}, u32[]{:S(2)}) %collective-permute-start.7) | collective-permute-done | bytes 45088 | tf_op jit(solution)/shard_map/ppermute | solution.py:531
  32.4 0.5 %collective-permute-start.8 = (f32[80,128]{1,0:T(8,128)S(1)}, f32[80,128]{1,0:T(8,128)S(1)}, u32[]{:S(2)}, u32[]{:S(2)}) collective-permute-start(f32[80,128]{1,0:T(8,128)S(1)} %get-tuple-element.67.rest_0_), channel_id=1, source_target_pairs={{0,4},{4,8},{8,12},{12,0},{1,5},{5,9},{9,13},{13,1},{2,6},{6,10},{... | collective-permute-start | bytes 122888 | tf_op jit(solution)/shard_map/ppermute | solution.py:542
  32.9 2.9 %collective-permute-start.9 = (f32[80,128]{1,0:T(8,128)S(1)}, f32[80,128]{1,0:T(8,128)S(1)}, u32[]{:S(2)}, u32[]{:S(2)}) collective-permute-start(f32[80,128]{1,0:T(8,128)S(1)} %get-tuple-element.67.rest_0_), channel_id=1, source_target_pairs={{0,8},{4,12},{8,0},{12,4},{1,9},{5,13},{9,1},{13,5},{2,10},{6,14},... | collective-permute-start | bytes 122888 | tf_op jit(solution)/shard_map/ppermute | solution.py:542
  35.8 1.9 %shard_map.134 = (bf16[16,128,256]{2,1,0:T(8,128)(2,1)}, bf16[16,128,256]{2,1,0:T(8,128)(2,1)}) custom-call(f32[8,128]{1,0:T(8,128)S(1)} %get-tuple-element.58.grad_ref, f32[16,128,256]{2,1,0:T(8,128)S(1)} %bitcast.16, f32[16,128,256]{2,1,0:T(8,128)S(1)} %get-tuple-element.60.edit_ref, bf16[8,128,256]{2,1,0:T(8,128)(2,1)S(1)} %collective-permute-done.11.across_ref, ...), custom_call_target="tpu_custom_call" | custom-call | flops 10000000 | bytes 5246976 | tf_op jit(solution)/shard_map/pallas_call | solution.py:406
  37.8 0.2 collective-permute-done.9.rest_2_
  38.0 0.7 %shard_map.135 = (f32[289,128]{1,0:T(8,128)}, f32[1,128]{1,0:T(1,128)}, f32[1,128]{1,0:T(1,128)}, f32[1,128]{1,0:T(1,128)}) custom-call(f32[80,128]{1,0:T(8,128)S(1)} %get-tuple-element.67.rest_0_, f32[80,128]{1,0:T(8,128)S(1)} %collective-permute-done.8.rest_1_, f32[80,128]{1,0:T(8,128)S(1)} %collective-permute-done.9.rest_2_, ...), custom_call_target="tpu_custom_call" | custom-call | flops 1000000 | bytes 164352 | tf_op jit(solution)/shard_map/pallas_call | solution.py:406
  (25 shorter events, 0.4 us)
Async XLA Ops:
  1.9 6.8 %collective-permute-start = (bf16[8,128,256]{2,1,0:T(8,128)(2,1)S(1)}, bf16[8,128,256]{2,1,0:T(8,128)(2,1)S(1)}, u32[]{:S(2)}, u32[]{:S(2)}) collective-permute-start(bf16[8,128,256]{2,1,0:T(8,128)(2,1)S(1)} %get-tuple-element.43), channel_id=1, source_target_pairs={{0,4},{4,0},{8,12},{12,8},{1,5},{5,1},{9,13},{13,9},{2,6},{6,2},{1... | collective-permute-start | bytes 1572872 | tf_op jit(solution)/shard_map/ppermute | solution.py:452
  2.4 6.8 %collective-permute-start.1 = (bf16[8,128,256]{2,1,0:T(8,128)(2,1)S(1)}, bf16[8,128,256]{2,1,0:T(8,128)(2,1)S(1)}, u32[]{:S(2)}, u32[]{:S(2)}) collective-permute-start(bf16[8,128,256]{2,1,0:T(8,128)(2,1)S(1)} %get-tuple-element.44), channel_id=1, source_target_pairs={{0,0},{4,8},{8,4},{12,12},{1,1},{5,9},{9,5},{13,13},{2,2},{6,10},{... | collective-permute-start | bytes 1572872 | tf_op jit(solution)/shard_map/ppermute | solution.py:453
  3.8 1.2 %copy-start = (bf16[1,16,128,256]{3,2,1,0:T(8,128)(2,1)S(1)}, bf16[1,16,128,256]{3,2,1,0:T(8,128)(2,1)}, u32[]{:S(2)}) copy-start(bf16[1,16,128,256]{3,2,1,0:T(8,128)(2,1)} %param.9) | copy-start | bytes 3145732
  5.0 1.2 %copy-start.2 = (bf16[1,16,128,256]{3,2,1,0:T(8,128)(2,1)S(1)}, bf16[1,16,128,256]{3,2,1,0:T(8,128)(2,1)}, u32[]{:S(2)}) copy-start(bf16[1,16,128,256]{3,2,1,0:T(8,128)(2,1)} %param.8) | copy-start | bytes 3145732
  8.6 0.7 %copy-start.4 = (f32[128]{0:T(128)S(1)}, f32[128]{0:T(128)}, u32[]{:S(2)}) copy-start(f32[128]{0:T(128)} %param.11) | copy-start | bytes 1540
  8.6 0.7 %copy-start.5 = (f32[128]{0:T(128)S(1)}, f32[128]{0:T(128)}, u32[]{:S(2)}) copy-start(f32[128]{0:T(128)} %param.12) | copy-start | bytes 1540
  9.3 11.4 %copy-start.3 = (bf16[1,16,128,256]{3,2,1,0:T(8,128)(2,1)S(1)}, bf16[1,16,128,256]{3,2,1,0:T(8,128)(2,1)}, u32[]{:S(2)}) copy-start(bf16[1,16,128,256]{3,2,1,0:T(8,128)(2,1)} %param.8) | copy-start | bytes 3145732
  13.0 15.8 %copy-start.1 = (bf16[1,16,128,256]{3,2,1,0:T(8,128)(2,1)S(1)}, bf16[1,16,128,256]{3,2,1,0:T(8,128)(2,1)}, u32[]{:S(2)}) copy-start(bf16[1,16,128,256]{3,2,1,0:T(8,128)(2,1)} %param.9) | copy-start | bytes 3145732
  13.0 10.1 %collective-permute-start.2 = (f32[88,128]{1,0:T(8,128)S(1)}, f32[88,128]{1,0:T(8,128)S(1)}, u32[]{:S(2)}, u32[]{:S(2)}) collective-permute-start(f32[88,128]{1,0:T(8,128)S(1)} %get-tuple-element.47), channel_id=1, source_target_pairs={{0,4},{4,8},{8,12},{12,0},{1,5},{5,9},{9,13},{13,1},{2,6},{6,10},{... | collective-permute-start | bytes 135176 | tf_op jit(solution)/shard_map/ppermute | solution.py:499
  17.6 5.5 %collective-permute-start.3 = (f32[88,128]{1,0:T(8,128)S(1)}, f32[88,128]{1,0:T(8,128)S(1)}, u32[]{:S(2)}, u32[]{:S(2)}) collective-permute-start(f32[88,128]{1,0:T(8,128)S(1)} %get-tuple-element.48), channel_id=1, source_target_pairs={{0,8},{4,12},{8,0},{12,4},{1,9},{5,13},{9,1},{13,5},{2,10},{6,14},... | collective-permute-start | bytes 135176 | tf_op jit(solution)/shard_map/ppermute | solution.py:499
  19.3 3.8 %collective-permute-start.4 = (f32[88,128]{1,0:T(8,128)S(1)}, f32[88,128]{1,0:T(8,128)S(1)}, u32[]{:S(2)}, u32[]{:S(2)}) collective-permute-start(f32[88,128]{1,0:T(8,128)S(1)} %get-tuple-element.49), channel_id=1, source_target_pairs={{0,12},{4,0},{8,4},{12,8},{1,13},{5,1},{9,5},{13,9},{2,14},{6,2},{... | collective-permute-start | bytes 135176 | tf_op jit(solution)/shard_map/ppermute | solution.py:499
  22.3 13.5 %collective-permute-start.11 = (bf16[8,128,256]{2,1,0:T(8,128)(2,1)S(1)}, bf16[8,128,256]{2,1,0:T(8,128)(2,1)S(1)}, u32[]{:S(2)}, u32[]{:S(2)}) collective-permute-start(bf16[8,128,256]{2,1,0:T(8,128)(2,1)S(1)} %get-tuple-element.61), channel_id=1, source_target_pairs={{0,4},{4,0},{8,12},{12,8},{1,5},{5,1},{9,13},{13,9},{2,6},{6,2},{1... | collective-permute-start | bytes 1572872 | tf_op jit(solution)/shard_map/ppermute | solution.py:513
  22.4 13.4 %collective-permute-start.12 = (bf16[8,128,256]{2,1,0:T(8,128)(2,1)S(1)}, bf16[8,128,256]{2,1,0:T(8,128)(2,1)S(1)}, u32[]{:S(2)}, u32[]{:S(2)}) collective-permute-start(bf16[8,128,256]{2,1,0:T(8,128)(2,1)S(1)} %get-tuple-element.62), channel_id=1, source_target_pairs={{0,0},{4,8},{8,4},{12,12},{1,1},{5,9},{9,5},{13,13},{2,2},{6,10},{... | collective-permute-start | bytes 1572872 | tf_op jit(solution)/shard_map/ppermute | solution.py:514
  23.2 8.6 %collective-permute-start.5 = (f32[88,128]{1,0:T(8,128)S(1)}, f32[88,128]{1,0:T(8,128)S(1)}, u32[]{:S(2)}, u32[]{:S(2)}) collective-permute-start(f32[88,128]{1,0:T(8,128)S(1)} %add_add_fusion.rest_0_), channel_id=1, source_target_pairs={{0,1},{1,2},{2,3},{3,0},{4,5},{5,6},{6,7},{7,4},{8,9},{9,10},{10,1... | collective-permute-start | bytes 135176 | tf_op jit(solution)/shard_map/ppermute | solution.py:531
  24.8 6.9 %collective-permute-start.6 = (f32[88,128]{1,0:T(8,128)S(1)}, f32[88,128]{1,0:T(8,128)S(1)}, u32[]{:S(2)}, u32[]{:S(2)}) collective-permute-start(f32[88,128]{1,0:T(8,128)S(1)} %add_add_fusion.rest_0_), channel_id=1, source_target_pairs={{0,2},{1,3},{2,0},{3,1},{4,6},{5,7},{6,4},{7,5},{8,10},{9,11},{10,... | collective-permute-start | bytes 135176 | tf_op jit(solution)/shard_map/ppermute | solution.py:531
  27.4 4.8 %collective-permute-start.7 = (f32[88,128]{1,0:T(8,128)S(1)}, f32[88,128]{1,0:T(8,128)S(1)}, u32[]{:S(2)}, u32[]{:S(2)}) collective-permute-start(f32[88,128]{1,0:T(8,128)S(1)} %add_add_fusion.rest_0_), channel_id=1, source_target_pairs={{0,3},{1,0},{2,1},{3,2},{4,7},{5,4},{6,5},{7,6},{8,11},{9,8},{10,9... | collective-permute-start | bytes 135176 | tf_op jit(solution)/shard_map/ppermute | solution.py:531
  32.4 5.4 %collective-permute-start.10 = (f32[80,128]{1,0:T(8,128)S(1)}, f32[80,128]{1,0:T(8,128)S(1)}, u32[]{:S(2)}, u32[]{:S(2)}) collective-permute-start(f32[80,128]{1,0:T(8,128)S(1)} %get-tuple-element.67.rest_0_), channel_id=1, source_target_pairs={{0,12},{4,0},{8,4},{12,8},{1,13},{5,1},{9,5},{13,9},{2,14},{6,2},{... | collective-permute-start | bytes 122888 | tf_op jit(solution)/shard_map/ppermute | solution.py:542
  32.4 5.3 %collective-permute-start.8 = (f32[80,128]{1,0:T(8,128)S(1)}, f32[80,128]{1,0:T(8,128)S(1)}, u32[]{:S(2)}, u32[]{:S(2)}) collective-permute-start(f32[80,128]{1,0:T(8,128)S(1)} %get-tuple-element.67.rest_0_), channel_id=1, source_target_pairs={{0,4},{4,8},{8,12},{12,0},{1,5},{5,9},{9,13},{13,1},{2,6},{6,10},{... | collective-permute-start | bytes 122888 | tf_op jit(solution)/shard_map/ppermute | solution.py:542
  32.9 5.0 %collective-permute-start.9 = (f32[80,128]{1,0:T(8,128)S(1)}, f32[80,128]{1,0:T(8,128)S(1)}, u32[]{:S(2)}, u32[]{:S(2)}) collective-permute-start(f32[80,128]{1,0:T(8,128)S(1)} %get-tuple-element.67.rest_0_), channel_id=1, source_target_pairs={{0,8},{4,12},{8,0},{12,4},{1,9},{5,13},{9,1},{13,5},{2,10},{6,14},... | collective-permute-start | bytes 122888 | tf_op jit(solution)/shard_map/ppermute | solution.py:542

commit v3 on v2

--- a/solution.py
+++ b/solution.py
@@ -41,10 +41,19 @@
     return (col == (row ^ (GROUP - 1))).astype(F32).astype(BF16)
 
 
-def spread_table(rows):
-    row, lane = iota((rows, POS * LANES), 0), iota((rows, POS * LANES), 1)
+def spread(p):
+    first = p * PER * SPAN
+    return first // 8 * 8, first % 8
+
+
+def spread_table(p, dim):
+    _, offset = spread(p)
+    count = (PER if p < POS - 1 else 1) * SPAN
+    dims = [LANES, LANES]
+    dims[dim] = -(-(count + offset) // 8) * 8 if p < POS - 1 else count
+    place, lane = iota(dims, dim), iota(dims, 1 - dim)
     dy, t = lane // WIN, lane % WIN
-    hit = (row == dy * SPAN + t) & (t < SPAN) & (dy < SPAN)
+    hit = (place == dy * SPAN + t + offset) & (t < SPAN) & (dy * SPAN < count)
     return hit.astype(F32).astype(BF16)
 
 
@@ -85,38 +94,67 @@
         out_ref[spot, g, :, at : at + LANES] = part.astype(BF16)
 
 
+def spread_weights(weight, wide_ref, tall_ref):
+    kout = weight.shape[1]
+    wides, talls = [], []
+    for p in range(POS):
+        row, _ = spread(p)
+        table = spread_table(p, 0)
+        part = weight[row : row + table.shape[0], :]
+        wides.append(tn(part, table))
+        talls.append(nn(spread_table(p, 1), part))
+    base = jnp.concatenate(wides, axis=1)
+    tall = jnp.concatenate(talls, axis=0).astype(BF16)[: SPAN * WIN]
+    tall_rows = tall_ref.shape[1]
+    for r in range(PER):
+        wide_ref[r] = (base if r == 0 else pltpu.roll(base, r * WIN, 1)).astype(BF16)
+        start = LANES + r * WIN
+        tall_ref[r, :start] = jnp.zeros((start, kout), BF16)
+        tall_ref[r, start : start + SPAN * WIN] = tall
+        tall_ref[r, start + SPAN * WIN :] = jnp.zeros((tall_rows - start - SPAN * WIN, kout), BF16)
+
+
 def inner_kernel(
     inv_root,
+    source_hbm,
+    edit_hbm,
+    weight_hbm,
     source_ref,
-    edit_ref,
-    weight_ref,
+    pad,
     turned_ref,
     corr_ref,
     wide_ref,
-    pad,
+    tall_ref,
+    own_ref,
     weight,
-    weight_sem,
+    sems,
 ):
     rows, groups, _, chan = source_ref.shape
-    copy = pltpu.make_async_copy(weight_ref, weight, weight_sem)
-    copy.start()
-    fill_padded(pad, 0, edit_ref)
+    weight_copy = pltpu.make_async_copy(weight_hbm, weight, sems.at[2])
+    weight_copy.start()
+    copies = []
+    cols = groups * GROUP
+    edit_copy = pltpu.make_async_copy(edit_hbm, pad.at[:, RADIUS : RADIUS + cols], sems.at[0])
+    source_copy = pltpu.make_async_copy(source_hbm, source_ref, sems.at[1])
+    edit_copy.start()
+    source_copy.start()
+    fill_columns(pad, 0, rows, groups * GROUP)
     turn = mirror(rows * GROUP)
-
-    def body(g, carry):
-        block = source_ref[:, g].reshape(rows * GROUP, chan)
-        lhs = nn(turn, block).astype(BF16)
+    weight_copy.wait()
+    spread_weights(weight, wide_ref, tall_ref)
+    source_copy.wait()
+    edit_copy.wait()
+    for g in range(groups):
+        lhs = nn(turn, source_ref[:, g].reshape(rows * GROUP, chan)).astype(BF16)
         turned_ref[:, g] = lhs.reshape(rows, GROUP, chan)
         for s in range(rows // 8):
             correlate_set(lhs, pad, 8 * s, g, inv_root, corr_ref, slice(0, rows), 2 * s * LANES)
-        return carry
-
-    for g in range(groups):
-        body(g, 0)
-    copy.wait()
-    base = tn(weight[...], spread_table(SPAN * SPAN))
-    for r in range(PER):
-        wide_ref[r] = (base if r == 0 else pltpu.roll(base, r * WIN, 1)).astype(BF16)
+    cols = groups * GROUP
+    for q in range(rows // PER):
+        start = (3 - q) * LANES
+        for r in range(PER):
+            lhs = corr_ref[q * PER + r].reshape(cols, 4 * LANES)
+            own_ref[q * PER + r] = nn(lhs, tall_ref[r, start : start + 4 * LANES])
 
 
 def edge_spot(parts, kind):
@@ -146,18 +184,37 @@
     return above
 
 
-def across_kernel(inv_root, parts, turned_ref, halo_ref, rim_ref, pad):
-    rim_scores(inv_root, parts, 0, turned_ref, halo_ref, pad, rim_ref)
+def rim_values(rim_ref, tall_ref, above, out_ref):
+    half, groups, _, lanes = rim_ref.shape
+    for i in range(half):
+        q, r = i // PER, i % PER
+        start = pl.multiple_of((1 - q) * LANES + above * 4 * LANES, LANES)
+        lhs = rim_ref[i].reshape(groups * GROUP, lanes)
+        out_ref[i] = nn(lhs, tall_ref[r, pl.ds(start, lanes), :])
+
+
+def across_kernel(
+    inv_root, parts, turned_ref, halo_ref, tall_ref, rim_ref, extra_ref, pad
+):
+    above = rim_scores(inv_root, parts, 0, turned_ref, halo_ref, pad, rim_ref)
+    rim_values(rim_ref, tall_ref, above, extra_ref)
 
 
 def slice_kernel(edit_ref, across_ref, beyond_ref, sems):
     rows = edit_ref.shape[0]
     odd = lax.rem(lax.axis_index("space"), 2)
     copies = []
-    for i, (start, ref) in enumerate(((odd, beyond_ref), (1 - odd, across_ref))):
-        block = edit_ref.at[pl.ds((rows - RADIUS) * start, RADIUS)]
-        copies.append(pltpu.make_async_copy(block, ref, sems.at[i]))
-        copies[i].start()
+    count = sems.shape[0] // 2
+    step = RADIUS // count
+    for start, ref in ((odd, beyond_ref), (1 - odd, across_ref)):
+        for i in range(count):
+            block = edit_ref.at[pl.ds((rows - RADIUS) * start + i * step, step)]
+            copies.append(
+                pltpu.make_async_copy(
+                    block, ref.at[i * step : (i + 1) * step], sems.at[len(copies)]
+                )
+            )
+            copies[-1].start()
     for copy in copies:
         copy.wait()
 
@@ -188,19 +245,23 @@
     turned_ref,
     corr_ref,
     rim_ref,
+    extra_ref,
+    own_ref,
     beyond_ref,
-    wide_ref,
+    tall_ref,
     bias_ref,
     head_ref,
     *rest,
 ):
     gate_ref = rest[0]
     piece_refs = rest[1 : 1 + parts]
-    pad, rims, stage = rest[1 + parts :]
+    pad, rims, extra, stage = rest[1 + parts :]
     rows, groups = turned_ref.shape[:2]
     above, _ = edge_spot(parts, 1)
     rims[1 - above] = rim_ref[...]
+    extra[1 - above] = extra_ref[...]
     rim_scores(inv_root, parts, 1, turned_ref, beyond_ref, pad, rims.at[above])
+    rim_values(rims.at[above], tall_ref, above, extra.at[above])
     bias, head = bias_ref[...], head_ref[...]
     kout = bias.shape[1]
     cols = groups * GROUP
@@ -210,7 +271,8 @@
     total = None
     for r in range(PER):
         corr = row_chunks(rims, corr_ref, r, rows)
-        value = nt(corr, wide_ref[r]) + bias
+        spots = [(q * PER + r, q // 2, q % 2 * PER + r) for q in range(rows // PER)]
+        value = jnp.concatenate([own_ref[y] + extra[h, i] for y, h, i in spots], axis=0) + bias
         gating = jax.nn.sigmoid(value)
         act = value * gating
         slope = gating * (1.0 + value * (1.0 - gating))
@@ -224,20 +286,26 @@
             grad = pltpu.roll(grad, POS * LANES - r * WIN, 1)
         total = grad if total is None else total + grad
     share = stage.shape[0] // parts
-    table = spread_table(stage.shape[0])
-    first = total.astype(BF16)
-    left = total - first.astype(F32)
-    second = left.astype(BF16)
-    third = (left - second.astype(F32)).astype(BF16)
-    packed = nt(table, first) + nt(table, second) + nt(table, third)
+    stage[...] = jnp.zeros(stage.shape, F32)
+    for p in range(POS):
+        row, _ = spread(p)
+        table = spread_table(p, 0)
+        left = total[:, p * LANES : (p + 1) * LANES]
+        packed = None
+        for _ in range(3):
+            term = left.astype(BF16)
+            left = left - term.astype(F32)
+            part = nt(table, term)
+            packed = part if packed is None else packed + part
+        stage[row : row + table.shape[0]] += packed
     scale = 1.0 / pixels
-    stage[...] = packed * scale
+    stage[:STAT] = stage[:STAT] * scale
     stage[STAT : STAT + 1] = head * slopes * scale
     stage[STAT + 1 : STAT + 2] = hidden * scale
     score = jnp.sum(hidden * head, axis=1, keepdims=True) * scale
     me = lax.axis_index("space")
     for k in range(parts):
-        start = pl.multiple_of(lax.rem(me + k, parts) * share, 8)
+        start = pl.multiple_of(partner(me, k, parts) * share, 8)
         piece_refs[k][:share] = stage[pl.ds(start, share), :]
         piece_refs[k][share:] = jnp.broadcast_to(score, (8, kout))
 
@@ -299,7 +367,7 @@
     gate_ref,
     wide_ref,
     source_ref,
-    edit_ref,
+    own_pad,
     across_ref,
     beyond_ref,
     source_out,
@@ -313,9 +381,8 @@
     quarter = rows // PER
     for kind, ref in ((0, across_ref), (1, beyond_ref)):
         above, inside = edge_spot(parts, kind)
-        fill_halo(pad, (8 + rows) * above, ref, inside)
-    fill_columns(pad, 0, 16 + rows, groups * GROUP)
-    pad[8 : 8 + rows, RADIUS : RADIUS + groups * GROUP] = edit_ref[...]
+        fill_halo(pad, 8 * above, ref, inside)
+    fill_columns(pad, 0, 16, groups * GROUP)
     zero = jnp.zeros((PER, groups, GROUP, LANES), BF16)
     for q, c in ((1, 0), (3, 2), (0, 5), (2, 7)):
         band[q * PER : (q + 1) * PER, :, :, c * LANES : (c + 1) * LANES] = zero
@@ -328,16 +395,18 @@
 
     def body(g, carry):
         start = g * GROUP
-        rhs = source_ref[:, g].reshape(rows * GROUP, chan)
+        near = source_ref[:, g].reshape(rows * GROUP, chan)
         for s in range(rows // 8):
             at = (2 + 2 * s) * LANES
             lhs = band[:, g, :, at : at + 2 * LANES].reshape(rows * GROUP, 2 * LANES)
-            grad = tn(lhs, rhs).reshape(8, WIN, chan)
+            grad = tn(lhs, near).reshape(8, WIN, chan)
             sums[8 * s : 8 * s + 8, start : start + WIN, :] += grad
         for i in range(2):
             at = i * 2 * LANES
             lhs = band[i * half : (i + 1) * half, g, :, at : at + 6 * LANES]
-            grad = nn(lhs.reshape(half * GROUP, 6 * LANES), window(pad, 8 * i, 24, g))
+            spots = [window(pad, 8 * i, 8, g), window(own_pad, 0, rows, g)]
+            rhs = jnp.concatenate(spots[::-1] if i else spots, axis=0)
+            grad = nn(lhs.reshape(half * GROUP, 6 * LANES), rhs)
             source_out[i * half : (i + 1) * half, g] = grad.reshape(half, GROUP, chan)
         return carry
 
@@ -347,15 +416,21 @@
     edit_out[...] = sums[:, RADIUS : RADIUS + cols]
 
 
-def judge_kernel(pairs, comp_ref, *rest):
+def partner(me, step, count):
+    if count & (count - 1):
+        return (me + step + count) % count
+    return me ^ abs(step)
+
+
+def judge_kernel(pairs, first_ref, second_ref, win_ref, *rest):
     piece_refs = rest[:pairs]
     total_ref, grad_ref, loss_ref = rest[pairs:]
     share = total_ref.shape[0]
     me = lax.axis_index("pair")
-    first, second, win = comp_ref[0:1], comp_ref[1:2], comp_ref[2:3]
+    first, second, win = first_ref[...], second_ref[...], win_ref[...]
     hots, margin = [], jnp.zeros(first.shape, F32)
     for k in range(pairs):
-        pid = lax.rem(me - k + pairs, pairs)
+        pid = partner(me, -k, pairs)
         hot = (first == pid).astype(F32) - (second == pid).astype(F32)
         score = piece_refs[k][share : share + 1, 0:1]
         margin = margin + hot * score
@@ -380,7 +455,7 @@
     share = piece_refs[0].shape[0]
     me = lax.axis_index("space")
     for k in range(parts):
-        start = pl.multiple_of(lax.rem(me - k + parts, parts) * share, 8)
+        start = pl.multiple_of(partner(me, -k, parts) * share, 8)
         stage[pl.ds(start, share), :] = piece_refs[k][...]
     conv_ref[...] = stage[: conv_ref.shape[0]]
     bias_ref[...] = stage[STAT : STAT + 1]
@@ -388,25 +463,50 @@
 
 
 def finish_kernel(
-    inv_root, parts, grad_ref, source_ref, edit_ref, across_ref, beyond_ref, source_out, edit_out
+    inv_root,
+    parts,
+    grad_ref,
+    source_ref,
+    edit_ref,
+    across_ref,
+    beyond_ref,
+    source_hbm,
+    edit_hbm,
+    source_out,
+    edit_out,
+    sems,
 ):
     scale = grad_ref[0:1, 0:1].reshape(1, 1, 1) * inv_root
-    source_out[...] = (source_ref[...] * scale).astype(BF16)
     rows = edit_ref.shape[0]
+    copies = []
+
+    def send(out, hbm, at):
+        copies.append(pltpu.make_async_copy(out.at[at], hbm.at[at], sems.at[len(copies)]))
+        copies[-1].start()
+
+    for y in range(0, rows, 4):
+        at = slice(y, y + 4)
+        source_out[at] = (source_ref[at] * scale).astype(BF16)
+        send(source_out, source_hbm, at)
     for kind, ref in ((0, across_ref), (1, beyond_ref)):
         above, inside = edge_spot(parts, kind)
-        at = pl.ds((rows - 8) * above, 8)
-        extra = jnp.where(inside, ref[...].astype(F32), 0.0)
-        edit_out[at] = ((edit_ref[at] + extra) * scale).astype(BF16)
-
-
-def call(kernel, outs, scratch, flops, *args, far=()):
+        for y in (0, 4):
+            at = pl.ds((rows - 8) * above + y, 4)
+            extra = jnp.where(inside, ref[y : y + 4].astype(F32), 0.0)
+            edit_out[at] = ((edit_ref[at] + extra) * scale).astype(BF16)
+            send(edit_out, edit_hbm, at)
+    for copy in copies:
+        copy.wait()
+
+
+def call(kernel, outs, scratch, flops, *args, far=(), far_out=False):
     nbytes = sum(a.size * a.dtype.itemsize for a in args)
     spaces = [pltpu.HBM if i in far else pltpu.VMEM for i in range(len(args))]
     return pl.pallas_call(
         kernel,
         out_shape=outs,
         in_specs=[pl.BlockSpec(memory_space=space) for space in spaces],
+        **({"out_specs": [pl.BlockSpec(memory_space=pltpu.HBM)] * len(outs)} if far_out else {}),
         scratch_shapes=scratch,
         compiler_params=pltpu.CompilerParams(vmem_limit_bytes=VMEM_LIMIT),
         cost_estimate=pl.CostEstimate(flops=flops, bytes_accessed=nbytes, transcendentals=0),
@@ -423,7 +523,7 @@
 
 def around(axis, step):
     count = lax.axis_size(axis)
-    return [(i, (i + step) % count) for i in range(count)]
+    return [(i, partner(i, step, count)) for i in range(count)]
 
 
 def local(
@@ -451,46 +551,52 @@
     )
     across = lax.ppermute(across, "space", to_across)
     beyond = lax.ppermute(beyond, "space", to_beyond)
-    turned, corr, wide = call(
+    near = (rows, groups, GROUP, chan)
+    rim_shape = (rows // 2, groups, GROUP, 8 * WIN)
+    held, own_pad, turned, corr, wide, tall, own = call(
         functools.partial(inner_kernel, inv_root),
         (
-            shape((rows, groups, GROUP, chan), BF16),
+            shape(near, BF16),
+            shape((rows, wide_cols, chan), BF16),
+            shape(near, BF16),
             shape((rows, groups, GROUP, rows * WIN), BF16),
             shape((PER, kout, POS * LANES), BF16),
+            shape((PER, (POS + 2) * LANES, kout), BF16),
+            shape((rows, columns, kout)),
         ),
-        [
-            pltpu.VMEM((rows, wide_cols, chan), BF16),
-            pltpu.VMEM((disp, kout), BF16),
-            pltpu.SemaphoreType.DMA,
-        ],
+        [pltpu.VMEM((disp, kout), BF16), pltpu.SemaphoreType.DMA((3,))],
         2 * 10**9,
         source,
         edit,
         conv_weight.T,
-        far=(2,),
-    )
-    (rim,) = call(
+        far=(0, 1, 2),
+    )
+    rim, extra = call(
         functools.partial(across_kernel, inv_root, space),
-        (shape((rows // 2, groups, GROUP, 8 * WIN), BF16),),
+        (shape(rim_shape, BF16), shape((rows // 2, columns, kout))),
         [pltpu.VMEM((RADIUS, wide_cols, chan), BF16)],
         10**9,
         turned,
         across,
+        tall,
     )
     gate, *pieces = call(
         functools.partial(outer_kernel, inv_root, pixels, space),
         (shape((rows, columns, kout), BF16),) + (shape((share + 8, kout)),) * space,
         [
             pltpu.VMEM((RADIUS, wide_cols, chan), BF16),
-            pltpu.VMEM((2, rows // 2, groups, GROUP, 8 * WIN), BF16),
+            pltpu.VMEM((2,) + rim_shape, BF16),
+            pltpu.VMEM((2, rows // 2, columns, kout), F32),
             pltpu.VMEM((share * space, kout), F32),
         ],
         2 * 10**9,
         turned,
         corr,
         rim,
+        extra,
+        own,
         beyond,
-        wide,
+        tall,
         conv_bias[None],
         head_weight[None],
     )
@@ -508,7 +614,7 @@
         10**9,
         gate,
         wide,
-        source,
+        held,
     )
     from_across = lax.ppermute(rim_across, "space", to_across)
     from_beyond = lax.ppermute(rim_beyond, "space", to_beyond)
@@ -516,40 +622,46 @@
         functools.partial(back_kernel, space),
         (shape((rows, groups, GROUP, chan)), shape((rows, columns, chan))),
         [
-            pltpu.VMEM((rows + 2 * RADIUS, wide_cols, chan), BF16),
+            pltpu.VMEM((2 * RADIUS, wide_cols, chan), BF16),
             pltpu.VMEM((rows, groups, GROUP, (rows + 2 * RADIUS) * WIN), BF16),
             pltpu.VMEM((rows, wide_cols, chan), F32),
         ],
         4 * 10**9,
         gate,
         wide,
-        source,
-        edit,
+        held,
+        own_pad,
         across,
         beyond,
     )
     others = [quarter] + [lax.ppermute(quarter, "pair", around("pair", k)) for k in range(1, pairs)]
     *others, source_sum, edit_sum = lax.optimization_barrier((*others, source_sum, edit_sum))
-    comps = jnp.stack([comp_first, comp_second, comp_win])
     total, score_grad, loss = call(
         functools.partial(judge_kernel, pairs),
         (shape((share, kout)), shape((8, LANES)), shape((1, LANES))),
         [],
         10**6,
-        comps,
+        comp_first[None],
+        comp_second[None],
+        comp_win[None],
         *others,
     )
     gathered = [total] + [lax.ppermute(total, "space", around("space", k)) for k in range(1, space)]
     source_grad, edit_grad = call(
         functools.partial(finish_kernel, inv_root, space),
         (result((rows, columns, chan), BF16),) * 2,
-        [],
+        [
+            pltpu.VMEM((rows, columns, chan), BF16),
+            pltpu.VMEM((rows, columns, chan), BF16),
+            pltpu.SemaphoreType.DMA((8,)),
+        ],
         10**7,
         score_grad,
         source_sum.reshape(rows, columns, chan),
         edit_sum,
         from_across,
         from_beyond,
+        far_out=True,
     )
     *gathered, source_grad, edit_grad = lax.optimization_barrier((*gathered, source_grad, edit_grad))
     conv_grad, bias_grad, head_grad, loss = call(

time: 38.9 us -> 36.6 us (0.941)
  local copies, waits for them, and re-layouts: 2.51 us -> 0.02 us
  waiting for transfers between devices: 0.71 us -> 3.15 us
  starting transfers between devices: 18.7 us -> 16.7 us
  other arithmetic: 0.72 us -> 0.02 us
    unnamed x12 -> x10, local copies, waits for them, and re-layouts: 2.51 us -> 0.02 us
    ppermute x3, waiting for transfers between devices: 0.48 us -> 1.72 us  [local(): lax.ppermute(quarter, 'pair', around('pair', k))]
    ppermute x3, starting transfers between devices: 5.59 us -> 4.45 us  [local(): lax.ppermute(quarter, 'pair', around('pair', k))]
    ppermute x3, starting transfers between devices: 3.43 us -> 2.41 us  [local(): lax.ppermute(total, 'space', around('space', k))]
    ppermute x3, waiting for transfers between devices: 0.01 us -> 0.73 us  [local(): quarter = quarter + lax.ppermute(pieces[k], 'space', around('space', k))]
    another operation x1 -> x0, other arithmetic: 0.7 us -> none  [local(): comps = jnp.stack([comp_first, comp_second, comp_win])]
    ppermute x3, waiting for transfers between devices: 0.22 us -> 0.69 us  [local(): lax.ppermute(total, 'space', around('space', k))]
  transfers between devices with their start and end apart: 13 -> 13, of which waited for: 2 -> 3; matrix products, arithmetic and copies ran while one was open for 2% -> 0% of each run, Pallas kernels for 25% -> 31%
where the time goes in v3:
time: 36.6 us; the launch traced here: 36.3 us
  starting transfers between devices  16.7 us (46%)
  Pallas kernels  15.6 us (43%)
  waiting for transfers between devices  3.15 us (9%)
  between operations  0.81 us (2%)
    pallas_call x9, Pallas kernels, call(): pl.pallas_call(kernel, out_shape=outs, in_specs=[pl.BlockSpec(memory_spac...  15.6 us
    ppermute x3, starting transfers between devices, local(): quarter = quarter + lax.ppermute(pieces[k], 'space', around('space', k))  7.48 us
    ppermute x3, starting transfers between devices, local(): lax.ppermute(quarter, 'pair', around('pair', k))  4.45 us
    ppermute x3, starting transfers between devices, local(): lax.ppermute(total, 'space', around('space', k))  2.41 us
    ppermute x3, waiting for transfers between devices, local(): lax.ppermute(quarter, 'pair', around('pair', k))  1.72 us
    ppermute x3, waiting for transfers between devices, local(): quarter = quarter + lax.ppermute(pieces[k], 'space', around('space', k))  0.73 us
  transfers between devices with their start and end apart: 13, of which 3 were waited for; matrix products, arithmetic and copies ran while one was open for 0% of the time, Pallas kernels for 31%

profile of v3, /device:TPU:0, one launch (start us, length us, event | category | flops | bytes accessed | tf_op | source)
XLA Modules:
  0.0 36.3 jit_solution(13940819218032629658)
XLA Ops:
  0.6 1.2 %shard_map.128 = (bf16[8,128,256]{2,1,0:T(8,128)(2,1)S(1)}, bf16[8,128,256]{2,1,0:T(8,128)(2,1)S(1)}) custom-call(bf16[16,128,256]{2,1,0:T(8,128)(2,1)} %bitcast.22), custom_call_target="tpu_custom_call" | custom-call | flops 10000 | bytes 1048576 | tf_op jit(solution)/shard_map/pallas_call | solution.py:505
  1.9 0.5 %collective-permute-start = (bf16[8,128,256]{2,1,0:T(8,128)(2,1)S(1)}, bf16[8,128,256]{2,1,0:T(8,128)(2,1)S(1)}, u32[]{:S(2)}, u32[]{:S(2)}) collective-permute-start(bf16[8,128,256]{2,1,0:T(8,128)(2,1)S(1)} %get-tuple-element.49), channel_id=1, source_target_pairs={{0,4},{4,0},{8,12},{12,8},{1,5},{5,1},{9,13},{13,9},{2,6},{6,2},{1... | collective-permute-start | bytes 1572872 | tf_op jit(solution)/shard_map/ppermute | solution.py:552
  2.4 0.7 %collective-permute-start.1 = (bf16[8,128,256]{2,1,0:T(8,128)(2,1)S(1)}, bf16[8,128,256]{2,1,0:T(8,128)(2,1)S(1)}, u32[]{:S(2)}, u32[]{:S(2)}) collective-permute-start(bf16[8,128,256]{2,1,0:T(8,128)(2,1)S(1)} %get-tuple-element.54), channel_id=1, source_target_pairs={{0,0},{4,8},{8,4},{12,12},{1,1},{5,9},{9,5},{13,13},{2,2},{6,10},{... | collective-permute-start | bytes 1572872 | tf_op jit(solution)/shard_map/ppermute | solution.py:553
  3.1 4.1 %shard_map.127 = (bf16[16,8,16,256]{3,2,1,0:T(8,128)(2,1)S(1)}, bf16[16,144,256]{2,1,0:T(8,128)(2,1)S(1)}, bf16[16,8,16,256]{3,2,1,0:T(8,128)(2,1)S(1)}, bf16[16...) custom-call(bf16[16,8,16,256]{3,2,1,0:T(8,128)(2,1)} %bitcast.24, ...), custom_call_target="tpu_custom_call" | custom-call | flops 2000000000 | bytes 2171136 | tf_op jit(solution)/shard_map/pallas_call | solution.py:505
  7.2 0.8 %shard_map.129 = (bf16[8,8,16,256]{3,2,1,0:T(8,128)(2,1)S(1)}, f32[8,128,128]{2,1,0:T(8,128)S(1)}) custom-call(bf16[16,8,16,256]{3,2,1,0:T(8,128)(2,1)S(1)} %get-tuple-element.47.turned_ref, bf16[8,128,256]{2,1,0:T(8,128)(2,1)S(1)} %collective-permute-done.halo_ref.across_ref, bf16[4,896,128]{2,1,0:T(8,128)(2,1)S(1)} %get-tuple-element.50.tall_ref), custom_call_target="tpu_custom_call" | custom-call | flops 1000000000 | bytes 2490368 | tf_op jit(solution)/shard_map/pallas_call | solution.py:505
  8.1 2.4 %shard_map.130 = (bf16[16,128,128]{2,1,0:T(8,128)(2,1)S(1)}, f32[88,128]{1,0:T(8,128)S(1)}, f32[88,128]{1,0:T(8,128)S(1)}, f32[88,128]{1,0:T(8,128)S(1)}, f32[88,128]{1,0:T(8,128)S(1)}) custom-call(bf16[16,8,16,256]{3,2,1,0:T(8,128)(2,1)S(1)} %get-tuple-element.47.turned_ref, bf16[16,8,16,512]{3,2,1,0:T(8,128)(2,1)S(1)} %get-tuple-element.48.corr_ref, ...), custom_call_target="tpu_custom_call" | custom-call | flops 2000000000 | bytes 6685696 | tf_op jit(solution)/shard_map/pallas_call | solution.py:505
  10.5 5.7 %collective-permute-start.2 = (f32[88,128]{1,0:T(8,128)S(1)}, f32[88,128]{1,0:T(8,128)S(1)}, u32[]{:S(2)}, u32[]{:S(2)}) collective-permute-start(f32[88,128]{1,0:T(8,128)S(1)} %get-tuple-element.56), channel_id=1, source_target_pairs={{0,4},{4,0},{8,12},{12,8},{1,5},{5,1},{9,13},{13,9},{2,6},{6,2},{1... | collective-permute-start | bytes 135176 | tf_op jit(solution)/shard_map/ppermute | solution.py:605
  16.2 1.7 %collective-permute-start.3 = (f32[88,128]{1,0:T(8,128)S(1)}, f32[88,128]{1,0:T(8,128)S(1)}, u32[]{:S(2)}, u32[]{:S(2)}) collective-permute-start(f32[88,128]{1,0:T(8,128)S(1)} %get-tuple-element.57), channel_id=1, source_target_pairs={{0,8},{4,12},{8,0},{12,4},{1,9},{5,13},{9,1},{13,5},{2,10},{6,14},... | collective-permute-start | bytes 135176 | tf_op jit(solution)/shard_map/ppermute | solution.py:605
  17.9 0.1 collective-permute-start.4
  18.0 1.6 %shard_map.133 = (bf16[8,128,256]{2,1,0:T(8,128)(2,1)S(1)}, bf16[8,128,256]{2,1,0:T(8,128)(2,1)S(1)}) custom-call(bf16[16,128,128]{2,1,0:T(8,128)(2,1)S(1)} %get-tuple-element.59.gate_ref, bf16[4,128,640]{2,1,0:T(8,128)(2,1)S(1)} %get-tuple-element.60.wide_ref, bf16[16,8,16,256]{3,2,1,0:T(8,128)(2,1)S(1)} %get-tuple-element.61.source_ref), custom_call_target="tpu_custom_call" | custom-call | flops 1000000000 | bytes 2228224 | tf_op jit(solution)/shard_map/pallas_call | solution.py:505
  19.7 0.4 %collective-permute-start.11 = (bf16[8,128,256]{2,1,0:T(8,128)(2,1)S(1)}, bf16[8,128,256]{2,1,0:T(8,128)(2,1)S(1)}, u32[]{:S(2)}, u32[]{:S(2)}) collective-permute-start(bf16[8,128,256]{2,1,0:T(8,128)(2,1)S(1)} %get-tuple-element.73), channel_id=1, source_target_pairs={{0,4},{4,0},{8,12},{12,8},{1,5},{5,1},{9,13},{13,9},{2,6},{6,2},{1... | collective-permute-start | bytes 1572872 | tf_op jit(solution)/shard_map/ppermute | solution.py:619
  20.1 0.7 %collective-permute-start.12 = (bf16[8,128,256]{2,1,0:T(8,128)(2,1)S(1)}, bf16[8,128,256]{2,1,0:T(8,128)(2,1)S(1)}, u32[]{:S(2)}, u32[]{:S(2)}) collective-permute-start(bf16[8,128,256]{2,1,0:T(8,128)(2,1)S(1)} %get-tuple-element.74), channel_id=1, source_target_pairs={{0,0},{4,8},{8,4},{12,12},{1,1},{5,9},{9,5},{13,13},{2,2},{6,10},{... | collective-permute-start | bytes 1572872 | tf_op jit(solution)/shard_map/ppermute | solution.py:620
  20.8 0.7 %collective-permute-done.4 = f32[88,128]{1,0:T(8,128)S(1)} collective-permute-done((f32[88,128]{1,0:T(8,128)S(1)}, f32[88,128]{1,0:T(8,128)S(1)}, u32[]{:S(2)}, u32[]{:S(2)}) %collective-permute-start.4) | collective-permute-done | bytes 45088 | tf_op jit(solution)/shard_map/ppermute | solution.py:605
  21.6 3.7 %collective-permute-start.7 = (f32[88,128]{1,0:T(8,128)S(1)}, f32[88,128]{1,0:T(8,128)S(1)}, u32[]{:S(2)}, u32[]{:S(2)}) collective-permute-start(f32[88,128]{1,0:T(8,128)S(1)} %add_add_fusion.rest_0_), channel_id=1, source_target_pairs={{0,3},{1,2},{2,1},{3,0},{4,7},{5,6},{6,5},{7,4},{8,11},{9,10},{10,... | collective-permute-start | bytes 135176 | tf_op jit(solution)/shard_map/ppermute | solution.py:637
  25.2 0.8 %collective-permute-start.5 = (f32[88,128]{1,0:T(8,128)S(1)}, f32[88,128]{1,0:T(8,128)S(1)}, u32[]{:S(2)}, u32[]{:S(2)}) collective-permute-start(f32[88,128]{1,0:T(8,128)S(1)} %add_add_fusion.rest_0_), channel_id=1, source_target_pairs={{0,1},{1,0},{2,3},{3,2},{4,5},{5,4},{6,7},{7,6},{8,9},{9,8},{10,11... | collective-permute-start | bytes 135176 | tf_op jit(solution)/shard_map/ppermute | solution.py:637
  26.0 2.9 %shard_map.131 = (f32[16,8,16,256]{3,2,1,0:T(8,128)S(1)}, f32[16,128,256]{2,1,0:T(8,128)S(1)}) custom-call(bf16[16,128,128]{2,1,0:T(8,128)(2,1)S(1)} %get-tuple-element.59.gate_ref, bf16[4,128,640]{2,1,0:T(8,128)(2,1)S(1)} %get-tuple-element.60.wide_ref, bf16[16,8,16,256]{3,2,1,0:T(8,128)(2,1)S(1)} %get-tuple-element.61.source_ref, ...), custom_call_target="tpu_custom_call" | custom-call | flops 4000000000 | bytes 4456448 | tf_op jit(solution)/shard_map/pallas_call | solution.py:505
  29.0 1.7 %collective-permute-done.6.rest_2_ = f32[88,128]{1,0:T(8,128)S(1)} collective-permute-done((f32[88,128]{1,0:T(8,128)S(1)}, f32[88,128]{1,0:T(8,128)S(1)}, u32[]{:S(2)}, u32[]{:S(2)}) %collective-permute-start.6) | collective-permute-done | bytes 45088 | tf_op jit(solution)/shard_map/ppermute | solution.py:637
  30.7 0.2 shard_map.132
  30.9 0.1 collective-permute-start.10
  31.0 2.3 %collective-permute-start.9 = (f32[80,128]{1,0:T(8,128)S(1)}, f32[80,128]{1,0:T(8,128)S(1)}, u32[]{:S(2)}, u32[]{:S(2)}) collective-permute-start(f32[80,128]{1,0:T(8,128)S(1)} %get-tuple-element.79.rest_0_), channel_id=1, source_target_pairs={{0,8},{4,12},{8,0},{12,4},{1,9},{5,13},{9,1},{13,5},{2,10},{6,14},... | collective-permute-start | bytes 122888 | tf_op jit(solution)/shard_map/ppermute | solution.py:649
  33.3 0.0 collective-permute-start.8
  33.3 1.6 %shard_map.134 = (bf16[16,128,256]{2,1,0:T(8,128)(2,1)}, bf16[16,128,256]{2,1,0:T(8,128)(2,1)}) custom-call(f32[8,128]{1,0:T(8,128)S(1)} %get-tuple-element.70.grad_ref, f32[16,128,256]{2,1,0:T(8,128)S(1)} %bitcast.16, f32[16,128,256]{2,1,0:T(8,128)S(1)} %get-tuple-element.72.edit_ref, bf16[8,128,256]{2,1,0:T(8,128)(2,1)S(1)} %collective-permute-done.11.across_ref, ...), custom_call_target="tpu_custom_call" | custom-call | flops 10000000 | bytes 5246976 | tf_op jit(solution)/shard_map/pallas_call | solution.py:505
  34.9 0.7 %collective-permute-done.9.rest_2_ = f32[80,128]{1,0:T(8,128)S(1)} collective-permute-done((f32[80,128]{1,0:T(8,128)S(1)}, f32[80,128]{1,0:T(8,128)S(1)}, u32[]{:S(2)}, u32[]{:S(2)}) %collective-permute-start.9) | collective-permute-done | bytes 40992 | tf_op jit(solution)/shard_map/ppermute | solution.py:649
  35.6 0.7 %shard_map.135 = (f32[289,128]{1,0:T(8,128)}, f32[1,128]{1,0:T(1,128)}, f32[1,128]{1,0:T(1,128)}, f32[1,128]{1,0:T(1,128)}) custom-call(f32[80,128]{1,0:T(8,128)S(1)} %get-tuple-element.79.rest_0_, f32[80,128]{1,0:T(8,128)S(1)} %collective-permute-done.8.rest_1_, f32[80,128]{1,0:T(8,128)S(1)} %collective-permute-done.9.rest_2_, ...), custom_call_target="tpu_custom_call" | custom-call | flops 1000000 | bytes 164352 | tf_op jit(solution)/shard_map/pallas_call | solution.py:505
  (22 shorter events, 0.1 us)
Async XLA Ops:
  1.9 5.4 %collective-permute-start = (bf16[8,128,256]{2,1,0:T(8,128)(2,1)S(1)}, bf16[8,128,256]{2,1,0:T(8,128)(2,1)S(1)}, u32[]{:S(2)}, u32[]{:S(2)}) collective-permute-start(bf16[8,128,256]{2,1,0:T(8,128)(2,1)S(1)} %get-tuple-element.49), channel_id=1, source_target_pairs={{0,4},{4,0},{8,12},{12,8},{1,5},{5,1},{9,13},{13,9},{2,6},{6,2},{1... | collective-permute-start | bytes 1572872 | tf_op jit(solution)/shard_map/ppermute | solution.py:552
  2.4 5.7 %collective-permute-start.1 = (bf16[8,128,256]{2,1,0:T(8,128)(2,1)S(1)}, bf16[8,128,256]{2,1,0:T(8,128)(2,1)S(1)}, u32[]{:S(2)}, u32[]{:S(2)}) collective-permute-start(bf16[8,128,256]{2,1,0:T(8,128)(2,1)S(1)} %get-tuple-element.54), channel_id=1, source_target_pairs={{0,0},{4,8},{8,4},{12,12},{1,1},{5,9},{9,5},{13,13},{2,2},{6,10},{... | collective-permute-start | bytes 1572872 | tf_op jit(solution)/shard_map/ppermute | solution.py:553
  7.2 0.9 %copy-start.3 = (f32[128]{0:T(128)S(1)}, f32[128]{0:T(128)}, u32[]{:S(2)}) copy-start(f32[128]{0:T(128)} %param.11) | copy-start | bytes 1540
  7.2 0.9 %copy-start.4 = (f32[128]{0:T(128)S(1)}, f32[128]{0:T(128)}, u32[]{:S(2)}) copy-start(f32[128]{0:T(128)} %param.12) | copy-start | bytes 1540
  10.5 10.3 %collective-permute-start.2 = (f32[88,128]{1,0:T(8,128)S(1)}, f32[88,128]{1,0:T(8,128)S(1)}, u32[]{:S(2)}, u32[]{:S(2)}) collective-permute-start(f32[88,128]{1,0:T(8,128)S(1)} %get-tuple-element.56), channel_id=1, source_target_pairs={{0,4},{4,0},{8,12},{12,8},{1,5},{5,1},{9,13},{13,9},{2,6},{6,2},{1... | collective-permute-start | bytes 135176 | tf_op jit(solution)/shard_map/ppermute | solution.py:605
  16.2 4.6 %collective-permute-start.3 = (f32[88,128]{1,0:T(8,128)S(1)}, f32[88,128]{1,0:T(8,128)S(1)}, u32[]{:S(2)}, u32[]{:S(2)}) collective-permute-start(f32[88,128]{1,0:T(8,128)S(1)} %get-tuple-element.57), channel_id=1, source_target_pairs={{0,8},{4,12},{8,0},{12,4},{1,9},{5,13},{9,1},{13,5},{2,10},{6,14},... | collective-permute-start | bytes 135176 | tf_op jit(solution)/shard_map/ppermute | solution.py:605
  17.9 3.6 %collective-permute-start.4 = (f32[88,128]{1,0:T(8,128)S(1)}, f32[88,128]{1,0:T(8,128)S(1)}, u32[]{:S(2)}, u32[]{:S(2)}) collective-permute-start(f32[88,128]{1,0:T(8,128)S(1)} %get-tuple-element.58), channel_id=1, source_target_pairs={{0,12},{4,8},{8,4},{12,0},{1,13},{5,9},{9,5},{13,1},{2,14},{6,10},... | collective-permute-start | bytes 135176 | tf_op jit(solution)/shard_map/ppermute | solution.py:605
  19.7 13.6 %collective-permute-start.11 = (bf16[8,128,256]{2,1,0:T(8,128)(2,1)S(1)}, bf16[8,128,256]{2,1,0:T(8,128)(2,1)S(1)}, u32[]{:S(2)}, u32[]{:S(2)}) collective-permute-start(bf16[8,128,256]{2,1,0:T(8,128)(2,1)S(1)} %get-tuple-element.73), channel_id=1, source_target_pairs={{0,4},{4,0},{8,12},{12,8},{1,5},{5,1},{9,13},{13,9},{2,6},{6,2},{1... | collective-permute-start | bytes 1572872 | tf_op jit(solution)/shard_map/ppermute | solution.py:619
  20.1 13.2 %collective-permute-start.12 = (bf16[8,128,256]{2,1,0:T(8,128)(2,1)S(1)}, bf16[8,128,256]{2,1,0:T(8,128)(2,1)S(1)}, u32[]{:S(2)}, u32[]{:S(2)}) collective-permute-start(bf16[8,128,256]{2,1,0:T(8,128)(2,1)S(1)} %get-tuple-element.74), channel_id=1, source_target_pairs={{0,0},{4,8},{8,4},{12,12},{1,1},{5,9},{9,5},{13,13},{2,2},{6,10},{... | collective-permute-start | bytes 1572872 | tf_op jit(solution)/shard_map/ppermute | solution.py:620
  21.6 7.4 %collective-permute-start.7 = (f32[88,128]{1,0:T(8,128)S(1)}, f32[88,128]{1,0:T(8,128)S(1)}, u32[]{:S(2)}, u32[]{:S(2)}) collective-permute-start(f32[88,128]{1,0:T(8,128)S(1)} %add_add_fusion.rest_0_), channel_id=1, source_target_pairs={{0,3},{1,2},{2,1},{3,0},{4,7},{5,6},{6,5},{7,4},{8,11},{9,10},{10,... | collective-permute-start | bytes 135176 | tf_op jit(solution)/shard_map/ppermute | solution.py:637
  25.2 5.4 %collective-permute-start.6 = (f32[88,128]{1,0:T(8,128)S(1)}, f32[88,128]{1,0:T(8,128)S(1)}, u32[]{:S(2)}, u32[]{:S(2)}) collective-permute-start(f32[88,128]{1,0:T(8,128)S(1)} %add_add_fusion.rest_0_), channel_id=1, source_target_pairs={{0,2},{1,3},{2,0},{3,1},{4,6},{5,7},{6,4},{7,5},{8,10},{9,11},{10,... | collective-permute-start | bytes 135176 | tf_op jit(solution)/shard_map/ppermute | solution.py:637
  25.2 5.4 %collective-permute-start.5 = (f32[88,128]{1,0:T(8,128)S(1)}, f32[88,128]{1,0:T(8,128)S(1)}, u32[]{:S(2)}, u32[]{:S(2)}) collective-permute-start(f32[88,128]{1,0:T(8,128)S(1)} %add_add_fusion.rest_0_), channel_id=1, source_target_pairs={{0,1},{1,0},{2,3},{3,2},{4,5},{5,4},{6,7},{7,6},{8,9},{9,8},{10,11... | collective-permute-start | bytes 135176 | tf_op jit(solution)/shard_map/ppermute | solution.py:637
  26.0 4.7 %copy-start = (s32[16]{0:T(128)S(1)}, s32[16]{0:T(128)}, u32[]{:S(2)}) copy-start(s32[16]{0:T(128)} %param.13) | copy-start | bytes 196
  26.0 4.7 %copy-start.1 = (s32[16]{0:T(128)S(1)}, s32[16]{0:T(128)}, u32[]{:S(2)}) copy-start(s32[16]{0:T(128)} %param.14) | copy-start | bytes 196
  26.0 4.7 %copy-start.2 = (s32[16]{0:T(128)S(1)}, s32[16]{0:T(128)}, u32[]{:S(2)}) copy-start(s32[16]{0:T(128)} %param.15) | copy-start | bytes 196
  30.9 4.0 %collective-permute-start.10 = (f32[80,128]{1,0:T(8,128)S(1)}, f32[80,128]{1,0:T(8,128)S(1)}, u32[]{:S(2)}, u32[]{:S(2)}) collective-permute-start(f32[80,128]{1,0:T(8,128)S(1)} %get-tuple-element.79.rest_0_), channel_id=1, source_target_pairs={{0,12},{4,8},{8,4},{12,0},{1,13},{5,9},{9,5},{13,1},{2,14},{6,10},... | collective-permute-start | bytes 122888 | tf_op jit(solution)/shard_map/ppermute | solution.py:649
  31.0 4.6 %collective-permute-start.9 = (f32[80,128]{1,0:T(8,128)S(1)}, f32[80,128]{1,0:T(8,128)S(1)}, u32[]{:S(2)}, u32[]{:S(2)}) collective-permute-start(f32[80,128]{1,0:T(8,128)S(1)} %get-tuple-element.79.rest_0_), channel_id=1, source_target_pairs={{0,8},{4,12},{8,0},{12,4},{1,9},{5,13},{9,1},{13,5},{2,10},{6,14},... | collective-permute-start | bytes 122888 | tf_op jit(solution)/shard_map/ppermute | solution.py:649
  33.3 2.3 %collective-permute-start.8 = (f32[80,128]{1,0:T(8,128)S(1)}, f32[80,128]{1,0:T(8,128)S(1)}, u32[]{:S(2)}, u32[]{:S(2)}) collective-permute-start(f32[80,128]{1,0:T(8,128)S(1)} %get-tuple-element.79.rest_0_), channel_id=1, source_target_pairs={{0,4},{4,0},{8,12},{12,8},{1,5},{5,1},{9,13},{13,9},{2,6},{6,2},{1... | collective-permute-start | bytes 122888 | tf_op jit(solution)/shard_map/ppermute | solution.py:649

commit v4 on v3

--- a/solution.py
+++ b/solution.py
@@ -253,9 +253,8 @@
     head_ref,
     *rest,
 ):
-    gate_ref = rest[0]
-    piece_refs = rest[1 : 1 + parts]
-    pad, rims, extra, stage = rest[1 + parts :]
+    *out_refs, pad, rims, extra, stage = rest
+    gate_ref, *piece_refs = out_refs
     rows, groups = turned_ref.shape[:2]
     above, _ = edge_spot(parts, 1)
     rims[1 - above] = rim_ref[...]
@@ -304,10 +303,25 @@
     stage[STAT + 1 : STAT + 2] = hidden * scale
     score = jnp.sum(hidden * head, axis=1, keepdims=True) * scale
     me = lax.axis_index("space")
-    for k in range(parts):
-        start = pl.multiple_of(partner(me, k, parts) * share, 8)
-        piece_refs[k][:share] = stage[pl.ds(start, share), :]
-        piece_refs[k][share:] = jnp.broadcast_to(score, (8, kout))
+    for side, ref in enumerate(piece_refs):
+        for i in range(ref.shape[0]):
+            piece = i if parts == 1 else 2 * i + (lax.rem(me, 2) ^ side)
+            start = pl.multiple_of(piece * share, 8)
+            ref[i, :share] = stage[pl.ds(start, share), :]
+            ref[i, share:] = jnp.broadcast_to(score, (8, kout))
+
+
+def split_kernel(bit, keep_ref, came_ref, next_keep, next_send):
+    mine = lax.rem(lax.axis_index("space") // bit, 2)
+    for i in range(next_keep.shape[0]):
+        for ref, at in ((next_keep, 2 * i + mine), (next_send, 2 * i + 1 - mine)):
+            ref[i] = keep_ref[at] + came_ref[at]
+
+
+def stack_kernel(first_ref, second_ref, out_ref):
+    count = first_ref.shape[0]
+    out_ref[:count] = first_ref[...]
+    out_ref[count:] = second_ref[...]
 
 
 def back_chunks(gate_ref, wide_ref, r, rows, groups):
@@ -362,27 +376,9 @@
     beyond_ref[...] = sums[pl.ds(low, 8), RADIUS : RADIUS + cols].astype(BF16)
 
 
-def back_kernel(
-    parts,
-    gate_ref,
-    wide_ref,
-    source_ref,
-    own_pad,
-    across_ref,
-    beyond_ref,
-    source_out,
-    edit_out,
-    pad,
-    band,
-    sums,
-):
+def edit_kernel(gate_ref, wide_ref, source_ref, band, edit_out, sums):
     rows, groups, _, chan = source_ref.shape
-    half = rows // 2
     quarter = rows // PER
-    for kind, ref in ((0, across_ref), (1, beyond_ref)):
-        above, inside = edge_spot(parts, kind)
-        fill_halo(pad, 8 * above, ref, inside)
-    fill_columns(pad, 0, 16, groups * GROUP)
     zero = jnp.zeros((PER, groups, GROUP, LANES), BF16)
     for q, c in ((1, 0), (3, 2), (0, 5), (2, 7)):
         band[q * PER : (q + 1) * PER, :, :, c * LANES : (c + 1) * LANES] = zero
@@ -392,8 +388,7 @@
                 at = (q + pos) * LANES
                 band[q * PER + r, :, :, at : at + LANES] = part[q]
     sums[...] = jnp.zeros(sums.shape, F32)
-
-    def body(g, carry):
+    for g in range(groups):
         start = g * GROUP
         near = source_ref[:, g].reshape(rows * GROUP, chan)
         for s in range(rows // 8):
@@ -401,6 +396,17 @@
             lhs = band[:, g, :, at : at + 2 * LANES].reshape(rows * GROUP, 2 * LANES)
             grad = tn(lhs, near).reshape(8, WIN, chan)
             sums[8 * s : 8 * s + 8, start : start + WIN, :] += grad
+    edit_out[...] = sums[:, RADIUS : RADIUS + groups * GROUP]
+
+
+def source_kernel(parts, band, own_pad, across_ref, beyond_ref, source_out, pad):
+    rows, groups, _, chan = source_out.shape
+    half = rows // 2
+    for kind, ref in ((0, across_ref), (1, beyond_ref)):
+        above, inside = edge_spot(parts, kind)
+        fill_halo(pad, 8 * above, ref, inside)
+    fill_columns(pad, 0, 16, groups * GROUP)
+    for g in range(groups):
         for i in range(2):
             at = i * 2 * LANES
             lhs = band[i * half : (i + 1) * half, g, :, at : at + 6 * LANES]
@@ -408,55 +414,46 @@
             rhs = jnp.concatenate(spots[::-1] if i else spots, axis=0)
             grad = nn(lhs.reshape(half * GROUP, 6 * LANES), rhs)
             source_out[i * half : (i + 1) * half, g] = grad.reshape(half, GROUP, chan)
-        return carry
-
-    for g in range(groups):
-        body(g, 0)
-    cols = groups * GROUP
-    edit_out[...] = sums[:, RADIUS : RADIUS + cols]
-
-
-def partner(me, step, count):
-    if count & (count - 1):
-        return (me + step + count) % count
-    return me ^ abs(step)
+
+
+def pieces_of(refs):
+    return [ref.at[i] for ref in refs for i in range(ref.shape[0])]
 
 
 def judge_kernel(pairs, first_ref, second_ref, win_ref, *rest):
-    piece_refs = rest[:pairs]
-    total_ref, grad_ref, loss_ref = rest[pairs:]
-    share = total_ref.shape[0]
+    *came_refs, total_ref, grad_ref, loss_ref = rest
+    share = total_ref.shape[1]
     me = lax.axis_index("pair")
     first, second, win = first_ref[...], second_ref[...], win_ref[...]
     hots, margin = [], jnp.zeros(first.shape, F32)
+    pieces = pieces_of(came_refs)
     for k in range(pairs):
-        pid = partner(me, -k, pairs)
+        pid = me ^ k
         hot = (first == pid).astype(F32) - (second == pid).astype(F32)
-        score = piece_refs[k][share : share + 1, 0:1]
+        score = pieces[k][share : share + 1, 0:1]
         margin = margin + hot * score
         hots.append(hot)
     sign = 2.0 * win.astype(F32) - 1.0
     loss = jnp.mean(jax.nn.softplus(-sign * margin), axis=1, keepdims=True)
     loss_ref[...] = jnp.broadcast_to(loss, loss_ref.shape)
     margin_grad = -sign * jax.nn.sigmoid(-sign * margin)
-    total = jnp.zeros(total_ref.shape, F32)
+    total = jnp.zeros(total_ref.shape[1:], F32)
     for k in range(pairs):
         grad = jnp.sum(margin_grad * hots[k], axis=1, keepdims=True)
         if k == 0:
             grad_ref[...] = jnp.broadcast_to(grad, grad_ref.shape)
-        total = total + grad * piece_refs[k][:share]
-    total_ref[...] = total
-
-
-def gather_kernel(parts, *rest):
-    piece_refs = rest[:parts]
-    loss_ref, conv_ref, bias_ref, head_ref, loss_out, stage = rest[parts:]
+        total = total + grad * pieces[k][:share]
+    total_ref[0] = total
+
+
+def gather_kernel(order, *rest):
+    *came_refs, loss_ref, conv_ref, bias_ref, head_ref, loss_out, stage = rest
     loss_out[...] = loss_ref[...]
-    share = piece_refs[0].shape[0]
     me = lax.axis_index("space")
-    for k in range(parts):
-        start = pl.multiple_of(partner(me, -k, parts) * share, 8)
-        stage[pl.ds(start, share), :] = piece_refs[k][...]
+    for flip, piece in zip(order, pieces_of(came_refs), strict=True):
+        share = piece.shape[0]
+        start = pl.multiple_of((me ^ flip) * share, 8)
+        stage[pl.ds(start, share), :] = piece[...]
     conv_ref[...] = stage[: conv_ref.shape[0]]
     bias_ref[...] = stage[STAT : STAT + 1]
     head_ref[...] = stage[STAT + 1 : STAT + 2]
@@ -521,9 +518,37 @@
     return pltpu.VMEM(dims, dtype)
 
 
-def around(axis, step):
-    count = lax.axis_size(axis)
-    return [(i, partner(i, step, count)) for i in range(count)]
+def place_bits(count):
+    bits = [1 << i for i in range(count.bit_length() - 1)]
+    assert count == 1 << len(bits)
+    return bits
+
+
+def swap(array, axis, bit):
+    return lax.ppermute(array, axis, [(i, i ^ bit) for i in range(lax.axis_size(axis))])
+
+
+def together(came, others):
+    came, *others = lax.optimization_barrier((came, *others))
+    return came, others
+
+
+def collect(array, axis, bits, covers):
+    order, done = [0], []
+    stacks = [array]
+    for i, bit in enumerate(bits):
+        came = swap(array, axis, bit)
+        cover = covers[i]() if i < len(covers) else ()
+        came, cover = together(came, cover)
+        done += cover
+        order += [o ^ bit for o in order]
+        stacks = [array, came]
+        if i < len(bits) - 1:
+            dims = (2 * array.shape[0], *array.shape[1:])
+            (array,) = call(stack_kernel, (shape(dims),), [], 10**4, array, came)
+    for cover in covers[len(bits) :]:
+        done += cover()
+    return stacks, order, done
 
 
 def local(
@@ -534,6 +559,7 @@
     inv_root = chan ** (-0.5)
     space, pairs = lax.axis_size("space"), lax.axis_size("pair")
     pixels = rows * space * columns
+    space_bits, pair_bits = place_bits(space), place_bits(pairs)
     groups = columns // GROUP
     wide_cols = columns + 2 * RADIUS
     share = -(-(disp + 2) // (8 * space)) * 8
@@ -580,9 +606,13 @@
         across,
         tall,
     )
+    half_pieces = max(space // 2, 1)
     gate, *pieces = call(
         functools.partial(outer_kernel, inv_root, pixels, space),
-        (shape((rows, columns, kout), BF16),) + (shape((share + 8, kout)),) * space,
+        (
+            shape((rows, columns, kout), BF16),
+            *(shape((half_pieces, share + 8, kout)),) * min(space, 2),
+        ),
         [
             pltpu.VMEM((RADIUS, wide_cols, chan), BF16),
             pltpu.VMEM((2,) + rim_shape, BF16),
@@ -600,15 +630,13 @@
         conv_bias[None],
         head_weight[None],
     )
-    quarter = pieces[0]
-    for k in range(1, space):
-        quarter = quarter + lax.ppermute(pieces[k], "space", around("space", k))
-    rim_across, rim_beyond = call(
+    came = [swap(pieces[1], "space", 1)] if space > 1 else []
+    rims = call(
         rim_kernel,
         (shape((RADIUS, columns, chan), BF16),) * 2,
         [
-            pltpu.VMEM((rows // 2, groups, GROUP, 8 * WIN), BF16),
-            pltpu.VMEM((rows // 2, groups, GROUP, 8 * WIN), BF16),
+            pltpu.VMEM(rim_shape, BF16),
+            pltpu.VMEM(rim_shape, BF16),
             pltpu.VMEM((2 * RADIUS, wide_cols, chan), F32),
         ],
         10**9,
@@ -616,60 +644,91 @@
         wide,
         held,
     )
+    *came, rim_across, rim_beyond = lax.optimization_barrier((*came, *rims))
+    from_beyond = lax.ppermute(rim_beyond, "space", to_beyond)
     from_across = lax.ppermute(rim_across, "space", to_across)
-    from_beyond = lax.ppermute(rim_beyond, "space", to_beyond)
-    source_sum, edit_sum = call(
-        functools.partial(back_kernel, space),
-        (shape((rows, groups, GROUP, chan)), shape((rows, columns, chan))),
-        [
-            pltpu.VMEM((2 * RADIUS, wide_cols, chan), BF16),
-            pltpu.VMEM((rows, groups, GROUP, (rows + 2 * RADIUS) * WIN), BF16),
-            pltpu.VMEM((rows, wide_cols, chan), F32),
-        ],
-        4 * 10**9,
-        gate,
-        wide,
-        held,
-        own_pad,
-        across,
-        beyond,
-    )
-    others = [quarter] + [lax.ppermute(quarter, "pair", around("pair", k)) for k in range(1, pairs)]
-    *others, source_sum, edit_sum = lax.optimization_barrier((*others, source_sum, edit_sum))
+    keep = pieces[0]
+    for bit in space_bits[1:]:
+        dims = (keep.shape[0] // 2, *keep.shape[1:])
+        keep, send = call(
+            functools.partial(split_kernel, bit), (shape(dims),) * 2, [], 10**4, keep, *came
+        )
+        came = [swap(send, "space", bit)]
+    quarter = keep + came[0] if came else keep
+
+    def edit_cover():
+        return call(
+            edit_kernel,
+            (
+                shape((rows, groups, GROUP, (rows + 2 * RADIUS) * WIN), BF16),
+                shape((rows, columns, chan)),
+            ),
+            [pltpu.VMEM((rows, wide_cols, chan), F32)],
+            2 * 10**9,
+            gate,
+            wide,
+            held,
+        )
+
+    edited = []
+
+    def edit_first():
+        edited.extend(edit_cover())
+        return edited
+
+    def source_cover():
+        return call(
+            functools.partial(source_kernel, space),
+            (shape(near),),
+            [pltpu.VMEM((2 * RADIUS, wide_cols, chan), BF16)],
+            2 * 10**9,
+            edited[0],
+            own_pad,
+            across,
+            beyond,
+        )
+
+    stacks, _, (_, edit_sum, source_sum) = collect(
+        quarter, "pair", pair_bits, (edit_first, source_cover)
+    )
     total, score_grad, loss = call(
         functools.partial(judge_kernel, pairs),
-        (shape((share, kout)), shape((8, LANES)), shape((1, LANES))),
+        (shape((1, share, kout)), shape((8, LANES)), shape((1, LANES))),
         [],
         10**6,
         comp_first[None],
         comp_second[None],
         comp_win[None],
-        *others,
-    )
-    gathered = [total] + [lax.ppermute(total, "space", around("space", k)) for k in range(1, space)]
-    source_grad, edit_grad = call(
-        functools.partial(finish_kernel, inv_root, space),
-        (result((rows, columns, chan), BF16),) * 2,
-        [
-            pltpu.VMEM((rows, columns, chan), BF16),
-            pltpu.VMEM((rows, columns, chan), BF16),
-            pltpu.SemaphoreType.DMA((8,)),
-        ],
-        10**7,
-        score_grad,
-        source_sum.reshape(rows, columns, chan),
-        edit_sum,
-        from_across,
-        from_beyond,
-        far_out=True,
-    )
-    *gathered, source_grad, edit_grad = lax.optimization_barrier((*gathered, source_grad, edit_grad))
+        *stacks,
+    )
+
+    def finish_cover():
+        return call(
+            functools.partial(finish_kernel, inv_root, space),
+            (result((rows, columns, chan), BF16),) * 2,
+            [
+                pltpu.VMEM((rows, columns, chan), BF16),
+                pltpu.VMEM((rows, columns, chan), BF16),
+                pltpu.SemaphoreType.DMA((8,)),
+            ],
+            10**7,
+            score_grad,
+            source_sum.reshape(rows, columns, chan),
+            edit_sum,
+            from_across,
+            from_beyond,
+            far_out=True,
+        )
+
+    stacks, order, (source_grad, edit_grad) = collect(
+        total, "space", space_bits[::-1], (finish_cover,)
+    )
     conv_grad, bias_grad, head_grad, loss = call(
-        functools.partial(gather_kernel, space),
+        functools.partial(gather_kernel, order),
         (result((disp, kout)), result((1, kout)), result((1, kout)), result((1, LANES))),
         [pltpu.VMEM((share * space, kout), F32)],
         10**6,
-        *gathered,
+        *stacks,
         loss,
     )
     return (

time: 36.6 us -> 46.6 us (1.27)
  waiting for transfers between devices: 3.15 us -> 11.1 us
  starting transfers between devices: 16.7 us -> 18.7 us
    ppermute x9 -> x6, waiting for transfers between devices: 3.14 us -> 11.1 us  [swap(): lax.ppermute(array, axis, [(i, i ^ bit) for i in range(lax.axis_size(axis...]
    ppermute x9 -> x6, starting transfers between devices: 14.3 us -> 16.7 us  [swap(): lax.ppermute(array, axis, [(i, i ^ bit) for i in range(lax.axis_size(axis...]
    pallas_call x9 -> x13, Pallas kernels: 15.6 us -> 15.8 us  [call(): pl.pallas_call(kernel, out_shape=outs, in_specs=[pl.BlockSpec(memory_spac...]
  transfers between devices with their start and end apart: 13 -> 10, of which waited for: 3 -> 4; matrix products, arithmetic and copies ran while one was open for 0% -> 0% of each run, Pallas kernels for 31% -> 25%
where the time goes in v4:
time: 46.6 us; the launch traced here: 46.4 us
  starting transfers between devices  18.7 us (40%)
  Pallas kernels  15.8 us (34%)
  waiting for transfers between devices  11.1 us (24%)
  between operations  0.8 us (2%)
    ppermute x6, starting transfers between devices, swap(): lax.ppermute(array, axis, [(i, i ^ bit) for i in range(lax.axis_size(axis...  16.7 us
    pallas_call x13, Pallas kernels, call(): pl.pallas_call(kernel, out_shape=outs, in_specs=[pl.BlockSpec(memory_spac...  15.8 us
    ppermute x6, waiting for transfers between devices, swap(): lax.ppermute(array, axis, [(i, i ^ bit) for i in range(lax.axis_size(axis...  11.1 us
  transfers between devices with their start and end apart: 10, of which 4 were waited for; matrix products, arithmetic and copies ran while one was open for 0% of the time, Pallas kernels for 25%

profile of v4, /device:TPU:0, one launch (start us, length us, event | category | flops | bytes accessed | tf_op | source)
XLA Modules:
  0.0 46.4 jit_solution(17823617657373629888)
XLA Ops:
  0.6 1.2 %shard_map.128 = (bf16[8,128,256]{2,1,0:T(8,128)(2,1)S(1)}, bf16[8,128,256]{2,1,0:T(8,128)(2,1)S(1)}) custom-call(bf16[16,128,256]{2,1,0:T(8,128)(2,1)} %bitcast.22), custom_call_target="tpu_custom_call" | custom-call | flops 10000 | bytes 1048576 | tf_op jit(solution)/shard_map/pallas_call | solution.py:502
  1.9 0.5 %collective-permute-start = (bf16[8,128,256]{2,1,0:T(8,128)(2,1)S(1)}, bf16[8,128,256]{2,1,0:T(8,128)(2,1)S(1)}, u32[]{:S(2)}, u32[]{:S(2)}) collective-permute-start(bf16[8,128,256]{2,1,0:T(8,128)(2,1)S(1)} %get-tuple-element.47), channel_id=1, source_target_pairs={{0,4},{4,0},{8,12},{12,8},{1,5},{5,1},{9,13},{13,9},{2,6},{6,2},{1... | collective-permute-start | bytes 1572872 | tf_op jit(solution)/shard_map/ppermute | solution.py:578
  2.4 0.7 %collective-permute-start.1 = (bf16[8,128,256]{2,1,0:T(8,128)(2,1)S(1)}, bf16[8,128,256]{2,1,0:T(8,128)(2,1)S(1)}, u32[]{:S(2)}, u32[]{:S(2)}) collective-permute-start(bf16[8,128,256]{2,1,0:T(8,128)(2,1)S(1)} %get-tuple-element.52), channel_id=1, source_target_pairs={{0,0},{4,8},{8,4},{12,12},{1,1},{5,9},{9,5},{13,13},{2,2},{6,10},{... | collective-permute-start | bytes 1572872 | tf_op jit(solution)/shard_map/ppermute | solution.py:579
  3.1 4.1 %shard_map.127 = (bf16[16,8,16,256]{3,2,1,0:T(8,128)(2,1)S(1)}, bf16[16,144,256]{2,1,0:T(8,128)(2,1)S(1)}, bf16[16,8,16,256]{3,2,1,0:T(8,128)(2,1)S(1)}, bf16[16...) custom-call(bf16[16,8,16,256]{3,2,1,0:T(8,128)(2,1)} %bitcast.24, ...), custom_call_target="tpu_custom_call" | custom-call | flops 2000000000 | bytes 2171136 | tf_op jit(solution)/shard_map/pallas_call | solution.py:502
  7.2 0.0 copy-start.3
  7.2 0.8 %shard_map.129 = (bf16[8,8,16,256]{3,2,1,0:T(8,128)(2,1)S(1)}, f32[8,128,128]{2,1,0:T(8,128)S(1)}) custom-call(bf16[16,8,16,256]{3,2,1,0:T(8,128)(2,1)S(1)} %get-tuple-element.45.turned_ref, bf16[8,128,256]{2,1,0:T(8,128)(2,1)S(1)} %collective-permute-done.halo_ref.across_ref, bf16[4,896,128]{2,1,0:T(8,128)(2,1)S(1)} %get-tuple-element.48.tall_ref), custom_call_target="tpu_custom_call" | custom-call | flops 1000000000 | bytes 2490368 | tf_op jit(solution)/shard_map/pallas_call | solution.py:502
  8.1 2.4 %shard_map.130 = (bf16[16,128,128]{2,1,0:T(8,128)(2,1)S(1)}, f32[2,88,128]{2,1,0:T(8,128)S(1)}, f32[2,88,128]{2,1,0:T(8,128)S(1)}) custom-call(bf16[16,8,16,256]{3,2,1,0:T(8,128)(2,1)S(1)} %get-tuple-element.45.turned_ref, bf16[16,8,16,512]{3,2,1,0:T(8,128)(2,1)S(1)} %get-tuple-element.46.corr_ref, bf16[8,8,16,256]{3,2,1,0:T(8,128)(2,1)S(1)} %get-tuple-element.49.rim_ref, ...), custom_call_target="tpu_custom_call" | custom-call | flops 2000000000 | bytes 6685696 | tf_op jit(solution)/shard_map/pallas_call | solution.py:502
  10.5 5.7 %collective-permute-start.2 = (f32[2,88,128]{2,1,0:T(8,128)S(1)}, f32[2,88,128]{2,1,0:T(8,128)S(1)}, u32[]{:S(2)}, u32[]{:S(2)}) collective-permute-start(f32[2,88,128]{2,1,0:T(8,128)S(1)} %get-tuple-element.54), channel_id=1, source_target_pairs={{0,4},{4,0},{8,12},{12,8},{1,5},{5,1},{9,13},{13,9},{2,6},{6,2},{1... | collective-permute-start | bytes 270344 | tf_op jit(solution)/shard_map/ppermute | solution.py:528
  16.2 1.6 %shard_map.131 = (bf16[8,128,256]{2,1,0:T(8,128)(2,1)S(1)}, bf16[8,128,256]{2,1,0:T(8,128)(2,1)S(1)}) custom-call(bf16[16,128,128]{2,1,0:T(8,128)(2,1)S(1)} %get-tuple-element.55.gate_ref, bf16[4,128,640]{2,1,0:T(8,128)(2,1)S(1)} %get-tuple-element.56.wide_ref, bf16[16,8,16,256]{3,2,1,0:T(8,128)(2,1)S(1)} %get-tuple-element.57.source_ref), custom_call_target="tpu_custom_call" | custom-call | flops 1000000000 | bytes 2228224 | tf_op jit(solution)/shard_map/pallas_call | solution.py:502
  17.9 0.1 collective-permute-start.7
  18.0 0.7 %collective-permute-start.8 = (bf16[8,128,256]{2,1,0:T(8,128)(2,1)S(1)}, bf16[8,128,256]{2,1,0:T(8,128)(2,1)S(1)}, u32[]{:S(2)}, u32[]{:S(2)}) collective-permute-start(bf16[8,128,256]{2,1,0:T(8,128)(2,1)S(1)} %get-tuple-element.73), channel_id=1, source_target_pairs={{0,0},{4,8},{8,4},{12,12},{1,1},{5,9},{9,5},{13,13},{2,2},{6,10},{... | collective-permute-start | bytes 1572872 | tf_op jit(solution)/shard_map/ppermute | solution.py:648
  18.7 3.4 %collective-permute-start.3 = (f32[1,88,128]{2,1,0:T(8,128)S(1)}, f32[1,88,128]{2,1,0:T(8,128)S(1)}, u32[]{:S(2)}, u32[]{:S(2)}) collective-permute-start(f32[1,88,128]{2,1,0:T(8,128)S(1)} %get-tuple-element.62), channel_id=1, source_target_pairs={{0,8},{4,12},{8,0},{12,4},{1,9},{5,13},{9,1},{13,5},{2,10},{6,14},... | collective-permute-start | bytes 135176 | tf_op jit(solution)/shard_map/ppermute | solution.py:528
  22.1 8.0 %collective-permute-done.3 = f32[1,88,128]{2,1,0:T(8,128)S(1)} collective-permute-done((f32[1,88,128]{2,1,0:T(8,128)S(1)}, f32[1,88,128]{2,1,0:T(8,128)S(1)}, u32[]{:S(2)}, u32[]{:S(2)}) %collective-permute-start.3) | collective-permute-done | bytes 45088 | tf_op jit(solution)/shard_map/ppermute | solution.py:528
  30.1 2.2 %collective-permute-start.4 = (f32[1,88,128]{2,1,0:T(8,128)S(1)}, f32[1,88,128]{2,1,0:T(8,128)S(1)}, u32[]{:S(2)}, u32[]{:S(2)}) collective-permute-start(f32[1,88,128]{2,1,0:T(8,128)S(1)} %add.3.first_ref), channel_id=1, source_target_pairs={{0,1},{1,0},{2,3},{3,2},{4,5},{5,4},{6,7},{7,6},{8,9},{9,8},{10,11... | collective-permute-start | bytes 135176 | tf_op jit(solution)/shard_map/ppermute | solution.py:528
  32.3 2.0 %shard_map.133 = (bf16[16,8,16,1024]{3,2,1,0:T(8,128)(2,1)S(1)}, f32[16,128,256]{2,1,0:T(8,128)S(1)}) custom-call(bf16[16,128,128]{2,1,0:T(8,128)(2,1)S(1)} %get-tuple-element.55.gate_ref, bf16[4,128,640]{2,1,0:T(8,128)(2,1)S(1)} %get-tuple-element.56.wide_ref, bf16[16,8,16,256]{3,2,1,0:T(8,128)(2,1)S(1)} %get-tuple-element.57.source_ref), custom_call_target="tpu_custom_call" | custom-call | flops 2000000000 | bytes 2228224 | tf_op jit(solution)/shard_map/pallas_call | solution.py:502
  34.4 3.3 %collective-permute-start.5 = (f32[2,88,128]{2,1,0:T(8,128)S(1)}, f32[2,88,128]{2,1,0:T(8,128)S(1)}, u32[]{:S(2)}, u32[]{:S(2)}) collective-permute-start(f32[2,88,128]{2,1,0:T(8,128)S(1)} %shard_map.134.rest_0_), channel_id=1, source_target_pairs={{0,2},{1,3},{2,0},{3,1},{4,6},{5,7},{6,4},{7,5},{8,10},{9,11},{10,... | collective-permute-start | bytes 270344 | tf_op jit(solution)/shard_map/ppermute | solution.py:528
  37.7 1.1 %shard_map.135 = f32[16,8,16,256]{3,2,1,0:T(8,128)S(1)} custom-call(bf16[16,8,16,1024]{3,2,1,0:T(8,128)(2,1)S(1)} %get-tuple-element.63.band, bf16[16,144,256]{2,1,0:T(8,128)(2,1)S(1)} %get-tuple-element.66.own_pad, bf16[8,128,256]{2,1,0:T(8,128)(2,1)S(1)} %collective-permute-done.halo_ref.across_ref, bf16[8,128,256]{2,1,0:T(8,128)(2,1)S(1)} %collective-permute-done.1.beyond_ref), custom_call_target="tpu_custom_call" | custom-call | flops 2000000000 | bytes 6422528 | tf_op jit(solution)/shard_map/pallas_call | solution.py:502
  38.8 1.4 %collective-permute-done.5.rest_1_ = f32[2,88,128]{2,1,0:T(8,128)S(1)} collective-permute-done((f32[2,88,128]{2,1,0:T(8,128)S(1)}, f32[2,88,128]{2,1,0:T(8,128)S(1)}, u32[]{:S(2)}, u32[]{:S(2)}) %collective-permute-start.5) | collective-permute-done | bytes 90144 | tf_op jit(solution)/shard_map/ppermute | solution.py:528
  40.2 0.2 shard_map.136
  40.4 2.1 %collective-permute-start.6 = (f32[1,80,128]{2,1,0:T(8,128)S(1)}, f32[1,80,128]{2,1,0:T(8,128)S(1)}, u32[]{:S(2)}, u32[]{:S(2)}) collective-permute-start(f32[1,80,128]{2,1,0:T(8,128)S(1)} %get-tuple-element.68.first_ref), channel_id=1, source_target_pairs={{0,8},{4,12},{8,0},{12,4},{1,9},{5,13},{9,1},{13,5},{2,10},{6,14},... | collective-permute-start | bytes 122888 | tf_op jit(solution)/shard_map/ppermute | solution.py:528
  42.5 1.5 %shard_map.137 = (bf16[16,128,256]{2,1,0:T(8,128)(2,1)}, bf16[16,128,256]{2,1,0:T(8,128)(2,1)}) custom-call(f32[8,128]{1,0:T(8,128)S(1)} %get-tuple-element.69.grad_ref, f32[16,128,256]{2,1,0:T(8,128)S(1)} %bitcast.16, f32[16,128,256]{2,1,0:T(8,128)S(1)} %get-tuple-element.71.edit_ref, bf16[8,128,256]{2,1,0:T(8,128)(2,1)S(1)} %collective-permute-done.7.across_ref, ...), custom_call_target="tpu_custom_call" | custom-call | flops 10000000 | bytes 5246976 | tf_op jit(solution)/shard_map/pallas_call | solution.py:502
  44.0 0.4 collective-permute-done.6.second_ref
  44.4 1.3 %collective-permute-done.9.rest_1_ = f32[2,80,128]{2,1,0:T(8,128)S(1)} collective-permute-done((f32[2,80,128]{2,1,0:T(8,128)S(1)}, f32[2,80,128]{2,1,0:T(8,128)S(1)}, u32[]{:S(2)}, u32[]{:S(2)}) %collective-permute-start.9) | collective-permute-done | bytes 81952 | tf_op jit(solution)/shard_map/ppermute | solution.py:528
  45.7 0.7 %shard_map.139 = (f32[289,128]{1,0:T(8,128)}, f32[1,128]{1,0:T(1,128)}, f32[1,128]{1,0:T(1,128)}, f32[1,128]{1,0:T(1,128)}) custom-call(f32[2,80,128]{2,1,0:T(8,128)S(1)} %shard_map.138.rest_0_, f32[2,80,128]{2,1,0:T(8,128)S(1)} %collective-permute-done.9.rest_1_, f32[1,128]{1,0:T(1,128)S(1)} %get-tuple-element.79.rest_2_), custom_call_target="tpu_custom_call" | custom-call | flops 1000000 | bytes 164352 | tf_op jit(solution)/shard_map/pallas_call | solution.py:502
  (20 shorter events, 0.1 us)
Async XLA Ops:
  1.9 5.4 %collective-permute-start = (bf16[8,128,256]{2,1,0:T(8,128)(2,1)S(1)}, bf16[8,128,256]{2,1,0:T(8,128)(2,1)S(1)}, u32[]{:S(2)}, u32[]{:S(2)}) collective-permute-start(bf16[8,128,256]{2,1,0:T(8,128)(2,1)S(1)} %get-tuple-element.47), channel_id=1, source_target_pairs={{0,4},{4,0},{8,12},{12,8},{1,5},{5,1},{9,13},{13,9},{2,6},{6,2},{1... | collective-permute-start | bytes 1572872 | tf_op jit(solution)/shard_map/ppermute | solution.py:578
  2.4 5.7 %collective-permute-start.1 = (bf16[8,128,256]{2,1,0:T(8,128)(2,1)S(1)}, bf16[8,128,256]{2,1,0:T(8,128)(2,1)S(1)}, u32[]{:S(2)}, u32[]{:S(2)}) collective-permute-start(bf16[8,128,256]{2,1,0:T(8,128)(2,1)S(1)} %get-tuple-element.52), channel_id=1, source_target_pairs={{0,0},{4,8},{8,4},{12,12},{1,1},{5,9},{9,5},{13,13},{2,2},{6,10},{... | collective-permute-start | bytes 1572872 | tf_op jit(solution)/shard_map/ppermute | solution.py:579
  7.2 0.9 %copy-start.3 = (f32[128]{0:T(128)S(1)}, f32[128]{0:T(128)}, u32[]{:S(2)}) copy-start(f32[128]{0:T(128)} %param.11) | copy-start | bytes 1540
  7.2 0.9 %copy-start.4 = (f32[128]{0:T(128)S(1)}, f32[128]{0:T(128)}, u32[]{:S(2)}) copy-start(f32[128]{0:T(128)} %param.12) | copy-start | bytes 1540
  10.5 7.4 %collective-permute-start.2 = (f32[2,88,128]{2,1,0:T(8,128)S(1)}, f32[2,88,128]{2,1,0:T(8,128)S(1)}, u32[]{:S(2)}, u32[]{:S(2)}) collective-permute-start(f32[2,88,128]{2,1,0:T(8,128)S(1)} %get-tuple-element.54), channel_id=1, source_target_pairs={{0,4},{4,0},{8,12},{12,8},{1,5},{5,1},{9,13},{13,9},{2,6},{6,2},{1... | collective-permute-start | bytes 270344 | tf_op jit(solution)/shard_map/ppermute | solution.py:528
  17.9 24.6 %collective-permute-start.7 = (bf16[8,128,256]{2,1,0:T(8,128)(2,1)S(1)}, bf16[8,128,256]{2,1,0:T(8,128)(2,1)S(1)}, u32[]{:S(2)}, u32[]{:S(2)}) collective-permute-start(bf16[8,128,256]{2,1,0:T(8,128)(2,1)S(1)} %get-tuple-element.72), channel_id=1, source_target_pairs={{0,4},{4,0},{8,12},{12,8},{1,5},{5,1},{9,13},{13,9},{2,6},{6,2},{1... | collective-permute-start | bytes 1572872 | tf_op jit(solution)/shard_map/ppermute | solution.py:649
  18.0 24.5 %collective-permute-start.8 = (bf16[8,128,256]{2,1,0:T(8,128)(2,1)S(1)}, bf16[8,128,256]{2,1,0:T(8,128)(2,1)S(1)}, u32[]{:S(2)}, u32[]{:S(2)}) collective-permute-start(bf16[8,128,256]{2,1,0:T(8,128)(2,1)S(1)} %get-tuple-element.73), channel_id=1, source_target_pairs={{0,0},{4,8},{8,4},{12,12},{1,1},{5,9},{9,5},{13,13},{2,2},{6,10},{... | collective-permute-start | bytes 1572872 | tf_op jit(solution)/shard_map/ppermute | solution.py:648
  18.7 11.4 %collective-permute-start.3 = (f32[1,88,128]{2,1,0:T(8,128)S(1)}, f32[1,88,128]{2,1,0:T(8,128)S(1)}, u32[]{:S(2)}, u32[]{:S(2)}) collective-permute-start(f32[1,88,128]{2,1,0:T(8,128)S(1)} %get-tuple-element.62), channel_id=1, source_target_pairs={{0,8},{4,12},{8,0},{12,4},{1,9},{5,13},{9,1},{13,5},{2,10},{6,14},... | collective-permute-start | bytes 135176 | tf_op jit(solution)/shard_map/ppermute | solution.py:528
  30.1 4.3 %collective-permute-start.4 = (f32[1,88,128]{2,1,0:T(8,128)S(1)}, f32[1,88,128]{2,1,0:T(8,128)S(1)}, u32[]{:S(2)}, u32[]{:S(2)}) collective-permute-start(f32[1,88,128]{2,1,0:T(8,128)S(1)} %add.3.first_ref), channel_id=1, source_target_pairs={{0,1},{1,0},{2,3},{3,2},{4,5},{5,4},{6,7},{7,6},{8,9},{9,8},{10,11... | collective-permute-start | bytes 135176 | tf_op jit(solution)/shard_map/ppermute | solution.py:528
  34.4 5.8 %collective-permute-start.5 = (f32[2,88,128]{2,1,0:T(8,128)S(1)}, f32[2,88,128]{2,1,0:T(8,128)S(1)}, u32[]{:S(2)}, u32[]{:S(2)}) collective-permute-start(f32[2,88,128]{2,1,0:T(8,128)S(1)} %shard_map.134.rest_0_), channel_id=1, source_target_pairs={{0,2},{1,3},{2,0},{3,1},{4,6},{5,7},{6,4},{7,5},{8,10},{9,11},{10,... | collective-permute-start | bytes 270344 | tf_op jit(solution)/shard_map/ppermute | solution.py:528
  37.7 2.5 %copy-start = (s32[16]{0:T(128)S(1)}, s32[16]{0:T(128)}, u32[]{:S(2)}) copy-start(s32[16]{0:T(128)} %param.13) | copy-start | bytes 196
  37.7 2.5 %copy-start.1 = (s32[16]{0:T(128)S(1)}, s32[16]{0:T(128)}, u32[]{:S(2)}) copy-start(s32[16]{0:T(128)} %param.14) | copy-start | bytes 196
  37.7 2.5 %copy-start.2 = (s32[16]{0:T(128)S(1)}, s32[16]{0:T(128)}, u32[]{:S(2)}) copy-start(s32[16]{0:T(128)} %param.15) | copy-start | bytes 196
  40.4 4.1 %collective-permute-start.6 = (f32[1,80,128]{2,1,0:T(8,128)S(1)}, f32[1,80,128]{2,1,0:T(8,128)S(1)}, u32[]{:S(2)}, u32[]{:S(2)}) collective-permute-start(f32[1,80,128]{2,1,0:T(8,128)S(1)} %get-tuple-element.68.first_ref), channel_id=1, source_target_pairs={{0,8},{4,12},{8,0},{12,4},{1,9},{5,13},{9,1},{13,5},{2,10},{6,14},... | collective-permute-start | bytes 122888 | tf_op jit(solution)/shard_map/ppermute | solution.py:528
  44.4 1.3 %collective-permute-start.9 = (f32[2,80,128]{2,1,0:T(8,128)S(1)}, f32[2,80,128]{2,1,0:T(8,128)S(1)}, u32[]{:S(2)}, u32[]{:S(2)}) collective-permute-start(f32[2,80,128]{2,1,0:T(8,128)S(1)} %shard_map.138.rest_0_), channel_id=1, source_target_pairs={{0,4},{4,0},{8,12},{12,8},{1,5},{5,1},{9,13},{13,9},{2,6},{6,2},{1... | collective-permute-start | bytes 245768 | tf_op jit(solution)/shard_map/ppermute | solution.py:528

commit v5 on v3

--- a/solution.py
+++ b/solution.py
@@ -526,6 +526,19 @@
     return [(i, partner(i, step, count)) for i in range(count)]
 
 
+def beyond_pairs(space, pairs):
+    table = []
+    for i in range(space):
+        other = i + 1 if i % 2 else i - 1
+        for p in range(pairs):
+            if 0 <= other < space:
+                to = other * pairs + p
+            else:
+                to = i * pairs + (p ^ 1 if p ^ 1 < pairs else p)
+            table.append((i * pairs + p, to))
+    return table
+
+
 def local(
     source_feats, edit_feats, conv_weight, conv_bias, head_weight, comp_first, comp_second, comp_win
 ):
@@ -540,7 +553,7 @@
     edit = edit_feats[0]
     source = source_feats.reshape(rows, groups, GROUP, chan)
     to_across = [(i, i ^ 1 if i ^ 1 < space else i) for i in range(space)]
-    to_beyond = [(i, b if 0 <= (b := i + 1 - 2 * ((i + 1) % 2)) < space else i) for i in range(space)]
+    to_beyond = beyond_pairs(space, pairs)
     across, beyond = call(
         slice_kernel,
         (shape((RADIUS, columns, chan), BF16),) * 2,
@@ -550,7 +563,7 @@
         far=(0,),
     )
     across = lax.ppermute(across, "space", to_across)
-    beyond = lax.ppermute(beyond, "space", to_beyond)
+    beyond = lax.ppermute(beyond, ("space", "pair"), to_beyond)
     near = (rows, groups, GROUP, chan)
     rim_shape = (rows // 2, groups, GROUP, 8 * WIN)
     held, own_pad, turned, corr, wide, tall, own = call(
@@ -617,7 +630,7 @@
         held,
     )
     from_across = lax.ppermute(rim_across, "space", to_across)
-    from_beyond = lax.ppermute(rim_beyond, "space", to_beyond)
+    from_beyond = lax.ppermute(rim_beyond, ("space", "pair"), to_beyond)
     source_sum, edit_sum = call(
         functools.partial(back_kernel, space),
         (shape((rows, groups, GROUP, chan)), shape((rows, columns, chan))),

time: 36.6 us -> 37.7 us (1.030)
  waiting for transfers between devices: 3.15 us -> 7.13 us
  starting transfers between devices: 16.7 us -> 13.9 us
    ppermute x3, starting transfers between devices: 7.48 us -> 1.94 us  [local(): quarter = quarter + lax.ppermute(pieces[k], 'space', around('space', k))]
    ppermute x2, starting transfers between devices: 1.36 us -> 4.71 us  [the longest x1 2.65 us: local(): beyond = lax.ppermute(beyond, ('space', 'pair'), to_beyond)]
    ppermute x3, waiting for transfers between devices: 1.72 us -> 4.16 us  [local(): lax.ppermute(quarter, 'pair', around('pair', k))]
    ppermute x2, waiting for transfers between devices: 0.01 us -> 2.13 us  [the longest x1 2.13 us: local(): beyond = lax.ppermute(beyond, ('space', 'pair'), to_beyond)]
    ppermute x3, waiting for transfers between devices: 0.73 us -> 0.01 us  [local(): quarter = quarter + lax.ppermute(pieces[k], 'space', around('space', k))]
    ppermute x3, starting transfers between devices: 2.41 us -> 1.91 us  [local(): lax.ppermute(total, 'space', around('space', k))]
  transfers between devices with their start and end apart: 13 -> 13, of which waited for: 3 -> 3; matrix products, arithmetic and copies ran while one was open for 0% -> 0% of each run, Pallas kernels for 31% -> 30%
where the time goes in v5:
time: 37.7 us; the launch traced here: 37.5 us
  Pallas kernels  15.6 us (41%)
  starting transfers between devices  13.9 us (37%)
  waiting for transfers between devices  7.13 us (19%)
  between operations  0.77 us (2%)
    pallas_call x9, Pallas kernels, call(): pl.pallas_call(kernel, out_shape=outs, in_specs=[pl.BlockSpec(memory_spac...  15.6 us
    ppermute x3, starting transfers between devices, local(): lax.ppermute(quarter, 'pair', around('pair', k))  4.45 us
    ppermute x3, waiting for transfers between devices, local(): lax.ppermute(quarter, 'pair', around('pair', k))  4.16 us
    ppermute x1, starting transfers between devices, local(): beyond = lax.ppermute(beyond, ('space', 'pair'), to_beyond)  2.65 us
    ppermute x1, waiting for transfers between devices, local(): beyond = lax.ppermute(beyond, ('space', 'pair'), to_beyond)  2.13 us
    ppermute x1, starting transfers between devices, local(): from_beyond = lax.ppermute(rim_beyond, ('space', 'pair'), to_beyond)  2.06 us
    ppermute x3, starting transfers between devices, local(): quarter = quarter + lax.ppermute(pieces[k], 'space', around('space', k))  1.94 us
    ppermute x3, starting transfers between devices, local(): lax.ppermute(total, 'space', around('space', k))  1.91 us
  transfers between devices with their start and end apart: 13, of which 3 were waited for; matrix products, arithmetic and copies ran while one was open for 0% of the time, Pallas kernels for 30%

profile of v5, /device:TPU:0, one launch (start us, length us, event | category | flops | bytes accessed | tf_op | source)
XLA Modules:
  0.0 37.5 jit_solution(6606083126408738473)
XLA Ops:
  0.6 1.2 %shard_map.128 = (bf16[8,128,256]{2,1,0:T(8,128)(2,1)S(1)}, bf16[8,128,256]{2,1,0:T(8,128)(2,1)S(1)}) custom-call(bf16[16,128,256]{2,1,0:T(8,128)(2,1)} %bitcast.22), custom_call_target="tpu_custom_call" | custom-call | flops 10000 | bytes 1048576 | tf_op jit(solution)/shard_map/pallas_call | solution.py:505
  1.9 0.5 %collective-permute-start = (bf16[8,128,256]{2,1,0:T(8,128)(2,1)S(1)}, bf16[8,128,256]{2,1,0:T(8,128)(2,1)S(1)}, u32[]{:S(2)}, u32[]{:S(2)}) collective-permute-start(bf16[8,128,256]{2,1,0:T(8,128)(2,1)S(1)} %get-tuple-element.49), channel_id=1, source_target_pairs={{0,4},{4,0},{8,12},{12,8},{1,5},{5,1},{9,13},{13,9},{2,6},{6,2},{1... | collective-permute-start | bytes 1572872 | tf_op jit(solution)/shard_map/ppermute | solution.py:565
  2.4 2.6 %collective-permute-start.1 = (bf16[8,128,256]{2,1,0:T(8,128)(2,1)S(1)}, bf16[8,128,256]{2,1,0:T(8,128)(2,1)S(1)}, u32[]{:S(2)}, u32[]{:S(2)}) collective-permute-start(bf16[8,128,256]{2,1,0:T(8,128)(2,1)S(1)} %get-tuple-element.54), channel_id=1, source_target_pairs={{0,1},{1,0},{2,3},{3,2},{4,8},{5,9},{6,10},{7,11},{8,4},{9,5},{10,... | collective-permute-start | bytes 1572872 | tf_op jit(solution)/shard_map/ppermute | solution.py:566
  5.0 4.1 %shard_map.127 = (bf16[16,8,16,256]{3,2,1,0:T(8,128)(2,1)S(1)}, bf16[16,144,256]{2,1,0:T(8,128)(2,1)S(1)}, bf16[16,8,16,256]{3,2,1,0:T(8,128)(2,1)S(1)}, bf16[16...) custom-call(bf16[16,8,16,256]{3,2,1,0:T(8,128)(2,1)} %bitcast.24, ...), custom_call_target="tpu_custom_call" | custom-call | flops 2000000000 | bytes 2171136 | tf_op jit(solution)/shard_map/pallas_call | solution.py:505
  9.2 0.9 %shard_map.129 = (bf16[8,8,16,256]{3,2,1,0:T(8,128)(2,1)S(1)}, f32[8,128,128]{2,1,0:T(8,128)S(1)}) custom-call(bf16[16,8,16,256]{3,2,1,0:T(8,128)(2,1)S(1)} %get-tuple-element.47.turned_ref, bf16[8,128,256]{2,1,0:T(8,128)(2,1)S(1)} %collective-permute-done.halo_ref.across_ref, bf16[4,896,128]{2,1,0:T(8,128)(2,1)S(1)} %get-tuple-element.50.tall_ref), custom_call_target="tpu_custom_call" | custom-call | flops 1000000000 | bytes 2490368 | tf_op jit(solution)/shard_map/pallas_call | solution.py:505
  10.1 2.1 %collective-permute-done.1.beyond_ref = bf16[8,128,256]{2,1,0:T(8,128)(2,1)S(1)} collective-permute-done((bf16[8,128,256]{2,1,0:T(8,128)(2,1)S(1)}, bf16[8,128,256]{2,1,0:T(8,128)(2,1)S(1)}, u32[]{:S(2)}, u32[]{:S(2)}) %collective-permute-start.1) | collective-permute-done | bytes 524320 | tf_op jit(solution)/shard_map/ppermute | solution.py:566
  12.2 2.4 %shard_map.130 = (bf16[16,128,128]{2,1,0:T(8,128)(2,1)S(1)}, f32[88,128]{1,0:T(8,128)S(1)}, f32[88,128]{1,0:T(8,128)S(1)}, f32[88,128]{1,0:T(8,128)S(1)}, f32[88,128]{1,0:T(8,128)S(1)}) custom-call(bf16[16,8,16,256]{3,2,1,0:T(8,128)(2,1)S(1)} %get-tuple-element.47.turned_ref, bf16[16,8,16,512]{3,2,1,0:T(8,128)(2,1)S(1)} %get-tuple-element.48.corr_ref, ...), custom_call_target="tpu_custom_call" | custom-call | flops 2000000000 | bytes 6685696 | tf_op jit(solution)/shard_map/pallas_call | solution.py:505
  14.6 0.1 collective-permute-start.2
  14.7 1.5 %collective-permute-start.3 = (f32[88,128]{1,0:T(8,128)S(1)}, f32[88,128]{1,0:T(8,128)S(1)}, u32[]{:S(2)}, u32[]{:S(2)}) collective-permute-start(f32[88,128]{1,0:T(8,128)S(1)} %get-tuple-element.57), channel_id=1, source_target_pairs={{0,8},{4,12},{8,0},{12,4},{1,9},{5,13},{9,1},{13,5},{2,10},{6,14},... | collective-permute-start | bytes 135176 | tf_op jit(solution)/shard_map/ppermute | solution.py:618
  16.2 0.3 collective-permute-start.4
  16.5 1.6 %shard_map.133 = (bf16[8,128,256]{2,1,0:T(8,128)(2,1)S(1)}, bf16[8,128,256]{2,1,0:T(8,128)(2,1)S(1)}) custom-call(bf16[16,128,128]{2,1,0:T(8,128)(2,1)S(1)} %get-tuple-element.59.gate_ref, bf16[4,128,640]{2,1,0:T(8,128)(2,1)S(1)} %get-tuple-element.60.wide_ref, bf16[16,8,16,256]{3,2,1,0:T(8,128)(2,1)S(1)} %get-tuple-element.61.source_ref), custom_call_target="tpu_custom_call" | custom-call | flops 1000000000 | bytes 2228224 | tf_op jit(solution)/shard_map/pallas_call | solution.py:505
  18.2 0.4 %collective-permute-start.11 = (bf16[8,128,256]{2,1,0:T(8,128)(2,1)S(1)}, bf16[8,128,256]{2,1,0:T(8,128)(2,1)S(1)}, u32[]{:S(2)}, u32[]{:S(2)}) collective-permute-start(bf16[8,128,256]{2,1,0:T(8,128)(2,1)S(1)} %get-tuple-element.73), channel_id=1, source_target_pairs={{0,4},{4,0},{8,12},{12,8},{1,5},{5,1},{9,13},{13,9},{2,6},{6,2},{1... | collective-permute-start | bytes 1572872 | tf_op jit(solution)/shard_map/ppermute | solution.py:632
  18.6 2.1 %collective-permute-start.12 = (bf16[8,128,256]{2,1,0:T(8,128)(2,1)S(1)}, bf16[8,128,256]{2,1,0:T(8,128)(2,1)S(1)}, u32[]{:S(2)}, u32[]{:S(2)}) collective-permute-start(bf16[8,128,256]{2,1,0:T(8,128)(2,1)S(1)} %get-tuple-element.74), channel_id=1, source_target_pairs={{0,1},{1,0},{2,3},{3,2},{4,8},{5,9},{6,10},{7,11},{8,4},{9,5},{10,... | collective-permute-start | bytes 1572872 | tf_op jit(solution)/shard_map/ppermute | solution.py:633
  20.7 3.0 %collective-permute-start.7 = (f32[88,128]{1,0:T(8,128)S(1)}, f32[88,128]{1,0:T(8,128)S(1)}, u32[]{:S(2)}, u32[]{:S(2)}) collective-permute-start(f32[88,128]{1,0:T(8,128)S(1)} %add_add_fusion.rest_0_), channel_id=1, source_target_pairs={{0,3},{1,2},{2,1},{3,0},{4,7},{5,6},{6,5},{7,4},{8,11},{9,10},{10,... | collective-permute-start | bytes 135176 | tf_op jit(solution)/shard_map/ppermute | solution.py:650
  23.7 1.4 %collective-permute-start.5 = (f32[88,128]{1,0:T(8,128)S(1)}, f32[88,128]{1,0:T(8,128)S(1)}, u32[]{:S(2)}, u32[]{:S(2)}) collective-permute-start(f32[88,128]{1,0:T(8,128)S(1)} %add_add_fusion.rest_0_), channel_id=1, source_target_pairs={{0,1},{1,0},{2,3},{3,2},{4,5},{5,4},{6,7},{7,6},{8,9},{9,8},{10,11... | collective-permute-start | bytes 135176 | tf_op jit(solution)/shard_map/ppermute | solution.py:650
  25.1 2.9 %shard_map.131 = (f32[16,8,16,256]{3,2,1,0:T(8,128)S(1)}, f32[16,128,256]{2,1,0:T(8,128)S(1)}) custom-call(bf16[16,128,128]{2,1,0:T(8,128)(2,1)S(1)} %get-tuple-element.59.gate_ref, bf16[4,128,640]{2,1,0:T(8,128)(2,1)S(1)} %get-tuple-element.60.wide_ref, bf16[16,8,16,256]{3,2,1,0:T(8,128)(2,1)S(1)} %get-tuple-element.61.source_ref, ...), custom_call_target="tpu_custom_call" | custom-call | flops 4000000000 | bytes 4456448 | tf_op jit(solution)/shard_map/pallas_call | solution.py:505
  28.1 4.2 %collective-permute-done.7.rest_3_ = f32[88,128]{1,0:T(8,128)S(1)} collective-permute-done((f32[88,128]{1,0:T(8,128)S(1)}, f32[88,128]{1,0:T(8,128)S(1)}, u32[]{:S(2)}, u32[]{:S(2)}) %collective-permute-start.7) | collective-permute-done | bytes 45088 | tf_op jit(solution)/shard_map/ppermute | solution.py:650
  32.3 0.2 shard_map.132
  32.4 0.1 collective-permute-start.10
  32.5 0.1 collective-permute-start.9
  32.6 1.8 %collective-permute-start.8 = (f32[80,128]{1,0:T(8,128)S(1)}, f32[80,128]{1,0:T(8,128)S(1)}, u32[]{:S(2)}, u32[]{:S(2)}) collective-permute-start(f32[80,128]{1,0:T(8,128)S(1)} %get-tuple-element.79.rest_0_), channel_id=1, source_target_pairs={{0,4},{4,0},{8,12},{12,8},{1,5},{5,1},{9,13},{13,9},{2,6},{6,2},{1... | collective-permute-start | bytes 122888 | tf_op jit(solution)/shard_map/ppermute | solution.py:662
  34.4 1.6 %shard_map.134 = (bf16[16,128,256]{2,1,0:T(8,128)(2,1)}, bf16[16,128,256]{2,1,0:T(8,128)(2,1)}) custom-call(f32[8,128]{1,0:T(8,128)S(1)} %get-tuple-element.70.grad_ref, f32[16,128,256]{2,1,0:T(8,128)S(1)} %bitcast.16, f32[16,128,256]{2,1,0:T(8,128)S(1)} %get-tuple-element.72.edit_ref, bf16[8,128,256]{2,1,0:T(8,128)(2,1)S(1)} %collective-permute-done.11.across_ref, ...), custom_call_target="tpu_custom_call" | custom-call | flops 10000000 | bytes 5246976 | tf_op jit(solution)/shard_map/pallas_call | solution.py:505
  36.0 0.8 %collective-permute-done.9.rest_2_ = f32[80,128]{1,0:T(8,128)S(1)} collective-permute-done((f32[80,128]{1,0:T(8,128)S(1)}, f32[80,128]{1,0:T(8,128)S(1)}, u32[]{:S(2)}, u32[]{:S(2)}) %collective-permute-start.9) | collective-permute-done | bytes 40992 | tf_op jit(solution)/shard_map/ppermute | solution.py:662
  36.8 0.7 %shard_map.135 = (f32[289,128]{1,0:T(8,128)}, f32[1,128]{1,0:T(1,128)}, f32[1,128]{1,0:T(1,128)}, f32[1,128]{1,0:T(1,128)}) custom-call(f32[80,128]{1,0:T(8,128)S(1)} %get-tuple-element.79.rest_0_, f32[80,128]{1,0:T(8,128)S(1)} %collective-permute-done.8.rest_1_, f32[80,128]{1,0:T(8,128)S(1)} %collective-permute-done.9.rest_2_, ...), custom_call_target="tpu_custom_call" | custom-call | flops 1000000 | bytes 164352 | tf_op jit(solution)/shard_map/pallas_call | solution.py:505
  (22 shorter events, 0.1 us)
Async XLA Ops:
  1.9 7.3 %collective-permute-start = (bf16[8,128,256]{2,1,0:T(8,128)(2,1)S(1)}, bf16[8,128,256]{2,1,0:T(8,128)(2,1)S(1)}, u32[]{:S(2)}, u32[]{:S(2)}) collective-permute-start(bf16[8,128,256]{2,1,0:T(8,128)(2,1)S(1)} %get-tuple-element.49), channel_id=1, source_target_pairs={{0,4},{4,0},{8,12},{12,8},{1,5},{5,1},{9,13},{13,9},{2,6},{6,2},{1... | collective-permute-start | bytes 1572872 | tf_op jit(solution)/shard_map/ppermute | solution.py:565
  2.4 9.8 %collective-permute-start.1 = (bf16[8,128,256]{2,1,0:T(8,128)(2,1)S(1)}, bf16[8,128,256]{2,1,0:T(8,128)(2,1)S(1)}, u32[]{:S(2)}, u32[]{:S(2)}) collective-permute-start(bf16[8,128,256]{2,1,0:T(8,128)(2,1)S(1)} %get-tuple-element.54), channel_id=1, source_target_pairs={{0,1},{1,0},{2,3},{3,2},{4,8},{5,9},{6,10},{7,11},{8,4},{9,5},{10,... | collective-permute-start | bytes 1572872 | tf_op jit(solution)/shard_map/ppermute | solution.py:566
  9.2 3.0 %copy-start.3 = (f32[128]{0:T(128)S(1)}, f32[128]{0:T(128)}, u32[]{:S(2)}) copy-start(f32[128]{0:T(128)} %param.11) | copy-start | bytes 1540
  9.2 3.0 %copy-start.4 = (f32[128]{0:T(128)S(1)}, f32[128]{0:T(128)}, u32[]{:S(2)}) copy-start(f32[128]{0:T(128)} %param.12) | copy-start | bytes 1540
  14.6 6.1 %collective-permute-start.2 = (f32[88,128]{1,0:T(8,128)S(1)}, f32[88,128]{1,0:T(8,128)S(1)}, u32[]{:S(2)}, u32[]{:S(2)}) collective-permute-start(f32[88,128]{1,0:T(8,128)S(1)} %get-tuple-element.56), channel_id=1, source_target_pairs={{0,4},{4,0},{8,12},{12,8},{1,5},{5,1},{9,13},{13,9},{2,6},{6,2},{1... | collective-permute-start | bytes 135176 | tf_op jit(solution)/shard_map/ppermute | solution.py:618
  14.7 5.9 %collective-permute-start.3 = (f32[88,128]{1,0:T(8,128)S(1)}, f32[88,128]{1,0:T(8,128)S(1)}, u32[]{:S(2)}, u32[]{:S(2)}) collective-permute-start(f32[88,128]{1,0:T(8,128)S(1)} %get-tuple-element.57), channel_id=1, source_target_pairs={{0,8},{4,12},{8,0},{12,4},{1,9},{5,13},{9,1},{13,5},{2,10},{6,14},... | collective-permute-start | bytes 135176 | tf_op jit(solution)/shard_map/ppermute | solution.py:618
  16.2 4.5 %collective-permute-start.4 = (f32[88,128]{1,0:T(8,128)S(1)}, f32[88,128]{1,0:T(8,128)S(1)}, u32[]{:S(2)}, u32[]{:S(2)}) collective-permute-start(f32[88,128]{1,0:T(8,128)S(1)} %get-tuple-element.58), channel_id=1, source_target_pairs={{0,12},{4,8},{8,4},{12,0},{1,13},{5,9},{9,5},{13,1},{2,14},{6,10},... | collective-permute-start | bytes 135176 | tf_op jit(solution)/shard_map/ppermute | solution.py:618
  18.2 16.2 %collective-permute-start.11 = (bf16[8,128,256]{2,1,0:T(8,128)(2,1)S(1)}, bf16[8,128,256]{2,1,0:T(8,128)(2,1)S(1)}, u32[]{:S(2)}, u32[]{:S(2)}) collective-permute-start(bf16[8,128,256]{2,1,0:T(8,128)(2,1)S(1)} %get-tuple-element.73), channel_id=1, source_target_pairs={{0,4},{4,0},{8,12},{12,8},{1,5},{5,1},{9,13},{13,9},{2,6},{6,2},{1... | collective-permute-start | bytes 1572872 | tf_op jit(solution)/shard_map/ppermute | solution.py:632
  18.6 15.8 %collective-permute-start.12 = (bf16[8,128,256]{2,1,0:T(8,128)(2,1)S(1)}, bf16[8,128,256]{2,1,0:T(8,128)(2,1)S(1)}, u32[]{:S(2)}, u32[]{:S(2)}) collective-permute-start(bf16[8,128,256]{2,1,0:T(8,128)(2,1)S(1)} %get-tuple-element.74), channel_id=1, source_target_pairs={{0,1},{1,0},{2,3},{3,2},{4,8},{5,9},{6,10},{7,11},{8,4},{9,5},{10,... | collective-permute-start | bytes 1572872 | tf_op jit(solution)/shard_map/ppermute | solution.py:633
  20.7 11.6 %collective-permute-start.7 = (f32[88,128]{1,0:T(8,128)S(1)}, f32[88,128]{1,0:T(8,128)S(1)}, u32[]{:S(2)}, u32[]{:S(2)}) collective-permute-start(f32[88,128]{1,0:T(8,128)S(1)} %add_add_fusion.rest_0_), channel_id=1, source_target_pairs={{0,3},{1,2},{2,1},{3,0},{4,7},{5,6},{6,5},{7,4},{8,11},{9,10},{10,... | collective-permute-start | bytes 135176 | tf_op jit(solution)/shard_map/ppermute | solution.py:650
  23.7 8.5 %collective-permute-start.6 = (f32[88,128]{1,0:T(8,128)S(1)}, f32[88,128]{1,0:T(8,128)S(1)}, u32[]{:S(2)}, u32[]{:S(2)}) collective-permute-start(f32[88,128]{1,0:T(8,128)S(1)} %add_add_fusion.rest_0_), channel_id=1, source_target_pairs={{0,2},{1,3},{2,0},{3,1},{4,6},{5,7},{6,4},{7,5},{8,10},{9,11},{10,... | collective-permute-start | bytes 135176 | tf_op jit(solution)/shard_map/ppermute | solution.py:650
  23.7 8.5 %collective-permute-start.5 = (f32[88,128]{1,0:T(8,128)S(1)}, f32[88,128]{1,0:T(8,128)S(1)}, u32[]{:S(2)}, u32[]{:S(2)}) collective-permute-start(f32[88,128]{1,0:T(8,128)S(1)} %add_add_fusion.rest_0_), channel_id=1, source_target_pairs={{0,1},{1,0},{2,3},{3,2},{4,5},{5,4},{6,7},{7,6},{8,9},{9,8},{10,11... | collective-permute-start | bytes 135176 | tf_op jit(solution)/shard_map/ppermute | solution.py:650
  25.1 7.1 %copy-start = (s32[16]{0:T(128)S(1)}, s32[16]{0:T(128)}, u32[]{:S(2)}) copy-start(s32[16]{0:T(128)} %param.13) | copy-start | bytes 196
  25.1 7.1 %copy-start.1 = (s32[16]{0:T(128)S(1)}, s32[16]{0:T(128)}, u32[]{:S(2)}) copy-start(s32[16]{0:T(128)} %param.14) | copy-start | bytes 196
  25.1 7.1 %copy-start.2 = (s32[16]{0:T(128)S(1)}, s32[16]{0:T(128)}, u32[]{:S(2)}) copy-start(s32[16]{0:T(128)} %param.15) | copy-start | bytes 196
  32.4 3.5 %collective-permute-start.10 = (f32[80,128]{1,0:T(8,128)S(1)}, f32[80,128]{1,0:T(8,128)S(1)}, u32[]{:S(2)}, u32[]{:S(2)}) collective-permute-start(f32[80,128]{1,0:T(8,128)S(1)} %get-tuple-element.79.rest_0_), channel_id=1, source_target_pairs={{0,12},{4,8},{8,4},{12,0},{1,13},{5,9},{9,5},{13,1},{2,14},{6,10},... | collective-permute-start | bytes 122888 | tf_op jit(solution)/shard_map/ppermute | solution.py:662
  32.5 4.3 %collective-permute-start.9 = (f32[80,128]{1,0:T(8,128)S(1)}, f32[80,128]{1,0:T(8,128)S(1)}, u32[]{:S(2)}, u32[]{:S(2)}) collective-permute-start(f32[80,128]{1,0:T(8,128)S(1)} %get-tuple-element.79.rest_0_), channel_id=1, source_target_pairs={{0,8},{4,12},{8,0},{12,4},{1,9},{5,13},{9,1},{13,5},{2,10},{6,14},... | collective-permute-start | bytes 122888 | tf_op jit(solution)/shard_map/ppermute | solution.py:662
  32.6 4.2 %collective-permute-start.8 = (f32[80,128]{1,0:T(8,128)S(1)}, f32[80,128]{1,0:T(8,128)S(1)}, u32[]{:S(2)}, u32[]{:S(2)}) collective-permute-start(f32[80,128]{1,0:T(8,128)S(1)} %get-tuple-element.79.rest_0_), channel_id=1, source_target_pairs={{0,4},{4,0},{8,12},{12,8},{1,5},{5,1},{9,13},{13,9},{2,6},{6,2},{1... | collective-permute-start | bytes 122888 | tf_op jit(solution)/shard_map/ppermute | solution.py:662

commit v6 on v3

--- a/solution.py
+++ b/solution.py
@@ -526,6 +526,16 @@
     return [(i, partner(i, step, count)) for i in range(count)]
 
 
+def beyond_pairs(teams, space):
+    table = []
+    for team in range(teams):
+        for i in range(space):
+            other = i + 1 if i % 2 else i - 1
+            to = (team, other) if 0 <= other < space else (team ^ 1 if team ^ 1 < teams else team, i)
+            table.append((team * space + i, to[0] * space + to[1]))
+    return table
+
+
 def local(
     source_feats, edit_feats, conv_weight, conv_bias, head_weight, comp_first, comp_second, comp_win
 ):
@@ -540,7 +550,7 @@
     edit = edit_feats[0]
     source = source_feats.reshape(rows, groups, GROUP, chan)
     to_across = [(i, i ^ 1 if i ^ 1 < space else i) for i in range(space)]
-    to_beyond = [(i, b if 0 <= (b := i + 1 - 2 * ((i + 1) % 2)) < space else i) for i in range(space)]
+    to_beyond = beyond_pairs(lax.axis_size("groups"), space)
     across, beyond = call(
         slice_kernel,
         (shape((RADIUS, columns, chan), BF16),) * 2,
@@ -550,7 +560,7 @@
         far=(0,),
     )
     across = lax.ppermute(across, "space", to_across)
-    beyond = lax.ppermute(beyond, "space", to_beyond)
+    beyond = lax.ppermute(beyond, ("groups", "space"), to_beyond)
     near = (rows, groups, GROUP, chan)
     rim_shape = (rows // 2, groups, GROUP, 8 * WIN)
     held, own_pad, turned, corr, wide, tall, own = call(
@@ -617,7 +627,7 @@
         held,
     )
     from_across = lax.ppermute(rim_across, "space", to_across)
-    from_beyond = lax.ppermute(rim_beyond, "space", to_beyond)
+    from_beyond = lax.ppermute(rim_beyond, ("groups", "space"), to_beyond)
     source_sum, edit_sum = call(
         functools.partial(back_kernel, space),
         (shape((rows, groups, GROUP, chan)), shape((rows, columns, chan))),

time: 36.6 us -> 34.6 us (0.945)
  starting transfers between devices: 16.7 us -> 13.9 us
  waiting for transfers between devices: 3.15 us -> 4.16 us
    ppermute x3, starting transfers between devices: 7.48 us -> 1.93 us  [local(): quarter = quarter + lax.ppermute(pieces[k], 'space', around('space', k))]
    ppermute x2, starting transfers between devices: 1.36 us -> 4.58 us  [the longest x1 2.56 us: local(): beyond = lax.ppermute(beyond, ('groups', 'space'), to_beyond)]
    ppermute x2, waiting for transfers between devices: 0.01 us -> 2.14 us  [the longest x1 2.14 us: local(): beyond = lax.ppermute(beyond, ('groups', 'space'), to_beyond)]
    ppermute x3, waiting for transfers between devices: 0.73 us -> 0.01 us  [local(): quarter = quarter + lax.ppermute(pieces[k], 'space', around('space', k))]
    ppermute x3, waiting for transfers between devices: 1.72 us -> 1.18 us  [local(): lax.ppermute(quarter, 'pair', around('pair', k))]
    ppermute x3, starting transfers between devices: 2.41 us -> 1.92 us  [local(): lax.ppermute(total, 'space', around('space', k))]
  transfers between devices with their start and end apart: 13 -> 13, of which waited for: 3 -> 3; matrix products, arithmetic and copies ran while one was open for 0% -> 0% of each run, Pallas kernels for 31% -> 33%
where the time goes in v6:
time: 34.6 us; the launch traced here: 34.5 us
  Pallas kernels  15.6 us (45%)
  starting transfers between devices  13.9 us (40%)
  waiting for transfers between devices  4.16 us (12%)
  between operations  0.77 us (2%)
    pallas_call x9, Pallas kernels, call(): pl.pallas_call(kernel, out_shape=outs, in_specs=[pl.BlockSpec(memory_spac...  15.6 us
    ppermute x3, starting transfers between devices, local(): lax.ppermute(quarter, 'pair', around('pair', k))  4.45 us
    ppermute x1, starting transfers between devices, local(): beyond = lax.ppermute(beyond, ('groups', 'space'), to_beyond)  2.56 us
    ppermute x1, waiting for transfers between devices, local(): beyond = lax.ppermute(beyond, ('groups', 'space'), to_beyond)  2.14 us
    ppermute x1, starting transfers between devices, local(): from_beyond = lax.ppermute(rim_beyond, ('groups', 'space'), to_beyond)  2.02 us
    ppermute x3, starting transfers between devices, local(): quarter = quarter + lax.ppermute(pieces[k], 'space', around('space', k))  1.93 us
    ppermute x3, starting transfers between devices, local(): lax.ppermute(total, 'space', around('space', k))  1.92 us
    ppermute x3, waiting for transfers between devices, local(): lax.ppermute(quarter, 'pair', around('pair', k))  1.18 us
  transfers between devices with their start and end apart: 13, of which 3 were waited for; matrix products, arithmetic and copies ran while one was open for 0% of the time, Pallas kernels for 33%

profile of v6, /device:TPU:0, one launch (start us, length us, event | category | flops | bytes accessed | tf_op | source)
XLA Modules:
  0.0 34.5 jit_solution(6758225909072917416)
XLA Ops:
  0.6 1.2 %shard_map.128 = (bf16[8,128,256]{2,1,0:T(8,128)(2,1)S(1)}, bf16[8,128,256]{2,1,0:T(8,128)(2,1)S(1)}) custom-call(bf16[16,128,256]{2,1,0:T(8,128)(2,1)} %bitcast.22), custom_call_target="tpu_custom_call" | custom-call | flops 10000 | bytes 1048576 | tf_op jit(solution)/shard_map/pallas_call | solution.py:505
  1.9 0.5 %collective-permute-start = (bf16[8,128,256]{2,1,0:T(8,128)(2,1)S(1)}, bf16[8,128,256]{2,1,0:T(8,128)(2,1)S(1)}, u32[]{:S(2)}, u32[]{:S(2)}) collective-permute-start(bf16[8,128,256]{2,1,0:T(8,128)(2,1)S(1)} %get-tuple-element.49), channel_id=1, source_target_pairs={{0,4},{4,0},{8,12},{12,8},{1,5},{5,1},{9,13},{13,9},{2,6},{6,2},{1... | collective-permute-start | bytes 1572872 | tf_op jit(solution)/shard_map/ppermute | solution.py:562
  2.4 2.6 %collective-permute-start.1 = (bf16[8,128,256]{2,1,0:T(8,128)(2,1)S(1)}, bf16[8,128,256]{2,1,0:T(8,128)(2,1)S(1)}, u32[]{:S(2)}, u32[]{:S(2)}) collective-permute-start(bf16[8,128,256]{2,1,0:T(8,128)(2,1)S(1)} %get-tuple-element.54), channel_id=1, source_target_pairs={{0,16},{4,8},{8,4},{12,28},{16,0},{20,24},{24,20},{28,12},{1,17},{... | collective-permute-start | bytes 1572872 | tf_op jit(solution)/shard_map/ppermute | solution.py:563
  5.0 4.1 %shard_map.127 = (bf16[16,8,16,256]{3,2,1,0:T(8,128)(2,1)S(1)}, bf16[16,144,256]{2,1,0:T(8,128)(2,1)S(1)}, bf16[16,8,16,256]{3,2,1,0:T(8,128)(2,1)S(1)}, bf16[16...) custom-call(bf16[16,8,16,256]{3,2,1,0:T(8,128)(2,1)} %bitcast.24, ...), custom_call_target="tpu_custom_call" | custom-call | flops 2000000000 | bytes 2171136 | tf_op jit(solution)/shard_map/pallas_call | solution.py:505
  9.1 0.8 %shard_map.129 = (bf16[8,8,16,256]{3,2,1,0:T(8,128)(2,1)S(1)}, f32[8,128,128]{2,1,0:T(8,128)S(1)}) custom-call(bf16[16,8,16,256]{3,2,1,0:T(8,128)(2,1)S(1)} %get-tuple-element.47.turned_ref, bf16[8,128,256]{2,1,0:T(8,128)(2,1)S(1)} %collective-permute-done.halo_ref.across_ref, bf16[4,896,128]{2,1,0:T(8,128)(2,1)S(1)} %get-tuple-element.50.tall_ref), custom_call_target="tpu_custom_call" | custom-call | flops 1000000000 | bytes 2490368 | tf_op jit(solution)/shard_map/pallas_call | solution.py:505
  10.0 2.1 %collective-permute-done.1.beyond_ref = bf16[8,128,256]{2,1,0:T(8,128)(2,1)S(1)} collective-permute-done((bf16[8,128,256]{2,1,0:T(8,128)(2,1)S(1)}, bf16[8,128,256]{2,1,0:T(8,128)(2,1)S(1)}, u32[]{:S(2)}, u32[]{:S(2)}) %collective-permute-start.1) | collective-permute-done | bytes 524320 | tf_op jit(solution)/shard_map/ppermute | solution.py:563
  12.1 2.4 %shard_map.130 = (bf16[16,128,128]{2,1,0:T(8,128)(2,1)S(1)}, f32[88,128]{1,0:T(8,128)S(1)}, f32[88,128]{1,0:T(8,128)S(1)}, f32[88,128]{1,0:T(8,128)S(1)}, f32[88,128]{1,0:T(8,128)S(1)}) custom-call(bf16[16,8,16,256]{3,2,1,0:T(8,128)(2,1)S(1)} %get-tuple-element.47.turned_ref, bf16[16,8,16,512]{3,2,1,0:T(8,128)(2,1)S(1)} %get-tuple-element.48.corr_ref, ...), custom_call_target="tpu_custom_call" | custom-call | flops 2000000000 | bytes 6685696 | tf_op jit(solution)/shard_map/pallas_call | solution.py:505
  14.5 0.2 collective-permute-start.2
  14.7 1.5 %collective-permute-start.3 = (f32[88,128]{1,0:T(8,128)S(1)}, f32[88,128]{1,0:T(8,128)S(1)}, u32[]{:S(2)}, u32[]{:S(2)}) collective-permute-start(f32[88,128]{1,0:T(8,128)S(1)} %get-tuple-element.57), channel_id=1, source_target_pairs={{0,8},{4,12},{8,0},{12,4},{1,9},{5,13},{9,1},{13,5},{2,10},{6,14},... | collective-permute-start | bytes 135176 | tf_op jit(solution)/shard_map/ppermute | solution.py:615
  16.2 0.2 collective-permute-start.4
  16.4 1.7 %shard_map.133 = (bf16[8,128,256]{2,1,0:T(8,128)(2,1)S(1)}, bf16[8,128,256]{2,1,0:T(8,128)(2,1)S(1)}) custom-call(bf16[16,128,128]{2,1,0:T(8,128)(2,1)S(1)} %get-tuple-element.59.gate_ref, bf16[4,128,640]{2,1,0:T(8,128)(2,1)S(1)} %get-tuple-element.60.wide_ref, bf16[16,8,16,256]{3,2,1,0:T(8,128)(2,1)S(1)} %get-tuple-element.61.source_ref), custom_call_target="tpu_custom_call" | custom-call | flops 1000000000 | bytes 2228224 | tf_op jit(solution)/shard_map/pallas_call | solution.py:505
  18.1 0.5 %collective-permute-start.11 = (bf16[8,128,256]{2,1,0:T(8,128)(2,1)S(1)}, bf16[8,128,256]{2,1,0:T(8,128)(2,1)S(1)}, u32[]{:S(2)}, u32[]{:S(2)}) collective-permute-start(bf16[8,128,256]{2,1,0:T(8,128)(2,1)S(1)} %get-tuple-element.73), channel_id=1, source_target_pairs={{0,4},{4,0},{8,12},{12,8},{1,5},{5,1},{9,13},{13,9},{2,6},{6,2},{1... | collective-permute-start | bytes 1572872 | tf_op jit(solution)/shard_map/ppermute | solution.py:629
  18.6 2.0 %collective-permute-start.12 = (bf16[8,128,256]{2,1,0:T(8,128)(2,1)S(1)}, bf16[8,128,256]{2,1,0:T(8,128)(2,1)S(1)}, u32[]{:S(2)}, u32[]{:S(2)}) collective-permute-start(bf16[8,128,256]{2,1,0:T(8,128)(2,1)S(1)} %get-tuple-element.74), channel_id=1, source_target_pairs={{0,16},{4,8},{8,4},{12,28},{16,0},{20,24},{24,20},{28,12},{1,17},{... | collective-permute-start | bytes 1572872 | tf_op jit(solution)/shard_map/ppermute | solution.py:630
  20.6 3.6 %collective-permute-start.7 = (f32[88,128]{1,0:T(8,128)S(1)}, f32[88,128]{1,0:T(8,128)S(1)}, u32[]{:S(2)}, u32[]{:S(2)}) collective-permute-start(f32[88,128]{1,0:T(8,128)S(1)} %add_add_fusion.rest_0_), channel_id=1, source_target_pairs={{0,3},{1,2},{2,1},{3,0},{4,7},{5,6},{6,5},{7,4},{8,11},{9,10},{10,... | collective-permute-start | bytes 135176 | tf_op jit(solution)/shard_map/ppermute | solution.py:647
  24.3 0.8 %collective-permute-start.5 = (f32[88,128]{1,0:T(8,128)S(1)}, f32[88,128]{1,0:T(8,128)S(1)}, u32[]{:S(2)}, u32[]{:S(2)}) collective-permute-start(f32[88,128]{1,0:T(8,128)S(1)} %add_add_fusion.rest_0_), channel_id=1, source_target_pairs={{0,1},{1,0},{2,3},{3,2},{4,5},{5,4},{6,7},{7,6},{8,9},{9,8},{10,11... | collective-permute-start | bytes 135176 | tf_op jit(solution)/shard_map/ppermute | solution.py:647
  25.1 2.9 %shard_map.131 = (f32[16,8,16,256]{3,2,1,0:T(8,128)S(1)}, f32[16,128,256]{2,1,0:T(8,128)S(1)}) custom-call(bf16[16,128,128]{2,1,0:T(8,128)(2,1)S(1)} %get-tuple-element.59.gate_ref, bf16[4,128,640]{2,1,0:T(8,128)(2,1)S(1)} %get-tuple-element.60.wide_ref, bf16[16,8,16,256]{3,2,1,0:T(8,128)(2,1)S(1)} %get-tuple-element.61.source_ref, ...), custom_call_target="tpu_custom_call" | custom-call | flops 4000000000 | bytes 4456448 | tf_op jit(solution)/shard_map/pallas_call | solution.py:505
  28.0 1.2 %collective-permute-done.6.rest_2_ = f32[88,128]{1,0:T(8,128)S(1)} collective-permute-done((f32[88,128]{1,0:T(8,128)S(1)}, f32[88,128]{1,0:T(8,128)S(1)}, u32[]{:S(2)}, u32[]{:S(2)}) %collective-permute-start.6) | collective-permute-done | bytes 45088 | tf_op jit(solution)/shard_map/ppermute | solution.py:647
  29.2 0.2 shard_map.132
  29.4 0.1 collective-permute-start.10
  29.5 0.5 %collective-permute-start.9 = (f32[80,128]{1,0:T(8,128)S(1)}, f32[80,128]{1,0:T(8,128)S(1)}, u32[]{:S(2)}, u32[]{:S(2)}) collective-permute-start(f32[80,128]{1,0:T(8,128)S(1)} %get-tuple-element.79.rest_0_), channel_id=1, source_target_pairs={{0,8},{4,12},{8,0},{12,4},{1,9},{5,13},{9,1},{13,5},{2,10},{6,14},... | collective-permute-start | bytes 122888 | tf_op jit(solution)/shard_map/ppermute | solution.py:659
  30.0 1.3 %collective-permute-start.8 = (f32[80,128]{1,0:T(8,128)S(1)}, f32[80,128]{1,0:T(8,128)S(1)}, u32[]{:S(2)}, u32[]{:S(2)}) collective-permute-start(f32[80,128]{1,0:T(8,128)S(1)} %get-tuple-element.79.rest_0_), channel_id=1, source_target_pairs={{0,4},{4,0},{8,12},{12,8},{1,5},{5,1},{9,13},{13,9},{2,6},{6,2},{1... | collective-permute-start | bytes 122888 | tf_op jit(solution)/shard_map/ppermute | solution.py:659
  31.3 1.6 %shard_map.134 = (bf16[16,128,256]{2,1,0:T(8,128)(2,1)}, bf16[16,128,256]{2,1,0:T(8,128)(2,1)}) custom-call(f32[8,128]{1,0:T(8,128)S(1)} %get-tuple-element.70.grad_ref, f32[16,128,256]{2,1,0:T(8,128)S(1)} %bitcast.16, f32[16,128,256]{2,1,0:T(8,128)S(1)} %get-tuple-element.72.edit_ref, bf16[8,128,256]{2,1,0:T(8,128)(2,1)S(1)} %collective-permute-done.11.across_ref, ...), custom_call_target="tpu_custom_call" | custom-call | flops 10000000 | bytes 5246976 | tf_op jit(solution)/shard_map/pallas_call | solution.py:505
  32.9 0.8 %collective-permute-done.9.rest_2_ = f32[80,128]{1,0:T(8,128)S(1)} collective-permute-done((f32[80,128]{1,0:T(8,128)S(1)}, f32[80,128]{1,0:T(8,128)S(1)}, u32[]{:S(2)}, u32[]{:S(2)}) %collective-permute-start.9) | collective-permute-done | bytes 40992 | tf_op jit(solution)/shard_map/ppermute | solution.py:659
  33.8 0.7 %shard_map.135 = (f32[289,128]{1,0:T(8,128)}, f32[1,128]{1,0:T(1,128)}, f32[1,128]{1,0:T(1,128)}, f32[1,128]{1,0:T(1,128)}) custom-call(f32[80,128]{1,0:T(8,128)S(1)} %get-tuple-element.79.rest_0_, f32[80,128]{1,0:T(8,128)S(1)} %collective-permute-done.8.rest_1_, f32[80,128]{1,0:T(8,128)S(1)} %collective-permute-done.9.rest_2_, ...), custom_call_target="tpu_custom_call" | custom-call | flops 1000000 | bytes 164352 | tf_op jit(solution)/shard_map/pallas_call | solution.py:505
  (22 shorter events, 0.1 us)
Async XLA Ops:
  1.9 7.2 %collective-permute-start = (bf16[8,128,256]{2,1,0:T(8,128)(2,1)S(1)}, bf16[8,128,256]{2,1,0:T(8,128)(2,1)S(1)}, u32[]{:S(2)}, u32[]{:S(2)}) collective-permute-start(bf16[8,128,256]{2,1,0:T(8,128)(2,1)S(1)} %get-tuple-element.49), channel_id=1, source_target_pairs={{0,4},{4,0},{8,12},{12,8},{1,5},{5,1},{9,13},{13,9},{2,6},{6,2},{1... | collective-permute-start | bytes 1572872 | tf_op jit(solution)/shard_map/ppermute | solution.py:562
  2.4 9.7 %collective-permute-start.1 = (bf16[8,128,256]{2,1,0:T(8,128)(2,1)S(1)}, bf16[8,128,256]{2,1,0:T(8,128)(2,1)S(1)}, u32[]{:S(2)}, u32[]{:S(2)}) collective-permute-start(bf16[8,128,256]{2,1,0:T(8,128)(2,1)S(1)} %get-tuple-element.54), channel_id=1, source_target_pairs={{0,16},{4,8},{8,4},{12,28},{16,0},{20,24},{24,20},{28,12},{1,17},{... | collective-permute-start | bytes 1572872 | tf_op jit(solution)/shard_map/ppermute | solution.py:563
  9.1 3.0 %copy-start.3 = (f32[128]{0:T(128)S(1)}, f32[128]{0:T(128)}, u32[]{:S(2)}) copy-start(f32[128]{0:T(128)} %param.11) | copy-start | bytes 1540
  9.1 3.0 %copy-start.4 = (f32[128]{0:T(128)S(1)}, f32[128]{0:T(128)}, u32[]{:S(2)}) copy-start(f32[128]{0:T(128)} %param.12) | copy-start | bytes 1540
  14.5 6.1 %collective-permute-start.2 = (f32[88,128]{1,0:T(8,128)S(1)}, f32[88,128]{1,0:T(8,128)S(1)}, u32[]{:S(2)}, u32[]{:S(2)}) collective-permute-start(f32[88,128]{1,0:T(8,128)S(1)} %get-tuple-element.56), channel_id=1, source_target_pairs={{0,4},{4,0},{8,12},{12,8},{1,5},{5,1},{9,13},{13,9},{2,6},{6,2},{1... | collective-permute-start | bytes 135176 | tf_op jit(solution)/shard_map/ppermute | solution.py:615
  14.7 5.9 %collective-permute-start.3 = (f32[88,128]{1,0:T(8,128)S(1)}, f32[88,128]{1,0:T(8,128)S(1)}, u32[]{:S(2)}, u32[]{:S(2)}) collective-permute-start(f32[88,128]{1,0:T(8,128)S(1)} %get-tuple-element.57), channel_id=1, source_target_pairs={{0,8},{4,12},{8,0},{12,4},{1,9},{5,13},{9,1},{13,5},{2,10},{6,14},... | collective-permute-start | bytes 135176 | tf_op jit(solution)/shard_map/ppermute | solution.py:615
  16.2 4.4 %collective-permute-start.4 = (f32[88,128]{1,0:T(8,128)S(1)}, f32[88,128]{1,0:T(8,128)S(1)}, u32[]{:S(2)}, u32[]{:S(2)}) collective-permute-start(f32[88,128]{1,0:T(8,128)S(1)} %get-tuple-element.58), channel_id=1, source_target_pairs={{0,12},{4,8},{8,4},{12,0},{1,13},{5,9},{9,5},{13,1},{2,14},{6,10},... | collective-permute-start | bytes 135176 | tf_op jit(solution)/shard_map/ppermute | solution.py:615
  18.1 13.3 %collective-permute-start.11 = (bf16[8,128,256]{2,1,0:T(8,128)(2,1)S(1)}, bf16[8,128,256]{2,1,0:T(8,128)(2,1)S(1)}, u32[]{:S(2)}, u32[]{:S(2)}) collective-permute-start(bf16[8,128,256]{2,1,0:T(8,128)(2,1)S(1)} %get-tuple-element.73), channel_id=1, source_target_pairs={{0,4},{4,0},{8,12},{12,8},{1,5},{5,1},{9,13},{13,9},{2,6},{6,2},{1... | collective-permute-start | bytes 1572872 | tf_op jit(solution)/shard_map/ppermute | solution.py:629
  18.6 12.8 %collective-permute-start.12 = (bf16[8,128,256]{2,1,0:T(8,128)(2,1)S(1)}, bf16[8,128,256]{2,1,0:T(8,128)(2,1)S(1)}, u32[]{:S(2)}, u32[]{:S(2)}) collective-permute-start(bf16[8,128,256]{2,1,0:T(8,128)(2,1)S(1)} %get-tuple-element.74), channel_id=1, source_target_pairs={{0,16},{4,8},{8,4},{12,28},{16,0},{20,24},{24,20},{28,12},{1,17},{... | collective-permute-start | bytes 1572872 | tf_op jit(solution)/shard_map/ppermute | solution.py:630
  20.6 7.4 %collective-permute-start.7 = (f32[88,128]{1,0:T(8,128)S(1)}, f32[88,128]{1,0:T(8,128)S(1)}, u32[]{:S(2)}, u32[]{:S(2)}) collective-permute-start(f32[88,128]{1,0:T(8,128)S(1)} %add_add_fusion.rest_0_), channel_id=1, source_target_pairs={{0,3},{1,2},{2,1},{3,0},{4,7},{5,6},{6,5},{7,4},{8,11},{9,10},{10,... | collective-permute-start | bytes 135176 | tf_op jit(solution)/shard_map/ppermute | solution.py:647
  24.3 4.9 %collective-permute-start.6 = (f32[88,128]{1,0:T(8,128)S(1)}, f32[88,128]{1,0:T(8,128)S(1)}, u32[]{:S(2)}, u32[]{:S(2)}) collective-permute-start(f32[88,128]{1,0:T(8,128)S(1)} %add_add_fusion.rest_0_), channel_id=1, source_target_pairs={{0,2},{1,3},{2,0},{3,1},{4,6},{5,7},{6,4},{7,5},{8,10},{9,11},{10,... | collective-permute-start | bytes 135176 | tf_op jit(solution)/shard_map/ppermute | solution.py:647
  24.3 4.9 %collective-permute-start.5 = (f32[88,128]{1,0:T(8,128)S(1)}, f32[88,128]{1,0:T(8,128)S(1)}, u32[]{:S(2)}, u32[]{:S(2)}) collective-permute-start(f32[88,128]{1,0:T(8,128)S(1)} %add_add_fusion.rest_0_), channel_id=1, source_target_pairs={{0,1},{1,0},{2,3},{3,2},{4,5},{5,4},{6,7},{7,6},{8,9},{9,8},{10,11... | collective-permute-start | bytes 135176 | tf_op jit(solution)/shard_map/ppermute | solution.py:647
  25.1 4.1 %copy-start = (s32[16]{0:T(128)S(1)}, s32[16]{0:T(128)}, u32[]{:S(2)}) copy-start(s32[16]{0:T(128)} %param.13) | copy-start | bytes 196
  25.1 4.1 %copy-start.1 = (s32[16]{0:T(128)S(1)}, s32[16]{0:T(128)}, u32[]{:S(2)}) copy-start(s32[16]{0:T(128)} %param.14) | copy-start | bytes 196
  25.1 4.1 %copy-start.2 = (s32[16]{0:T(128)S(1)}, s32[16]{0:T(128)}, u32[]{:S(2)}) copy-start(s32[16]{0:T(128)} %param.15) | copy-start | bytes 196
  29.4 3.5 %collective-permute-start.10 = (f32[80,128]{1,0:T(8,128)S(1)}, f32[80,128]{1,0:T(8,128)S(1)}, u32[]{:S(2)}, u32[]{:S(2)}) collective-permute-start(f32[80,128]{1,0:T(8,128)S(1)} %get-tuple-element.79.rest_0_), channel_id=1, source_target_pairs={{0,12},{4,8},{8,4},{12,0},{1,13},{5,9},{9,5},{13,1},{2,14},{6,10},... | collective-permute-start | bytes 122888 | tf_op jit(solution)/shard_map/ppermute | solution.py:659
  29.5 4.3 %collective-permute-start.9 = (f32[80,128]{1,0:T(8,128)S(1)}, f32[80,128]{1,0:T(8,128)S(1)}, u32[]{:S(2)}, u32[]{:S(2)}) collective-permute-start(f32[80,128]{1,0:T(8,128)S(1)} %get-tuple-element.79.rest_0_), channel_id=1, source_target_pairs={{0,8},{4,12},{8,0},{12,4},{1,9},{5,13},{9,1},{13,5},{2,10},{6,14},... | collective-permute-start | bytes 122888 | tf_op jit(solution)/shard_map/ppermute | solution.py:659
  30.0 3.8 %collective-permute-start.8 = (f32[80,128]{1,0:T(8,128)S(1)}, f32[80,128]{1,0:T(8,128)S(1)}, u32[]{:S(2)}, u32[]{:S(2)}) collective-permute-start(f32[80,128]{1,0:T(8,128)S(1)} %get-tuple-element.79.rest_0_), channel_id=1, source_target_pairs={{0,4},{4,0},{8,12},{12,8},{1,5},{5,1},{9,13},{13,9},{2,6},{6,2},{1... | collective-permute-start | bytes 122888 | tf_op jit(solution)/shard_map/ppermute | solution.py:659

commit v7 on v6

--- a/solution.py
+++ b/solution.py
@@ -107,46 +107,50 @@
     tall = jnp.concatenate(talls, axis=0).astype(BF16)[: SPAN * WIN]
     tall_rows = tall_ref.shape[1]
     for r in range(PER):
-        wide_ref[r] = (base if r == 0 else pltpu.roll(base, r * WIN, 1)).astype(BF16)
+        edge = jnp.zeros((kout, LANES), BF16)
+        moved = base if r == 0 else pltpu.roll(base, r * WIN, 1)
+        wide_ref[r] = jnp.concatenate([edge, moved.astype(BF16), edge], axis=1)
         start = LANES + r * WIN
         tall_ref[r, :start] = jnp.zeros((start, kout), BF16)
         tall_ref[r, start : start + SPAN * WIN] = tall
         tall_ref[r, start + SPAN * WIN :] = jnp.zeros((tall_rows - start - SPAN * WIN, kout), BF16)
 
 
-def inner_kernel(
-    inv_root,
+def load_kernel(
     source_hbm,
     edit_hbm,
     weight_hbm,
     source_ref,
     pad,
     turned_ref,
-    corr_ref,
     wide_ref,
     tall_ref,
-    own_ref,
     weight,
     sems,
 ):
     rows, groups, _, chan = source_ref.shape
+    cols = groups * GROUP
     weight_copy = pltpu.make_async_copy(weight_hbm, weight, sems.at[2])
+    source_copy = pltpu.make_async_copy(source_hbm, source_ref, sems.at[1])
+    edit_copy = pltpu.make_async_copy(edit_hbm, pad.at[:, RADIUS : RADIUS + cols], sems.at[0])
     weight_copy.start()
-    copies = []
-    cols = groups * GROUP
-    edit_copy = pltpu.make_async_copy(edit_hbm, pad.at[:, RADIUS : RADIUS + cols], sems.at[0])
-    source_copy = pltpu.make_async_copy(source_hbm, source_ref, sems.at[1])
+    source_copy.start()
     edit_copy.start()
-    source_copy.start()
-    fill_columns(pad, 0, rows, groups * GROUP)
+    fill_columns(pad, 0, rows, cols)
     turn = mirror(rows * GROUP)
     weight_copy.wait()
     spread_weights(weight, wide_ref, tall_ref)
     source_copy.wait()
-    edit_copy.wait()
     for g in range(groups):
         lhs = nn(turn, source_ref[:, g].reshape(rows * GROUP, chan)).astype(BF16)
         turned_ref[:, g] = lhs.reshape(rows, GROUP, chan)
+    edit_copy.wait()
+
+
+def inner_kernel(inv_root, turned_ref, pad, tall_ref, corr_ref, own_ref):
+    rows, groups, _, chan = turned_ref.shape
+    for g in range(groups):
+        lhs = turned_ref[:, g].reshape(rows * GROUP, chan)
         for s in range(rows // 8):
             correlate_set(lhs, pad, 8 * s, g, inv_root, corr_ref, slice(0, rows), 2 * s * LANES)
     cols = groups * GROUP
@@ -193,11 +197,72 @@
         out_ref[i] = nn(lhs, tall_ref[r, pl.ds(start, lanes), :])
 
 
+def half_rows(above, own_ref, extra, corr_ref, rim, strip, bias_ref, head_ref, gate_ref, gate_at):
+    half, groups = rim.shape[:2]
+    cols = groups * GROUP
+    rim_lanes, own_lanes = rim.shape[3], corr_ref.shape[3]
+
+    @pl.when(above == 0)
+    def _():
+        strip[:, :, :, :rim_lanes] = rim[...]
+        strip[:, :, :, rim_lanes:] = corr_ref[:half]
+
+    @pl.when(above == 1)
+    def _():
+        strip[:, :, :, :own_lanes] = corr_ref[half:]
+        strip[:, :, :, own_lanes:] = rim[...]
+
+    bias, head = bias_ref[...], head_ref[...]
+    kout = bias.shape[1]
+    turn = mirror(cols)
+    hidden = jnp.zeros((1, kout), F32)
+    slopes = jnp.zeros((1, kout), F32)
+    total = None
+    for r in range(PER):
+        rows = [q * PER + r for q in range(half // PER)]
+        value = jnp.concatenate([own_ref[half * above + i] + extra[i] for i in rows], axis=0) + bias
+        gating = jax.nn.sigmoid(value)
+        act = value * gating
+        slope = gating * (1.0 + value * (1.0 - gating))
+        hidden = hidden + jnp.sum(act, axis=0, keepdims=True)
+        slopes = slopes + jnp.sum(slope, axis=0, keepdims=True)
+        pre = (slope * head).astype(BF16)
+        for q, i in enumerate(rows):
+            gate_ref[gate_at + i] = nn(turn, pre[q * cols : (q + 1) * cols]).astype(BF16)
+        corr = [strip[i, :, :, i // PER * LANES : (i // PER + POS) * LANES] for i in rows]
+        corr = jnp.concatenate([c.reshape(cols, POS * LANES) for c in corr], axis=0)
+        grad = tn(pre, corr)
+        if r:
+            grad = pltpu.roll(grad, POS * LANES - r * WIN, 1)
+        total = grad if total is None else total + grad
+    return hidden, slopes, total
+
+
 def across_kernel(
-    inv_root, parts, turned_ref, halo_ref, tall_ref, rim_ref, extra_ref, pad
+    inv_root,
+    parts,
+    turned_ref,
+    corr_ref,
+    own_ref,
+    halo_ref,
+    tall_ref,
+    bias_ref,
+    head_ref,
+    gate_ref,
+    sums_ref,
+    total_ref,
+    pad,
+    rim,
+    extra,
+    strip,
 ):
-    above = rim_scores(inv_root, parts, 0, turned_ref, halo_ref, pad, rim_ref)
-    rim_values(rim_ref, tall_ref, above, extra_ref)
+    above = rim_scores(inv_root, parts, 0, turned_ref, halo_ref, pad, rim)
+    rim_values(rim, tall_ref, above, extra)
+    hidden, slopes, total_ref[...] = half_rows(
+        above, own_ref, extra, corr_ref, rim, strip, bias_ref, head_ref, gate_ref, 0
+    )
+    sums_ref[0:1] = hidden
+    sums_ref[1:2] = slopes
 
 
 def slice_kernel(edit_ref, across_ref, beyond_ref, sems):
@@ -219,23 +284,14 @@
         copy.wait()
 
 
-def row_chunks(rims, corr_ref, r, rows):
-    pieces = []
-    half = rows // 2
-    for q in range(rows // PER):
-        y = q * PER + r
-        parts = []
-        for c in range(q, q + POS):
-            if c < 2:
-                part = rims[0, y, :, :, c * LANES : (c + 1) * LANES]
-            elif c < 2 + rows // PER:
-                part = corr_ref[y, :, :, (c - 2) * LANES : (c - 1) * LANES]
-            else:
-                at = c - 2 - rows // PER
-                part = rims[1, y - half, :, :, at * LANES : (at + 1) * LANES]
-            parts.append(part.reshape(part.shape[0] * part.shape[1], LANES))
-        pieces.append(jnp.concatenate(parts, axis=1))
-    return jnp.concatenate(pieces, axis=0)
+def put_rows(stage, share, row, values):
+    done = 0
+    while done < values.shape[0]:
+        piece, at = divmod(row + done, share - 1)
+        count = min(values.shape[0] - done, share - 1 - at)
+        start = piece * share + at
+        stage[start : start + count] = values[done : done + count]
+        done += count
 
 
 def outer_kernel(
@@ -244,70 +300,42 @@
     parts,
     turned_ref,
     corr_ref,
-    rim_ref,
-    extra_ref,
     own_ref,
-    beyond_ref,
+    halo_ref,
     tall_ref,
     bias_ref,
     head_ref,
+    near_gate_ref,
+    near_sums_ref,
+    near_total_ref,
     *rest,
 ):
-    gate_ref = rest[0]
-    piece_refs = rest[1 : 1 + parts]
-    pad, rims, extra, stage = rest[1 + parts :]
-    rows, groups = turned_ref.shape[:2]
-    above, _ = edge_spot(parts, 1)
-    rims[1 - above] = rim_ref[...]
-    extra[1 - above] = extra_ref[...]
-    rim_scores(inv_root, parts, 1, turned_ref, beyond_ref, pad, rims.at[above])
-    rim_values(rims.at[above], tall_ref, above, extra.at[above])
-    bias, head = bias_ref[...], head_ref[...]
-    kout = bias.shape[1]
-    cols = groups * GROUP
-    turn = mirror(cols)
-    hidden = jnp.zeros((1, kout), F32)
-    slopes = jnp.zeros((1, kout), F32)
-    total = None
-    for r in range(PER):
-        corr = row_chunks(rims, corr_ref, r, rows)
-        spots = [(q * PER + r, q // 2, q % 2 * PER + r) for q in range(rows // PER)]
-        value = jnp.concatenate([own_ref[y] + extra[h, i] for y, h, i in spots], axis=0) + bias
-        gating = jax.nn.sigmoid(value)
-        act = value * gating
-        slope = gating * (1.0 + value * (1.0 - gating))
-        hidden = hidden + jnp.sum(act, axis=0, keepdims=True)
-        slopes = slopes + jnp.sum(slope, axis=0, keepdims=True)
-        pre = (slope * head).astype(BF16)
-        for q in range(rows // PER):
-            gate_ref[q * PER + r] = nn(turn, pre[q * cols : (q + 1) * cols]).astype(BF16)
-        grad = tn(pre, corr)
-        if r:
-            grad = pltpu.roll(grad, POS * LANES - r * WIN, 1)
-        total = grad if total is None else total + grad
+    gate_ref, *piece_refs, pad, rim, extra, strip, stage = rest
+    half = rim.shape[0]
+    above = rim_scores(inv_root, parts, 1, turned_ref, halo_ref, pad, rim)
+    rim_values(rim, tall_ref, above, extra)
+    gate_ref[pl.ds(half * (1 - above), half)] = near_gate_ref[...]
+    hidden, slopes, total = half_rows(
+        above, own_ref, extra, corr_ref, rim, strip, bias_ref, head_ref, gate_ref, half * above
+    )
+    hidden = hidden + near_sums_ref[0:1]
+    slopes = slopes + near_sums_ref[1:2]
+    total = total + near_total_ref[...]
+    head = head_ref[...]
+    kout = head.shape[1]
     share = stage.shape[0] // parts
     stage[...] = jnp.zeros(stage.shape, F32)
-    for p in range(POS):
-        row, _ = spread(p)
-        table = spread_table(p, 0)
-        left = total[:, p * LANES : (p + 1) * LANES]
-        packed = None
-        for _ in range(3):
-            term = left.astype(BF16)
-            left = left - term.astype(F32)
-            part = nt(table, term)
-            packed = part if packed is None else packed + part
-        stage[row : row + table.shape[0]] += packed
     scale = 1.0 / pixels
-    stage[:STAT] = stage[:STAT] * scale
-    stage[STAT : STAT + 1] = head * slopes * scale
-    stage[STAT + 1 : STAT + 2] = hidden * scale
+    turned = jnp.transpose(total) * scale
+    for dy in range(SPAN):
+        put_rows(stage, share, dy * SPAN, turned[dy * WIN : dy * WIN + SPAN])
+    put_rows(stage, share, STAT, jnp.concatenate([head * slopes, hidden], axis=0) * scale)
     score = jnp.sum(hidden * head, axis=1, keepdims=True) * scale
     me = lax.axis_index("space")
     for k in range(parts):
         start = pl.multiple_of(partner(me, k, parts) * share, 8)
-        piece_refs[k][:share] = stage[pl.ds(start, share), :]
-        piece_refs[k][share:] = jnp.broadcast_to(score, (8, kout))
+        piece_refs[k][...] = stage[pl.ds(start, share), :]
+        piece_refs[k][share - 1 :] = jnp.broadcast_to(score, (1, kout))
 
 
 def back_chunks(gate_ref, wide_ref, r, rows, groups):
@@ -315,51 +343,29 @@
     lhs = jnp.concatenate([gate_ref[q * PER + r] for q in range(quarter)], axis=0)
     out = []
     for pos in range(POS):
-        grad = nn(lhs, wide_ref[r, :, pos * LANES : (pos + 1) * LANES])
+        grad = nn(lhs, wide_ref[r, :, (pos + 1) * LANES : (pos + 2) * LANES])
         grad = skew(grad.reshape(quarter * groups, GROUP, LANES), 0)
         out.append(grad.astype(BF16).reshape(quarter, groups, GROUP, LANES))
     return out
 
 
-def rim_kernel(gate_ref, wide_ref, source_ref, across_ref, beyond_ref, band_lo, band_hi, sums):
+def rim_kernel(kind, parts, gate_ref, wide_ref, source_ref, out_ref, band, sums):
     rows, groups, _, chan = source_ref.shape
     half = rows // 2
-    quarter = rows // PER
-    zero = jnp.zeros((groups, GROUP, LANES), BF16)
-    for r in range(PER):
-        for q in range(quarter):
-            y = q * PER + r
-            for c in (0, 1, 6, 7):
-                pos = c - q
-                band, row = (band_lo, y) if c < 2 else (band_hi, y - half)
-                if not 0 <= row < half:
-                    continue
-                at = (c if c < 2 else c - 6) * LANES
-                if 0 <= pos < POS:
-                    grad = nn(gate_ref[y], wide_ref[r, :, pos * LANES : (pos + 1) * LANES])
-                    part = skew(grad.reshape(groups, GROUP, LANES), 0).astype(BF16)
-                else:
-                    part = zero
-                band[row, :, :, at : at + LANES] = part
+    above, _ = edge_spot(parts, kind)
+    first = 0 if gate_ref.shape[0] == half else half * above
+    for i in range(half):
+        q, r = i // PER, i % PER
+        start = pl.multiple_of((1 - q) * LANES + above * 4 * LANES, LANES)
+        grad = nn(gate_ref[first + i], wide_ref[r, :, pl.ds(start, 2 * LANES)])
+        parts_of = skew_wide(grad.reshape(groups, GROUP, 2 * LANES), 0)
+        band[i] = jnp.concatenate(parts_of, axis=2).astype(BF16)
     sums[...] = jnp.zeros(sums.shape, F32)
-
-    def body(g, carry):
-        start = g * GROUP
-        for i, band in enumerate((band_lo, band_hi)):
-            lhs = band[:, g].reshape(half * GROUP, 2 * LANES)
-            rhs = source_ref[i * half : (i + 1) * half, g].reshape(half * GROUP, chan)
-            grad = tn(lhs, rhs).reshape(8, WIN, chan)
-            sums[8 * i : 8 * i + 8, start : start + WIN, :] += grad
-        return carry
-
     for g in range(groups):
-        body(g, 0)
-    cols = groups * GROUP
-    odd = lax.rem(lax.axis_index("space"), 2)
-    low = pl.multiple_of(8 * odd, 8)
-    high = pl.multiple_of(8 - 8 * odd, 8)
-    across_ref[...] = sums[pl.ds(high, 8), RADIUS : RADIUS + cols].astype(BF16)
-    beyond_ref[...] = sums[pl.ds(low, 8), RADIUS : RADIUS + cols].astype(BF16)
+        lhs = band[:, g].reshape(half * GROUP, 2 * LANES)
+        rhs = source_ref[pl.ds(half * above, half), g].reshape(half * GROUP, chan)
+        sums[:, g * GROUP : g * GROUP + WIN, :] += tn(lhs, rhs).reshape(8, WIN, chan)
+    out_ref[...] = sums[:, RADIUS : RADIUS + groups * GROUP].astype(BF16)
 
 
 def back_kernel(
@@ -432,7 +438,7 @@
     for k in range(pairs):
         pid = partner(me, -k, pairs)
         hot = (first == pid).astype(F32) - (second == pid).astype(F32)
-        score = piece_refs[k][share : share + 1, 0:1]
+        score = piece_refs[k][share - 1 : share, 0:1]
         margin = margin + hot * score
         hots.append(hot)
     sign = 2.0 * win.astype(F32) - 1.0
@@ -444,7 +450,7 @@
         grad = jnp.sum(margin_grad * hots[k], axis=1, keepdims=True)
         if k == 0:
             grad_ref[...] = jnp.broadcast_to(grad, grad_ref.shape)
-        total = total + grad * piece_refs[k][:share]
+        total = total + grad * piece_refs[k][...]
     total_ref[...] = total
 
 
@@ -457,9 +463,14 @@
     for k in range(parts):
         start = pl.multiple_of(partner(me, -k, parts) * share, 8)
         stage[pl.ds(start, share), :] = piece_refs[k][...]
-    conv_ref[...] = stage[: conv_ref.shape[0]]
-    bias_ref[...] = stage[STAT : STAT + 1]
-    head_ref[...] = stage[STAT + 1 : STAT + 2]
+    rows = conv_ref.shape[0]
+    for piece in range(-(-rows // (share - 1))):
+        row = piece * (share - 1)
+        count = min(share - 1, rows - row)
+        conv_ref[row : row + count] = stage[piece * share : piece * share + count]
+    for i, ref in enumerate((bias_ref, head_ref)):
+        piece, at = divmod(STAT + i, share - 1)
+        ref[...] = stage[piece * share + at : piece * share + at + 1]
 
 
 def finish_kernel(
@@ -536,6 +547,10 @@
     return table
 
 
+def swap(array, axis, bit):
+    return lax.ppermute(array, axis, [(i, i ^ bit) for i in range(lax.axis_size(axis))])
+
+
 def local(
     source_feats, edit_feats, conv_weight, conv_bias, head_weight, comp_first, comp_second, comp_win
 ):
@@ -544,9 +559,12 @@
     inv_root = chan ** (-0.5)
     space, pairs = lax.axis_size("space"), lax.axis_size("pair")
     pixels = rows * space * columns
+    assert space & (space - 1) == 0
     groups = columns // GROUP
     wide_cols = columns + 2 * RADIUS
-    share = -(-(disp + 2) // (8 * space)) * 8
+    share = 8
+    while (share - 1) * space < disp + 2:
+        share += 8
     edit = edit_feats[0]
     source = source_feats.reshape(rows, groups, GROUP, chan)
     to_across = [(i, i ^ 1 if i ^ 1 < space else i) for i in range(space)]
@@ -563,71 +581,99 @@
     beyond = lax.ppermute(beyond, ("groups", "space"), to_beyond)
     near = (rows, groups, GROUP, chan)
     rim_shape = (rows // 2, groups, GROUP, 8 * WIN)
-    held, own_pad, turned, corr, wide, tall, own = call(
-        functools.partial(inner_kernel, inv_root),
+    held, own_pad, turned, wide, tall = call(
+        load_kernel,
         (
             shape(near, BF16),
             shape((rows, wide_cols, chan), BF16),
             shape(near, BF16),
-            shape((rows, groups, GROUP, rows * WIN), BF16),
-            shape((PER, kout, POS * LANES), BF16),
+            shape((PER, kout, (POS + 2) * LANES), BF16),
             shape((PER, (POS + 2) * LANES, kout), BF16),
-            shape((rows, columns, kout)),
         ),
         [pltpu.VMEM((disp, kout), BF16), pltpu.SemaphoreType.DMA((3,))],
-        2 * 10**9,
+        10**4,
         source,
         edit,
         conv_weight.T,
         far=(0, 1, 2),
     )
-    rim, extra = call(
+    corr, own = call(
+        functools.partial(inner_kernel, inv_root),
+        (shape((rows, groups, GROUP, rows * WIN), BF16), shape((rows, columns, kout))),
+        [],
+        2 * 10**9,
+        turned,
+        own_pad,
+        tall,
+    )
+    work = [
+        pltpu.VMEM((RADIUS, wide_cols, chan), BF16),
+        pltpu.VMEM(rim_shape, BF16),
+        pltpu.VMEM((rows // 2, columns, kout), F32),
+        pltpu.VMEM((rows // 2, groups, GROUP, (rows + RADIUS) * WIN), BF16),
+    ]
+    near_gate, near_sums, near_total = call(
         functools.partial(across_kernel, inv_root, space),
-        (shape(rim_shape, BF16), shape((rows // 2, columns, kout))),
-        [pltpu.VMEM((RADIUS, wide_cols, chan), BF16)],
+        (
+            shape((rows // 2, columns, kout), BF16),
+            shape((2, kout)),
+            shape((kout, POS * LANES)),
+        ),
+        work,
         10**9,
         turned,
+        corr,
+        own,
         across,
         tall,
-    )
+        conv_bias[None],
+        head_weight[None],
+    )
+
+    def rim_terms(kind, gates):
+        (terms,) = call(
+            functools.partial(rim_kernel, kind, space),
+            (shape((RADIUS, columns, chan), BF16),),
+            [pltpu.VMEM(rim_shape, BF16), pltpu.VMEM((RADIUS, wide_cols, chan), F32)],
+            10**9,
+            gates,
+            wide,
+            held,
+        )
+        return terms
+
+    terms, far = lax.optimization_barrier((rim_terms(0, near_gate), beyond))
+    from_across = lax.ppermute(terms, "space", to_across)
     gate, *pieces = call(
         functools.partial(outer_kernel, inv_root, pixels, space),
-        (shape((rows, columns, kout), BF16),) + (shape((share + 8, kout)),) * space,
-        [
-            pltpu.VMEM((RADIUS, wide_cols, chan), BF16),
-            pltpu.VMEM((2,) + rim_shape, BF16),
-            pltpu.VMEM((2, rows // 2, columns, kout), F32),
-            pltpu.VMEM((share * space, kout), F32),
-        ],
+        (shape((rows, columns, kout), BF16),) + (shape((share, kout)),) * space,
+        work + [pltpu.VMEM((share * space, kout), F32)],
         2 * 10**9,
         turned,
         corr,
-        rim,
-        extra,
         own,
-        beyond,
+        far,
         tall,
         conv_bias[None],
         head_weight[None],
-    )
+        near_gate,
+        near_sums,
+        near_total,
+    )
+    crossings = range(2, space, 2)
+    far_terms = rim_terms(1, gate)
+    came = {k: swap(pieces[k + 1], "space", 1) for k in (*crossings, 0) if k + 1 < space}
+    paired = dict(enumerate(pieces))
+    if crossings:
+        used = [came[k] for k in crossings]
+        far_terms, *used = lax.optimization_barrier((far_terms, *used))
+        for k, other in zip(crossings, used):
+            paired[k] = pieces[k] + other
+    crossed = [swap(paired[k], "space", k) for k in crossings]
+    from_beyond = lax.ppermute(far_terms, ("groups", "space"), to_beyond)
     quarter = pieces[0]
-    for k in range(1, space):
-        quarter = quarter + lax.ppermute(pieces[k], "space", around("space", k))
-    rim_across, rim_beyond = call(
-        rim_kernel,
-        (shape((RADIUS, columns, chan), BF16),) * 2,
-        [
-            pltpu.VMEM((rows // 2, groups, GROUP, 8 * WIN), BF16),
-            pltpu.VMEM((rows // 2, groups, GROUP, 8 * WIN), BF16),
-            pltpu.VMEM((2 * RADIUS, wide_cols, chan), F32),
-        ],
-        10**9,
-        gate,
-        wide,
-        held,
-    )
-    from_across = lax.ppermute(rim_across, "space", to_across)
-    from_beyond = lax.ppermute(rim_beyond, ("groups", "space"), to_beyond)
+    for other in (*(came[k] for k in (0,) if space > 1), *crossed):
+        quarter = quarter + other
     source_sum, edit_sum = call(
         functools.partial(back_kernel, space),
         (shape((rows, groups, GROUP, chan)), shape((rows, columns, chan))),
@@ -656,7 +702,11 @@
         comp_win[None],
         *others,
     )
-    gathered = [total] + [lax.ppermute(total, "space", around("space", k)) for k in range(1, space)]
+    gathered = {0: total}
+    for k in crossings:
+        gathered[k] = swap(total, "space", k)
+    if space > 1:
+        gathered[1] = swap(total, "space", 1)
     source_grad, edit_grad = call(
         functools.partial(finish_kernel, inv_root, space),
         (result((rows, columns, chan), BF16),) * 2,
@@ -673,7 +723,12 @@
         from_beyond,
         far_out=True,
     )
-    *gathered, source_grad, edit_grad = lax.optimization_barrier((*gathered, source_grad, edit_grad))
+    if crossings:
+        used = [gathered[k] for k in crossings]
+        source_grad, edit_grad, *used = lax.optimization_barrier((source_grad, edit_grad, *used))
+        for k, other in zip(crossings, used):
+            gathered[k], gathered[k + 1] = other, swap(other, "space", 1)
+    gathered = [gathered[k] for k in range(space)]
     conv_grad, bias_grad, head_grad, loss = call(
         functools.partial(gather_kernel, space),
         (result((disp, kout)), result((1, kout)), result((1, kout)), result((1, LANES))),

time: 34.6 us -> 34.9 us (level)
  waiting for transfers between devices: 4.16 us -> 6.23 us
  starting transfers between devices: 13.9 us -> 12.6 us
  Pallas kernels: 15.6 us -> 15.1 us
    ppermute x8, waiting for transfers between devices: 0.84 us -> 3.71 us  [the longest x6 3.71 us: swap(): lax.ppermute(array, axis, [(i, i ^ bit) for i in range(lax.axis_size(axis...]
    ppermute x8, starting transfers between devices: 6.35 us -> 4.63 us  [the longest x6 3.11 us: swap(): lax.ppermute(array, axis, [(i, i ^ bit) for i in range(lax.axis_size(axis...]
    ppermute x1, waiting for transfers between devices: 2.14 us -> 1.31 us  [local(): beyond = lax.ppermute(beyond, ('groups', 'space'), to_beyond)]
    pallas_call x9 -> x11, Pallas kernels: 15.6 us -> 15.1 us  [call(): pl.pallas_call(kernel, out_shape=outs, in_specs=[pl.BlockSpec(memory_spac...]
    ppermute x3, starting transfers between devices: 4.45 us -> 4.84 us  [local(): lax.ppermute(quarter, 'pair', around('pair', k))]
  transfers between devices with their start and end apart: 13 -> 13, of which waited for: 3 -> 6; matrix products, arithmetic and copies ran while one was open for 0% -> 0% of each run, Pallas kernels for 33% -> 33%
where the time goes in v7:
time: 34.9 us; the launch traced here: 34.7 us
  Pallas kernels  15.1 us (43%)
  starting transfers between devices  12.6 us (36%)
  waiting for transfers between devices  6.23 us (18%)
  between operations  0.8 us (2%)
    pallas_call x11, Pallas kernels, call(): pl.pallas_call(kernel, out_shape=outs, in_specs=[pl.BlockSpec(memory_spac...  15.1 us
    ppermute x3, starting transfers between devices, local(): lax.ppermute(quarter, 'pair', around('pair', k))  4.84 us
    ppermute x6, waiting for transfers between devices, swap(): lax.ppermute(array, axis, [(i, i ^ bit) for i in range(lax.axis_size(axis...  3.71 us
    ppermute x6, starting transfers between devices, swap(): lax.ppermute(array, axis, [(i, i ^ bit) for i in range(lax.axis_size(axis...  3.11 us
    ppermute x1, starting transfers between devices, local(): beyond = lax.ppermute(beyond, ('groups', 'space'), to_beyond)  2.56 us
    ppermute x1, starting transfers between devices, local(): from_beyond = lax.ppermute(far_terms, ('groups', 'space'), to_beyond)  1.49 us
    ppermute x1, waiting for transfers between devices, local(): beyond = lax.ppermute(beyond, ('groups', 'space'), to_beyond)  1.31 us
    ppermute x3, waiting for transfers between devices, local(): lax.ppermute(quarter, 'pair', around('pair', k))  1.21 us
  transfers between devices with their start and end apart: 13, of which 6 were waited for; matrix products, arithmetic and copies ran while one was open for 0% of the time, Pallas kernels for 33%

profile of v7, /device:TPU:0, one launch (start us, length us, event | category | flops | bytes accessed | tf_op | source)
XLA Modules:
  0.0 34.7 jit_solution(11793951494252577563)
XLA Ops:
  0.6 1.2 %shard_map.129 = (bf16[8,128,256]{2,1,0:T(8,128)(2,1)S(1)}, bf16[8,128,256]{2,1,0:T(8,128)(2,1)S(1)}) custom-call(bf16[16,128,256]{2,1,0:T(8,128)(2,1)} %bitcast.24), custom_call_target="tpu_custom_call" | custom-call | flops 10000 | bytes 1048576 | tf_op jit(solution)/shard_map/pallas_call | solution.py:516
  1.9 0.5 %collective-permute-start = (bf16[8,128,256]{2,1,0:T(8,128)(2,1)S(1)}, bf16[8,128,256]{2,1,0:T(8,128)(2,1)S(1)}, u32[]{:S(2)}, u32[]{:S(2)}) collective-permute-start(bf16[8,128,256]{2,1,0:T(8,128)(2,1)S(1)} %get-tuple-element.52), channel_id=1, source_target_pairs={{0,4},{4,0},{8,12},{12,8},{1,5},{5,1},{9,13},{13,9},{2,6},{6,2},{1... | collective-permute-start | bytes 1572872 | tf_op jit(solution)/shard_map/ppermute | solution.py:580
  2.4 2.6 %collective-permute-start.1 = (bf16[8,128,256]{2,1,0:T(8,128)(2,1)S(1)}, bf16[8,128,256]{2,1,0:T(8,128)(2,1)S(1)}, u32[]{:S(2)}, u32[]{:S(2)}) collective-permute-start(bf16[8,128,256]{2,1,0:T(8,128)(2,1)S(1)} %get-tuple-element.56), channel_id=1, source_target_pairs={{0,16},{4,8},{8,4},{12,28},{16,0},{20,24},{24,20},{28,12},{1,17},{... | collective-permute-start | bytes 1572872 | tf_op jit(solution)/shard_map/ppermute | solution.py:581
  5.0 1.8 %shard_map.127 = (bf16[16,8,16,256]{3,2,1,0:T(8,128)(2,1)S(1)}, bf16[16,144,256]{2,1,0:T(8,128)(2,1)S(1)}, bf16[16,8,16,256]{3,2,1,0:T(8,128)(2,1)S(1)}, bf16[4,...) custom-call(bf16[16,8,16,256]{3,2,1,0:T(8,128)(2,1)} %bitcast.26, bf16[16,128,256]{2,1,0:T(8,128)(2,1)} %bitcast.25, ...), custom_call_target="tpu_custom_call" | custom-call | flops 10000 | bytes 2171136 | tf_op jit(solution)/shard_map/pallas_call | solution.py:516
  6.8 1.5 %shard_map.128 = (bf16[16,8,16,512]{3,2,1,0:T(8,128)(2,1)S(1)}, f32[16,128,128]{2,1,0:T(8,128)S(1)}) custom-call(bf16[16,8,16,256]{3,2,1,0:T(8,128)(2,1)S(1)} %get-tuple-element.47.turned_ref, bf16[16,144,256]{2,1,0:T(8,128)(2,1)S(1)} %get-tuple-element.48.pad.own_pad, bf16[4,896,128]{2,1,0:T(8,128)(2,1)S(1)} %get-tuple-element.49.tall_ref), custom_call_target="tpu_custom_call" | custom-call | flops 2000000000 | bytes 3145728 | tf_op jit(solution)/shard_map/pallas_call | solution.py:516
  8.3 1.7 %shard_map.130 = (bf16[8,128,128]{2,1,0:T(8,128)(2,1)S(1)}, f32[2,128]{1,0:T(2,128)S(1)}, f32[128,640]{1,0:T(8,128)S(1)}) custom-call(bf16[16,8,16,256]{3,2,1,0:T(8,128)(2,1)S(1)} %get-tuple-element.47.turned_ref, bf16[16,8,16,512]{3,2,1,0:T(8,128)(2,1)S(1)} %get-tuple-element.50.corr_ref, f32[16,128,128]{2,1,0:T(8,128)S(1)} %get-tuple-element.51.own_ref, ...), custom_call_target="tpu_custom_call" | custom-call | flops 1000000000 | bytes 5637120 | tf_op jit(solution)/shard_map/pallas_call | solution.py:516
  10.0 0.8 %shard_map.131 = bf16[8,128,256]{2,1,0:T(8,128)(2,1)S(1)} custom-call(bf16[8,128,128]{2,1,0:T(8,128)(2,1)S(1)} %get-tuple-element.53.gate_ref.near_gate_ref, bf16[4,128,896]{2,1,0:T(8,128)(2,1)S(1)} %get-tuple-element.54.wide_ref, bf16[16,8,16,256]{3,2,1,0:T(8,128)(2,1)S(1)} %get-tuple-element.55.source_ref), custom_call_target="tpu_custom_call" | custom-call | flops 1000000000 | bytes 2228224 | tf_op jit(solution)/shard_map/pallas_call | solution.py:516
  10.8 1.3 %collective-permute-done.1.halo_ref.beyond_ref = bf16[8,128,256]{2,1,0:T(8,128)(2,1)S(1)} collective-permute-done((bf16[8,128,256]{2,1,0:T(8,128)(2,1)S(1)}, bf16[8,128,256]{2,1,0:T(8,128)(2,1)S(1)}, u32[]{:S(2)}, u32[]{:S(2)}) %collective-permute-start.1) | collective-permute-done | bytes 524320 | tf_op jit(solution)/shard_map/ppermute | solution.py:581
  12.1 1.8 %shard_map.132 = (bf16[16,128,128]{2,1,0:T(8,128)(2,1)S(1)}, f32[80,128]{1,0:T(8,128)S(1)}, f32[80,128]{1,0:T(8,128)S(1)}, f32[80,128]{1,0:T(8,128)S(1)}, f32[80,128]{1,0:T(8,128)S(1)}) custom-call(bf16[16,8,16,256]{3,2,1,0:T(8,128)(2,1)S(1)} %get-tuple-element.47.turned_ref, bf16[16,8,16,512]{3,2,1,0:T(8,128)(2,1)S(1)} %get-tuple-element.50.corr_ref, ...), custom_call_target="tpu_custom_call" | custom-call | flops 2000000000 | bytes 6227968 | tf_op jit(solution)/shard_map/pallas_call | solution.py:516
  13.9 0.2 collective-permute-start.2
  14.1 0.4 %collective-permute-start.3 = (f32[80,128]{1,0:T(8,128)S(1)}, f32[80,128]{1,0:T(8,128)S(1)}, u32[]{:S(2)}, u32[]{:S(2)}) collective-permute-start(f32[80,128]{1,0:T(8,128)S(1)} %get-tuple-element.64), channel_id=1, source_target_pairs={{0,4},{4,0},{8,12},{12,8},{1,5},{5,1},{9,13},{13,9},{2,6},{6,2},{1... | collective-permute-start | bytes 122888 | tf_op jit(solution)/shard_map/ppermute | solution.py:551
  14.5 0.8 %shard_map.133 = bf16[8,128,256]{2,1,0:T(8,128)(2,1)S(1)} custom-call(bf16[16,128,128]{2,1,0:T(8,128)(2,1)S(1)} %get-tuple-element.63.gate_ref, bf16[4,128,896]{2,1,0:T(8,128)(2,1)S(1)} %get-tuple-element.54.wide_ref, bf16[16,8,16,256]{3,2,1,0:T(8,128)(2,1)S(1)} %get-tuple-element.55.source_ref), custom_call_target="tpu_custom_call" | custom-call | flops 1000000000 | bytes 2490368 | tf_op jit(solution)/shard_map/pallas_call | solution.py:516
  15.4 1.5 %collective-permute-start.4 = (f32[80,128]{1,0:T(8,128)S(1)}, f32[80,128]{1,0:T(8,128)S(1)}, u32[]{:S(2)}, u32[]{:S(2)}) collective-permute-start(f32[80,128]{1,0:T(8,128)S(1)} %add.10), channel_id=1, source_target_pairs={{0,8},{4,12},{8,0},{12,4},{1,9},{5,13},{9,1},{13,5},{2,10},{6,14},... | collective-permute-start | bytes 122888 | tf_op jit(solution)/shard_map/ppermute | solution.py:551
  16.9 1.5 %collective-permute-start.9 = (bf16[8,128,256]{2,1,0:T(8,128)(2,1)S(1)}, bf16[8,128,256]{2,1,0:T(8,128)(2,1)S(1)}, u32[]{:S(2)}, u32[]{:S(2)}) collective-permute-start(bf16[8,128,256]{2,1,0:T(8,128)(2,1)S(1)} %shard_map.133), channel_id=1, source_target_pairs={{0,16},{4,8},{8,4},{12,28},{16,0},{20,24},{24,20},{28,12},{1,17},{... | collective-permute-start | bytes 1572872 | tf_op jit(solution)/shard_map/ppermute | solution.py:673
  18.4 1.0 %collective-permute-done.4 = f32[80,128]{1,0:T(8,128)S(1)} collective-permute-done((f32[80,128]{1,0:T(8,128)S(1)}, f32[80,128]{1,0:T(8,128)S(1)}, u32[]{:S(2)}, u32[]{:S(2)}) %collective-permute-start.4) | collective-permute-done | bytes 40992 | tf_op jit(solution)/shard_map/ppermute | solution.py:551
  19.4 4.2 %collective-permute-start.7 = (f32[80,128]{1,0:T(8,128)S(1)}, f32[80,128]{1,0:T(8,128)S(1)}, u32[]{:S(2)}, u32[]{:S(2)}) collective-permute-start(f32[80,128]{1,0:T(8,128)S(1)} %add_add_fusion.rest_0_), channel_id=1, source_target_pairs={{0,3},{1,2},{2,1},{3,0},{4,7},{5,6},{6,5},{7,4},{8,11},{9,10},{10,... | collective-permute-start | bytes 122888 | tf_op jit(solution)/shard_map/ppermute | solution.py:693
  23.7 0.6 %collective-permute-start.5 = (f32[80,128]{1,0:T(8,128)S(1)}, f32[80,128]{1,0:T(8,128)S(1)}, u32[]{:S(2)}, u32[]{:S(2)}) collective-permute-start(f32[80,128]{1,0:T(8,128)S(1)} %add_add_fusion.rest_0_), channel_id=1, source_target_pairs={{0,1},{1,0},{2,3},{3,2},{4,5},{5,4},{6,7},{7,6},{8,9},{9,8},{10,11... | collective-permute-start | bytes 122888 | tf_op jit(solution)/shard_map/ppermute | solution.py:693
  24.3 3.0 %shard_map.134 = (f32[16,8,16,256]{3,2,1,0:T(8,128)S(1)}, f32[16,128,256]{2,1,0:T(8,128)S(1)}) custom-call(bf16[16,128,128]{2,1,0:T(8,128)(2,1)S(1)} %get-tuple-element.63.gate_ref, bf16[4,128,896]{2,1,0:T(8,128)(2,1)S(1)} %get-tuple-element.54.wide_ref, bf16[16,8,16,256]{3,2,1,0:T(8,128)(2,1)S(1)} %get-tuple-element.55.source_ref, ...), custom_call_target="tpu_custom_call" | custom-call | flops 4000000000 | bytes 4718592 | tf_op jit(solution)/shard_map/pallas_call | solution.py:516
  27.3 1.2 %collective-permute-done.6.rest_2_ = f32[80,128]{1,0:T(8,128)S(1)} collective-permute-done((f32[80,128]{1,0:T(8,128)S(1)}, f32[80,128]{1,0:T(8,128)S(1)}, u32[]{:S(2)}, u32[]{:S(2)}) %collective-permute-start.6) | collective-permute-done | bytes 40992 | tf_op jit(solution)/shard_map/ppermute | solution.py:693
  28.8 1.0 %collective-permute-start.10 = (f32[80,128]{1,0:T(8,128)S(1)}, f32[80,128]{1,0:T(8,128)S(1)}, u32[]{:S(2)}, u32[]{:S(2)}) collective-permute-start(f32[80,128]{1,0:T(8,128)S(1)} %get-tuple-element.79.rest_0_), channel_id=1, source_target_pairs={{0,8},{4,12},{8,0},{12,4},{1,9},{5,13},{9,1},{13,5},{2,10},{6,14},... | collective-permute-start | bytes 122888 | tf_op jit(solution)/shard_map/ppermute | solution.py:551
  29.8 1.6 %shard_map.136 = (bf16[16,128,256]{2,1,0:T(8,128)(2,1)}, bf16[16,128,256]{2,1,0:T(8,128)(2,1)}) custom-call(f32[8,128]{1,0:T(8,128)S(1)} %get-tuple-element.72.grad_ref, f32[16,128,256]{2,1,0:T(8,128)S(1)} %bitcast.16, f32[16,128,256]{2,1,0:T(8,128)S(1)} %get-tuple-element.74.edit_ref, bf16[8,128,256]{2,1,0:T(8,128)(2,1)S(1)} %collective-permute-done.8.across_ref, ...), custom_call_target="tpu_custom_call" | custom-call | flops 10000000 | bytes 5246976 | tf_op jit(solution)/shard_map/pallas_call | solution.py:516
  31.4 1.4 %collective-permute-done.10.rest_2_ = f32[80,128]{1,0:T(8,128)S(1)} collective-permute-done((f32[80,128]{1,0:T(8,128)S(1)}, f32[80,128]{1,0:T(8,128)S(1)}, u32[]{:S(2)}, u32[]{:S(2)}) %collective-permute-start.10) | collective-permute-done | bytes 40992 | tf_op jit(solution)/shard_map/ppermute | solution.py:551
  32.8 1.2 %collective-permute-done.12.rest_3_ = f32[80,128]{1,0:T(8,128)S(1)} collective-permute-done((f32[80,128]{1,0:T(8,128)S(1)}, f32[80,128]{1,0:T(8,128)S(1)}, u32[]{:S(2)}, u32[]{:S(2)}) %collective-permute-start.12) | collective-permute-done | bytes 40992 | tf_op jit(solution)/shard_map/ppermute | solution.py:551
  34.0 0.7 %shard_map.137 = (f32[289,128]{1,0:T(8,128)}, f32[1,128]{1,0:T(1,128)}, f32[1,128]{1,0:T(1,128)}, f32[1,128]{1,0:T(1,128)}) custom-call(f32[80,128]{1,0:T(8,128)S(1)} %get-tuple-element.79.rest_0_, f32[80,128]{1,0:T(8,128)S(1)} %collective-permute-done.11.rest_1_, f32[80,128]{1,0:T(8,128)S(1)} %collective-permute-done.10.rest_2_, ...), custom_call_target="tpu_custom_call" | custom-call | flops 1000000 | bytes 164352 | tf_op jit(solution)/shard_map/pallas_call | solution.py:516
  (25 shorter events, 0.3 us)
Async XLA Ops:
  1.9 6.4 %collective-permute-start = (bf16[8,128,256]{2,1,0:T(8,128)(2,1)S(1)}, bf16[8,128,256]{2,1,0:T(8,128)(2,1)S(1)}, u32[]{:S(2)}, u32[]{:S(2)}) collective-permute-start(bf16[8,128,256]{2,1,0:T(8,128)(2,1)S(1)} %get-tuple-element.52), channel_id=1, source_target_pairs={{0,4},{4,0},{8,12},{12,8},{1,5},{5,1},{9,13},{13,9},{2,6},{6,2},{1... | collective-permute-start | bytes 1572872 | tf_op jit(solution)/shard_map/ppermute | solution.py:580
  2.4 9.7 %collective-permute-start.1 = (bf16[8,128,256]{2,1,0:T(8,128)(2,1)S(1)}, bf16[8,128,256]{2,1,0:T(8,128)(2,1)S(1)}, u32[]{:S(2)}, u32[]{:S(2)}) collective-permute-start(bf16[8,128,256]{2,1,0:T(8,128)(2,1)S(1)} %get-tuple-element.56), channel_id=1, source_target_pairs={{0,16},{4,8},{8,4},{12,28},{16,0},{20,24},{24,20},{28,12},{1,17},{... | collective-permute-start | bytes 1572872 | tf_op jit(solution)/shard_map/ppermute | solution.py:581
  6.8 1.5 %copy-start = (f32[128]{0:T(128)S(1)}, f32[128]{0:T(128)}, u32[]{:S(2)}) copy-start(f32[128]{0:T(128)} %param.11) | copy-start | bytes 1540
  6.8 1.5 %copy-start.1 = (f32[128]{0:T(128)S(1)}, f32[128]{0:T(128)}, u32[]{:S(2)}) copy-start(f32[128]{0:T(128)} %param.12) | copy-start | bytes 1540
  13.9 4.5 %collective-permute-start.2 = (f32[80,128]{1,0:T(8,128)S(1)}, f32[80,128]{1,0:T(8,128)S(1)}, u32[]{:S(2)}, u32[]{:S(2)}) collective-permute-start(f32[80,128]{1,0:T(8,128)S(1)} %get-tuple-element.61), channel_id=1, source_target_pairs={{0,4},{4,0},{8,12},{12,8},{1,5},{5,1},{9,13},{13,9},{2,6},{6,2},{1... | collective-permute-start | bytes 122888 | tf_op jit(solution)/shard_map/ppermute | solution.py:551
  14.1 1.2 %collective-permute-start.3 = (f32[80,128]{1,0:T(8,128)S(1)}, f32[80,128]{1,0:T(8,128)S(1)}, u32[]{:S(2)}, u32[]{:S(2)}) collective-permute-start(f32[80,128]{1,0:T(8,128)S(1)} %get-tuple-element.64), channel_id=1, source_target_pairs={{0,4},{4,0},{8,12},{12,8},{1,5},{5,1},{9,13},{13,9},{2,6},{6,2},{1... | collective-permute-start | bytes 122888 | tf_op jit(solution)/shard_map/ppermute | solution.py:551
  15.4 4.0 %collective-permute-start.4 = (f32[80,128]{1,0:T(8,128)S(1)}, f32[80,128]{1,0:T(8,128)S(1)}, u32[]{:S(2)}, u32[]{:S(2)}) collective-permute-start(f32[80,128]{1,0:T(8,128)S(1)} %add.10), channel_id=1, source_target_pairs={{0,8},{4,12},{8,0},{12,4},{1,9},{5,13},{9,1},{13,5},{2,10},{6,14},... | collective-permute-start | bytes 122888 | tf_op jit(solution)/shard_map/ppermute | solution.py:551
  16.9 12.9 %collective-permute-start.8 = (bf16[8,128,256]{2,1,0:T(8,128)(2,1)S(1)}, bf16[8,128,256]{2,1,0:T(8,128)(2,1)S(1)}, u32[]{:S(2)}, u32[]{:S(2)}) collective-permute-start(bf16[8,128,256]{2,1,0:T(8,128)(2,1)S(1)} %shard_map.131), channel_id=1, source_target_pairs={{0,4},{4,0},{8,12},{12,8},{1,5},{5,1},{9,13},{13,9},{2,6},{6,2},{1... | collective-permute-start | bytes 1572872 | tf_op jit(solution)/shard_map/ppermute | solution.py:646
  16.9 12.9 %collective-permute-start.9 = (bf16[8,128,256]{2,1,0:T(8,128)(2,1)S(1)}, bf16[8,128,256]{2,1,0:T(8,128)(2,1)S(1)}, u32[]{:S(2)}, u32[]{:S(2)}) collective-permute-start(bf16[8,128,256]{2,1,0:T(8,128)(2,1)S(1)} %shard_map.133), channel_id=1, source_target_pairs={{0,16},{4,8},{8,4},{12,28},{16,0},{20,24},{24,20},{28,12},{1,17},{... | collective-permute-start | bytes 1572872 | tf_op jit(solution)/shard_map/ppermute | solution.py:673
  19.4 9.1 %copy-start.2 = (s32[16]{0:T(128)S(1)}, s32[16]{0:T(128)}, u32[]{:S(2)}) copy-start(s32[16]{0:T(128)} %param.13) | copy-start | bytes 196
  19.4 9.1 %copy-start.3 = (s32[16]{0:T(128)S(1)}, s32[16]{0:T(128)}, u32[]{:S(2)}) copy-start(s32[16]{0:T(128)} %param.14) | copy-start | bytes 196
  19.4 9.1 %copy-start.4 = (s32[16]{0:T(128)S(1)}, s32[16]{0:T(128)}, u32[]{:S(2)}) copy-start(s32[16]{0:T(128)} %param.15) | copy-start | bytes 196
  19.4 7.9 %collective-permute-start.7 = (f32[80,128]{1,0:T(8,128)S(1)}, f32[80,128]{1,0:T(8,128)S(1)}, u32[]{:S(2)}, u32[]{:S(2)}) collective-permute-start(f32[80,128]{1,0:T(8,128)S(1)} %add_add_fusion.rest_0_), channel_id=1, source_target_pairs={{0,3},{1,2},{2,1},{3,0},{4,7},{5,6},{6,5},{7,4},{8,11},{9,10},{10,... | collective-permute-start | bytes 122888 | tf_op jit(solution)/shard_map/ppermute | solution.py:693
  23.6 4.9 %collective-permute-start.6 = (f32[80,128]{1,0:T(8,128)S(1)}, f32[80,128]{1,0:T(8,128)S(1)}, u32[]{:S(2)}, u32[]{:S(2)}) collective-permute-start(f32[80,128]{1,0:T(8,128)S(1)} %add_add_fusion.rest_0_), channel_id=1, source_target_pairs={{0,2},{1,3},{2,0},{3,1},{4,6},{5,7},{6,4},{7,5},{8,10},{9,11},{10,... | collective-permute-start | bytes 122888 | tf_op jit(solution)/shard_map/ppermute | solution.py:693
  23.7 4.9 %collective-permute-start.5 = (f32[80,128]{1,0:T(8,128)S(1)}, f32[80,128]{1,0:T(8,128)S(1)}, u32[]{:S(2)}, u32[]{:S(2)}) collective-permute-start(f32[80,128]{1,0:T(8,128)S(1)} %add_add_fusion.rest_0_), channel_id=1, source_target_pairs={{0,1},{1,0},{2,3},{3,2},{4,5},{5,4},{6,7},{7,6},{8,9},{9,8},{10,11... | collective-permute-start | bytes 122888 | tf_op jit(solution)/shard_map/ppermute | solution.py:693
  28.8 4.1 %collective-permute-start.10 = (f32[80,128]{1,0:T(8,128)S(1)}, f32[80,128]{1,0:T(8,128)S(1)}, u32[]{:S(2)}, u32[]{:S(2)}) collective-permute-start(f32[80,128]{1,0:T(8,128)S(1)} %get-tuple-element.79.rest_0_), channel_id=1, source_target_pairs={{0,8},{4,12},{8,0},{12,4},{1,9},{5,13},{9,1},{13,5},{2,10},{6,14},... | collective-permute-start | bytes 122888 | tf_op jit(solution)/shard_map/ppermute | solution.py:551
  29.8 3.1 %collective-permute-start.11 = (f32[80,128]{1,0:T(8,128)S(1)}, f32[80,128]{1,0:T(8,128)S(1)}, u32[]{:S(2)}, u32[]{:S(2)}) collective-permute-start(f32[80,128]{1,0:T(8,128)S(1)} %get-tuple-element.79.rest_0_), channel_id=1, source_target_pairs={{0,4},{4,0},{8,12},{12,8},{1,5},{5,1},{9,13},{13,9},{2,6},{6,2},{1... | collective-permute-start | bytes 122888 | tf_op jit(solution)/shard_map/ppermute | solution.py:551
  32.8 1.2 %collective-permute-start.12 = (f32[80,128]{1,0:T(8,128)S(1)}, f32[80,128]{1,0:T(8,128)S(1)}, u32[]{:S(2)}, u32[]{:S(2)}) collective-permute-start(f32[80,128]{1,0:T(8,128)S(1)} %collective-permute-done.10.rest_2_), channel_id=1, source_target_pairs={{0,4},{4,0},{8,12},{12,8},{1,5},{5,1},{9,13},{13,9},{2,6},{6,2},{1... | collective-permute-start | bytes 122888 | tf_op jit(solution)/shard_map/ppermute | solution.py:551

commit v8 on v7

--- a/solution.py
+++ b/solution.py
@@ -451,7 +451,7 @@
         if k == 0:
             grad_ref[...] = jnp.broadcast_to(grad, grad_ref.shape)
         total = total + grad * piece_refs[k][...]
-    total_ref[...] = total
+    total_ref[...] = total.astype(total_ref.dtype)
 
 
 def gather_kernel(parts, *rest):
@@ -462,7 +462,7 @@
     me = lax.axis_index("space")
     for k in range(parts):
         start = pl.multiple_of(partner(me, -k, parts) * share, 8)
-        stage[pl.ds(start, share), :] = piece_refs[k][...]
+        stage[pl.ds(start, share), :] = piece_refs[k][...].astype(F32)
     rows = conv_ref.shape[0]
     for piece in range(-(-rows // (share - 1))):
         row = piece * (share - 1)
@@ -547,10 +547,6 @@
     return table
 
 
-def swap(array, axis, bit):
-    return lax.ppermute(array, axis, [(i, i ^ bit) for i in range(lax.axis_size(axis))])
-
-
 def local(
     source_feats, edit_feats, conv_weight, conv_bias, head_weight, comp_first, comp_second, comp_win
 ):
@@ -559,7 +555,6 @@
     inv_root = chan ** (-0.5)
     space, pairs = lax.axis_size("space"), lax.axis_size("pair")
     pixels = rows * space * columns
-    assert space & (space - 1) == 0
     groups = columns // GROUP
     wide_cols = columns + 2 * RADIUS
     share = 8
@@ -660,20 +655,10 @@
         near_sums,
         near_total,
     )
-    crossings = range(2, space, 2)
-    far_terms = rim_terms(1, gate)
-    came = {k: swap(pieces[k + 1], "space", 1) for k in (*crossings, 0) if k + 1 < space}
-    paired = dict(enumerate(pieces))
-    if crossings:
-        used = [came[k] for k in crossings]
-        far_terms, *used = lax.optimization_barrier((far_terms, *used))
-        for k, other in zip(crossings, used):
-            paired[k] = pieces[k] + other
-    crossed = [swap(paired[k], "space", k) for k in crossings]
-    from_beyond = lax.ppermute(far_terms, ("groups", "space"), to_beyond)
+    from_beyond = lax.ppermute(rim_terms(1, gate), ("groups", "space"), to_beyond)
     quarter = pieces[0]
-    for other in (*(came[k] for k in (0,) if space > 1), *crossed):
-        quarter = quarter + other
+    for k in reversed(range(1, space)):
+        quarter = quarter + lax.ppermute(pieces[k], "space", around("space", k))
     source_sum, edit_sum = call(
         functools.partial(back_kernel, space),
         (shape((rows, groups, GROUP, chan)), shape((rows, columns, chan))),
@@ -694,7 +679,7 @@
     *others, source_sum, edit_sum = lax.optimization_barrier((*others, source_sum, edit_sum))
     total, score_grad, loss = call(
         functools.partial(judge_kernel, pairs),
-        (shape((share, kout)), shape((8, LANES)), shape((1, LANES))),
+        (shape((share, kout), BF16), shape((8, LANES)), shape((1, LANES))),
         [],
         10**6,
         comp_first[None],
@@ -702,11 +687,7 @@
         comp_win[None],
         *others,
     )
-    gathered = {0: total}
-    for k in crossings:
-        gathered[k] = swap(total, "space", k)
-    if space > 1:
-        gathered[1] = swap(total, "space", 1)
+    gathered = [total] + [lax.ppermute(total, "space", around("space", k)) for k in range(1, space)]
     source_grad, edit_grad = call(
         functools.partial(finish_kernel, inv_root, space),
         (result((rows, columns, chan), BF16),) * 2,
@@ -723,12 +704,7 @@
         from_beyond,
         far_out=True,
     )
-    if crossings:
-        used = [gathered[k] for k in crossings]
-        source_grad, edit_grad, *used = lax.optimization_barrier((source_grad, edit_grad, *used))
-        for k, other in zip(crossings, used):
-            gathered[k], gathered[k + 1] = other, swap(other, "space", 1)
-    gathered = [gathered[k] for k in range(space)]
+    *gathered, source_grad, edit_grad = lax.optimization_barrier((*gathered, source_grad, edit_grad))
     conv_grad, bias_grad, head_grad, loss = call(
         functools.partial(gather_kernel, space),
         (result((disp, kout)), result((1, kout)), result((1, kout)), result((1, LANES))),

time: 34.9 us -> 33 us (0.946)
  waiting for transfers between devices: 6.23 us -> 3.4 us
  starting transfers between devices: 12.6 us -> 13.5 us
    ppermute x7, waiting for transfers between devices: 3.71 us -> 0.99 us  [the longest x3 0.5 us: local(): lax.ppermute(total, 'space', around('space', k))]
    ppermute x7, starting transfers between devices: 4.6 us -> 5.93 us  [the longest x1 2.08 us: local(): lax.ppermute(rim_terms(1, gate), ('groups', 'space'), to_beyond)]
    ppermute x3, starting transfers between devices: 4.84 us -> 4.45 us  [local(): lax.ppermute(quarter, 'pair', around('pair', k))]
  transfers between devices with their start and end apart: 13 -> 13, of which waited for: 6 -> 4; matrix products, arithmetic and copies ran while one was open for 0% -> 0% of each run, Pallas kernels for 33% -> 35%
where the time goes in v8:
time: 33 us; the launch traced here: 32.8 us
  Pallas kernels  15.1 us (46%)
  starting transfers between devices  13.5 us (41%)
  waiting for transfers between devices  3.4 us (10%)
  between operations  0.81 us (2%)
    pallas_call x11, Pallas kernels, call(): pl.pallas_call(kernel, out_shape=outs, in_specs=[pl.BlockSpec(memory_spac...  15.1 us
    ppermute x3, starting transfers between devices, local(): lax.ppermute(quarter, 'pair', around('pair', k))  4.45 us
    ppermute x1, starting transfers between devices, local(): beyond = lax.ppermute(beyond, ('groups', 'space'), to_beyond)  2.56 us
    ppermute x1, starting transfers between devices, local(): lax.ppermute(rim_terms(1, gate), ('groups', 'space'), to_beyond)  2.08 us
    ppermute x3, starting transfers between devices, local(): quarter = quarter + lax.ppermute(pieces[k], 'space', around('space', k))  1.93 us
    ppermute x3, starting transfers between devices, local(): lax.ppermute(total, 'space', around('space', k))  1.92 us
    ppermute x1, waiting for transfers between devices, local(): beyond = lax.ppermute(beyond, ('groups', 'space'), to_beyond)  1.31 us
    ppermute x3, waiting for transfers between devices, local(): lax.ppermute(quarter, 'pair', around('pair', k))  1.1 us
  transfers between devices with their start and end apart: 13, of which 4 were waited for; matrix products, arithmetic and copies ran while one was open for 0% of the time, Pallas kernels for 35%

profile of v8, /device:TPU:0, one launch (start us, length us, event | category | flops | bytes accessed | tf_op | source)
XLA Modules:
  0.0 32.8 jit_solution(12110343084141555465)
XLA Ops:
  0.6 1.2 %shard_map.129 = (bf16[8,128,256]{2,1,0:T(8,128)(2,1)S(1)}, bf16[8,128,256]{2,1,0:T(8,128)(2,1)S(1)}) custom-call(bf16[16,128,256]{2,1,0:T(8,128)(2,1)} %bitcast.24), custom_call_target="tpu_custom_call" | custom-call | flops 10000 | bytes 1048576 | tf_op jit(solution)/shard_map/pallas_call | solution.py:516
  1.9 0.5 %collective-permute-start = (bf16[8,128,256]{2,1,0:T(8,128)(2,1)S(1)}, bf16[8,128,256]{2,1,0:T(8,128)(2,1)S(1)}, u32[]{:S(2)}, u32[]{:S(2)}) collective-permute-start(bf16[8,128,256]{2,1,0:T(8,128)(2,1)S(1)} %get-tuple-element.53), channel_id=1, source_target_pairs={{0,4},{4,0},{8,12},{12,8},{1,5},{5,1},{9,13},{13,9},{2,6},{6,2},{1... | collective-permute-start | bytes 1572872 | tf_op jit(solution)/shard_map/ppermute | solution.py:575
  2.4 2.6 %collective-permute-start.1 = (bf16[8,128,256]{2,1,0:T(8,128)(2,1)S(1)}, bf16[8,128,256]{2,1,0:T(8,128)(2,1)S(1)}, u32[]{:S(2)}, u32[]{:S(2)}) collective-permute-start(bf16[8,128,256]{2,1,0:T(8,128)(2,1)S(1)} %get-tuple-element.57), channel_id=1, source_target_pairs={{0,16},{4,8},{8,4},{12,28},{16,0},{20,24},{24,20},{28,12},{1,17},{... | collective-permute-start | bytes 1572872 | tf_op jit(solution)/shard_map/ppermute | solution.py:576
  5.0 1.8 %shard_map.127 = (bf16[16,8,16,256]{3,2,1,0:T(8,128)(2,1)S(1)}, bf16[16,144,256]{2,1,0:T(8,128)(2,1)S(1)}, bf16[16,8,16,256]{3,2,1,0:T(8,128)(2,1)S(1)}, bf16[4,...) custom-call(bf16[16,8,16,256]{3,2,1,0:T(8,128)(2,1)} %bitcast.26, bf16[16,128,256]{2,1,0:T(8,128)(2,1)} %bitcast.25, ...), custom_call_target="tpu_custom_call" | custom-call | flops 10000 | bytes 2171136 | tf_op jit(solution)/shard_map/pallas_call | solution.py:516
  6.8 1.5 %shard_map.128 = (bf16[16,8,16,512]{3,2,1,0:T(8,128)(2,1)S(1)}, f32[16,128,128]{2,1,0:T(8,128)S(1)}) custom-call(bf16[16,8,16,256]{3,2,1,0:T(8,128)(2,1)S(1)} %get-tuple-element.48.turned_ref, bf16[16,144,256]{2,1,0:T(8,128)(2,1)S(1)} %get-tuple-element.49.pad.own_pad, bf16[4,896,128]{2,1,0:T(8,128)(2,1)S(1)} %get-tuple-element.50.tall_ref), custom_call_target="tpu_custom_call" | custom-call | flops 2000000000 | bytes 3145728 | tf_op jit(solution)/shard_map/pallas_call | solution.py:516
  8.3 1.7 %shard_map.130 = (bf16[8,128,128]{2,1,0:T(8,128)(2,1)S(1)}, f32[2,128]{1,0:T(2,128)S(1)}, f32[128,640]{1,0:T(8,128)S(1)}) custom-call(bf16[16,8,16,256]{3,2,1,0:T(8,128)(2,1)S(1)} %get-tuple-element.48.turned_ref, bf16[16,8,16,512]{3,2,1,0:T(8,128)(2,1)S(1)} %get-tuple-element.51.corr_ref, f32[16,128,128]{2,1,0:T(8,128)S(1)} %get-tuple-element.52.own_ref, ...), custom_call_target="tpu_custom_call" | custom-call | flops 1000000000 | bytes 5637120 | tf_op jit(solution)/shard_map/pallas_call | solution.py:516
  10.0 0.8 %shard_map.131 = bf16[8,128,256]{2,1,0:T(8,128)(2,1)S(1)} custom-call(bf16[8,128,128]{2,1,0:T(8,128)(2,1)S(1)} %get-tuple-element.54.gate_ref.near_gate_ref, bf16[4,128,896]{2,1,0:T(8,128)(2,1)S(1)} %get-tuple-element.55.wide_ref, bf16[16,8,16,256]{3,2,1,0:T(8,128)(2,1)S(1)} %get-tuple-element.56.source_ref), custom_call_target="tpu_custom_call" | custom-call | flops 1000000000 | bytes 2228224 | tf_op jit(solution)/shard_map/pallas_call | solution.py:516
  10.8 1.3 %collective-permute-done.1.halo_ref.beyond_ref = bf16[8,128,256]{2,1,0:T(8,128)(2,1)S(1)} collective-permute-done((bf16[8,128,256]{2,1,0:T(8,128)(2,1)S(1)}, bf16[8,128,256]{2,1,0:T(8,128)(2,1)S(1)}, u32[]{:S(2)}, u32[]{:S(2)}) %collective-permute-start.1) | collective-permute-done | bytes 524320 | tf_op jit(solution)/shard_map/ppermute | solution.py:576
  12.1 1.8 %shard_map.132 = (bf16[16,128,128]{2,1,0:T(8,128)(2,1)S(1)}, f32[80,128]{1,0:T(8,128)S(1)}, f32[80,128]{1,0:T(8,128)S(1)}, f32[80,128]{1,0:T(8,128)S(1)}, f32[80,128]{1,0:T(8,128)S(1)}) custom-call(bf16[16,8,16,256]{3,2,1,0:T(8,128)(2,1)S(1)} %get-tuple-element.48.turned_ref, bf16[16,8,16,512]{3,2,1,0:T(8,128)(2,1)S(1)} %get-tuple-element.51.corr_ref, ...), custom_call_target="tpu_custom_call" | custom-call | flops 2000000000 | bytes 6227968 | tf_op jit(solution)/shard_map/pallas_call | solution.py:516
  13.9 1.3 %collective-permute-start.2 = (f32[80,128]{1,0:T(8,128)S(1)}, f32[80,128]{1,0:T(8,128)S(1)}, u32[]{:S(2)}, u32[]{:S(2)}) collective-permute-start(f32[80,128]{1,0:T(8,128)S(1)} %get-tuple-element.62), channel_id=1, source_target_pairs={{0,12},{4,8},{8,4},{12,0},{1,13},{5,9},{9,5},{13,1},{2,14},{6,10},... | collective-permute-start | bytes 122888 | tf_op jit(solution)/shard_map/ppermute | solution.py:661
  15.2 0.6 %collective-permute-start.3 = (f32[80,128]{1,0:T(8,128)S(1)}, f32[80,128]{1,0:T(8,128)S(1)}, u32[]{:S(2)}, u32[]{:S(2)}) collective-permute-start(f32[80,128]{1,0:T(8,128)S(1)} %get-tuple-element.63), channel_id=1, source_target_pairs={{0,8},{4,12},{8,0},{12,4},{1,9},{5,13},{9,1},{13,5},{2,10},{6,14},... | collective-permute-start | bytes 122888 | tf_op jit(solution)/shard_map/ppermute | solution.py:661
  15.8 0.8 %shard_map.135 = bf16[8,128,256]{2,1,0:T(8,128)(2,1)S(1)} custom-call(bf16[16,128,128]{2,1,0:T(8,128)(2,1)S(1)} %get-tuple-element.65.gate_ref, bf16[4,128,896]{2,1,0:T(8,128)(2,1)S(1)} %get-tuple-element.55.wide_ref, bf16[16,8,16,256]{3,2,1,0:T(8,128)(2,1)S(1)} %get-tuple-element.56.source_ref), custom_call_target="tpu_custom_call" | custom-call | flops 1000000000 | bytes 2490368 | tf_op jit(solution)/shard_map/pallas_call | solution.py:516
  16.6 2.1 %collective-permute-start.12 = (bf16[8,128,256]{2,1,0:T(8,128)(2,1)S(1)}, bf16[8,128,256]{2,1,0:T(8,128)(2,1)S(1)}, u32[]{:S(2)}, u32[]{:S(2)}) collective-permute-start(bf16[8,128,256]{2,1,0:T(8,128)(2,1)S(1)} %shard_map.135), channel_id=1, source_target_pairs={{0,16},{4,8},{8,4},{12,28},{16,0},{20,24},{24,20},{28,12},{1,17},{... | collective-permute-start | bytes 1572872 | tf_op jit(solution)/shard_map/ppermute | solution.py:658
  18.7 0.5 %collective-permute-done.3 = f32[80,128]{1,0:T(8,128)S(1)} collective-permute-done((f32[80,128]{1,0:T(8,128)S(1)}, f32[80,128]{1,0:T(8,128)S(1)}, u32[]{:S(2)}, u32[]{:S(2)}) %collective-permute-start.3) | collective-permute-done | bytes 40992 | tf_op jit(solution)/shard_map/ppermute | solution.py:661
  19.3 3.7 %collective-permute-start.7 = (f32[80,128]{1,0:T(8,128)S(1)}, f32[80,128]{1,0:T(8,128)S(1)}, u32[]{:S(2)}, u32[]{:S(2)}) collective-permute-start(f32[80,128]{1,0:T(8,128)S(1)} %add_add_fusion.rest_0_), channel_id=1, source_target_pairs={{0,3},{1,2},{2,1},{3,0},{4,7},{5,6},{6,5},{7,4},{8,11},{9,10},{10,... | collective-permute-start | bytes 122888 | tf_op jit(solution)/shard_map/ppermute | solution.py:678
  23.0 0.7 %collective-permute-start.5 = (f32[80,128]{1,0:T(8,128)S(1)}, f32[80,128]{1,0:T(8,128)S(1)}, u32[]{:S(2)}, u32[]{:S(2)}) collective-permute-start(f32[80,128]{1,0:T(8,128)S(1)} %add_add_fusion.rest_0_), channel_id=1, source_target_pairs={{0,1},{1,0},{2,3},{3,2},{4,5},{5,4},{6,7},{7,6},{8,9},{9,8},{10,11... | collective-permute-start | bytes 122888 | tf_op jit(solution)/shard_map/ppermute | solution.py:678
  23.7 3.0 %shard_map.133 = (f32[16,8,16,256]{3,2,1,0:T(8,128)S(1)}, f32[16,128,256]{2,1,0:T(8,128)S(1)}) custom-call(bf16[16,128,128]{2,1,0:T(8,128)(2,1)S(1)} %get-tuple-element.65.gate_ref, bf16[4,128,896]{2,1,0:T(8,128)(2,1)S(1)} %get-tuple-element.55.wide_ref, bf16[16,8,16,256]{3,2,1,0:T(8,128)(2,1)S(1)} %get-tuple-element.56.source_ref, ...), custom_call_target="tpu_custom_call" | custom-call | flops 4000000000 | bytes 4718592 | tf_op jit(solution)/shard_map/pallas_call | solution.py:516
  26.8 1.1 %collective-permute-done.6.rest_2_ = f32[80,128]{1,0:T(8,128)S(1)} collective-permute-done((f32[80,128]{1,0:T(8,128)S(1)}, f32[80,128]{1,0:T(8,128)S(1)}, u32[]{:S(2)}, u32[]{:S(2)}) %collective-permute-start.6) | collective-permute-done | bytes 40992 | tf_op jit(solution)/shard_map/ppermute | solution.py:678
  27.9 0.2 shard_map.134
  28.2 1.1 %collective-permute-start.9 = (bf16[80,128]{1,0:T(8,128)(2,1)S(1)}, bf16[80,128]{1,0:T(8,128)(2,1)S(1)}, u32[]{:S(2)}, u32[]{:S(2)}) collective-permute-start(bf16[80,128]{1,0:T(8,128)(2,1)S(1)} %get-tuple-element.81.rest_0_), channel_id=1, source_target_pairs={{0,8},{4,12},{8,0},{12,4},{1,9},{5,13},{9,1},{13,5},{2,10},{6,14},... | collective-permute-start | bytes 61448 | tf_op jit(solution)/shard_map/ppermute | solution.py:690
  29.3 0.7 %collective-permute-start.8 = (bf16[80,128]{1,0:T(8,128)(2,1)S(1)}, bf16[80,128]{1,0:T(8,128)(2,1)S(1)}, u32[]{:S(2)}, u32[]{:S(2)}) collective-permute-start(bf16[80,128]{1,0:T(8,128)(2,1)S(1)} %get-tuple-element.81.rest_0_), channel_id=1, source_target_pairs={{0,4},{4,0},{8,12},{12,8},{1,5},{5,1},{9,13},{13,9},{2,6},{6,2},{1... | collective-permute-start | bytes 61448 | tf_op jit(solution)/shard_map/ppermute | solution.py:690
  30.0 1.6 %shard_map.136 = (bf16[16,128,256]{2,1,0:T(8,128)(2,1)}, bf16[16,128,256]{2,1,0:T(8,128)(2,1)}) custom-call(f32[8,128]{1,0:T(8,128)S(1)} %get-tuple-element.73.grad_ref, f32[16,128,256]{2,1,0:T(8,128)S(1)} %bitcast.16, f32[16,128,256]{2,1,0:T(8,128)S(1)} %get-tuple-element.75.edit_ref, bf16[8,128,256]{2,1,0:T(8,128)(2,1)S(1)} %collective-permute-done.11.across_ref, ...), custom_call_target="tpu_custom_call" | custom-call | flops 10000000 | bytes 5246976 | tf_op jit(solution)/shard_map/pallas_call | solution.py:516
  31.6 0.5 %collective-permute-done.9.rest_2_ = bf16[80,128]{1,0:T(8,128)(2,1)S(1)} collective-permute-done((bf16[80,128]{1,0:T(8,128)(2,1)S(1)}, bf16[80,128]{1,0:T(8,128)(2,1)S(1)}, u32[]{:S(2)}, u32[]{:S(2)}) %collective-permute-start.9) | collective-permute-done | bytes 20512 | tf_op jit(solution)/shard_map/ppermute | solution.py:690
  32.1 0.7 %shard_map.137 = (f32[289,128]{1,0:T(8,128)}, f32[1,128]{1,0:T(1,128)}, f32[1,128]{1,0:T(1,128)}, f32[1,128]{1,0:T(1,128)}) custom-call(bf16[80,128]{1,0:T(8,128)(2,1)S(1)} %get-tuple-element.81.rest_0_, bf16[80,128]{1,0:T(8,128)(2,1)S(1)} %collective-permute-done.8.rest_1_, bf16[80,128]{1,0:T(8,128)(2,1)S(1)} %collective-permute-done.9.rest_2_, ...), custom_call_target="tpu_custom_call" | custom-call | flops 1000000 | bytes 82432 | tf_op jit(solution)/shard_map/pallas_call | solution.py:516
  (24 shorter events, 0.2 us)
Async XLA Ops:
  1.9 6.4 %collective-permute-start = (bf16[8,128,256]{2,1,0:T(8,128)(2,1)S(1)}, bf16[8,128,256]{2,1,0:T(8,128)(2,1)S(1)}, u32[]{:S(2)}, u32[]{:S(2)}) collective-permute-start(bf16[8,128,256]{2,1,0:T(8,128)(2,1)S(1)} %get-tuple-element.53), channel_id=1, source_target_pairs={{0,4},{4,0},{8,12},{12,8},{1,5},{5,1},{9,13},{13,9},{2,6},{6,2},{1... | collective-permute-start | bytes 1572872 | tf_op jit(solution)/shard_map/ppermute | solution.py:575
  2.4 9.7 %collective-permute-start.1 = (bf16[8,128,256]{2,1,0:T(8,128)(2,1)S(1)}, bf16[8,128,256]{2,1,0:T(8,128)(2,1)S(1)}, u32[]{:S(2)}, u32[]{:S(2)}) collective-permute-start(bf16[8,128,256]{2,1,0:T(8,128)(2,1)S(1)} %get-tuple-element.57), channel_id=1, source_target_pairs={{0,16},{4,8},{8,4},{12,28},{16,0},{20,24},{24,20},{28,12},{1,17},{... | collective-permute-start | bytes 1572872 | tf_op jit(solution)/shard_map/ppermute | solution.py:576
  6.8 1.5 %copy-start = (f32[128]{0:T(128)S(1)}, f32[128]{0:T(128)}, u32[]{:S(2)}) copy-start(f32[128]{0:T(128)} %param.11) | copy-start | bytes 1540
  6.8 1.5 %copy-start.1 = (f32[128]{0:T(128)S(1)}, f32[128]{0:T(128)}, u32[]{:S(2)}) copy-start(f32[128]{0:T(128)} %param.12) | copy-start | bytes 1540
  13.9 4.8 %collective-permute-start.2 = (f32[80,128]{1,0:T(8,128)S(1)}, f32[80,128]{1,0:T(8,128)S(1)}, u32[]{:S(2)}, u32[]{:S(2)}) collective-permute-start(f32[80,128]{1,0:T(8,128)S(1)} %get-tuple-element.62), channel_id=1, source_target_pairs={{0,12},{4,8},{8,4},{12,0},{1,13},{5,9},{9,5},{13,1},{2,14},{6,10},... | collective-permute-start | bytes 122888 | tf_op jit(solution)/shard_map/ppermute | solution.py:661
  15.2 4.0 %collective-permute-start.3 = (f32[80,128]{1,0:T(8,128)S(1)}, f32[80,128]{1,0:T(8,128)S(1)}, u32[]{:S(2)}, u32[]{:S(2)}) collective-permute-start(f32[80,128]{1,0:T(8,128)S(1)} %get-tuple-element.63), channel_id=1, source_target_pairs={{0,8},{4,12},{8,0},{12,4},{1,9},{5,13},{9,1},{13,5},{2,10},{6,14},... | collective-permute-start | bytes 122888 | tf_op jit(solution)/shard_map/ppermute | solution.py:661
  15.8 3.5 %collective-permute-start.4 = (f32[80,128]{1,0:T(8,128)S(1)}, f32[80,128]{1,0:T(8,128)S(1)}, u32[]{:S(2)}, u32[]{:S(2)}) collective-permute-start(f32[80,128]{1,0:T(8,128)S(1)} %get-tuple-element.64), channel_id=1, source_target_pairs={{0,4},{4,0},{8,12},{12,8},{1,5},{5,1},{9,13},{13,9},{2,6},{6,2},{1... | collective-permute-start | bytes 122888 | tf_op jit(solution)/shard_map/ppermute | solution.py:661
  16.6 13.4 %collective-permute-start.12 = (bf16[8,128,256]{2,1,0:T(8,128)(2,1)S(1)}, bf16[8,128,256]{2,1,0:T(8,128)(2,1)S(1)}, u32[]{:S(2)}, u32[]{:S(2)}) collective-permute-start(bf16[8,128,256]{2,1,0:T(8,128)(2,1)S(1)} %shard_map.135), channel_id=1, source_target_pairs={{0,16},{4,8},{8,4},{12,28},{16,0},{20,24},{24,20},{28,12},{1,17},{... | collective-permute-start | bytes 1572872 | tf_op jit(solution)/shard_map/ppermute | solution.py:658
  18.7 11.3 %collective-permute-start.11 = (bf16[8,128,256]{2,1,0:T(8,128)(2,1)S(1)}, bf16[8,128,256]{2,1,0:T(8,128)(2,1)S(1)}, u32[]{:S(2)}, u32[]{:S(2)}) collective-permute-start(bf16[8,128,256]{2,1,0:T(8,128)(2,1)S(1)} %shard_map.131), channel_id=1, source_target_pairs={{0,4},{4,0},{8,12},{12,8},{1,5},{5,1},{9,13},{13,9},{2,6},{6,2},{1... | collective-permute-start | bytes 1572872 | tf_op jit(solution)/shard_map/ppermute | solution.py:641
  19.2 8.6 %copy-start.2 = (s32[16]{0:T(128)S(1)}, s32[16]{0:T(128)}, u32[]{:S(2)}) copy-start(s32[16]{0:T(128)} %param.13) | copy-start | bytes 196
  19.2 8.6 %copy-start.3 = (s32[16]{0:T(128)S(1)}, s32[16]{0:T(128)}, u32[]{:S(2)}) copy-start(s32[16]{0:T(128)} %param.14) | copy-start | bytes 196
  19.3 8.6 %copy-start.4 = (s32[16]{0:T(128)S(1)}, s32[16]{0:T(128)}, u32[]{:S(2)}) copy-start(s32[16]{0:T(128)} %param.15) | copy-start | bytes 196
  19.3 7.5 %collective-permute-start.7 = (f32[80,128]{1,0:T(8,128)S(1)}, f32[80,128]{1,0:T(8,128)S(1)}, u32[]{:S(2)}, u32[]{:S(2)}) collective-permute-start(f32[80,128]{1,0:T(8,128)S(1)} %add_add_fusion.rest_0_), channel_id=1, source_target_pairs={{0,3},{1,2},{2,1},{3,0},{4,7},{5,6},{6,5},{7,4},{8,11},{9,10},{10,... | collective-permute-start | bytes 122888 | tf_op jit(solution)/shard_map/ppermute | solution.py:678
  23.0 4.9 %collective-permute-start.6 = (f32[80,128]{1,0:T(8,128)S(1)}, f32[80,128]{1,0:T(8,128)S(1)}, u32[]{:S(2)}, u32[]{:S(2)}) collective-permute-start(f32[80,128]{1,0:T(8,128)S(1)} %add_add_fusion.rest_0_), channel_id=1, source_target_pairs={{0,2},{1,3},{2,0},{3,1},{4,6},{5,7},{6,4},{7,5},{8,10},{9,11},{10,... | collective-permute-start | bytes 122888 | tf_op jit(solution)/shard_map/ppermute | solution.py:678
  23.0 4.9 %collective-permute-start.5 = (f32[80,128]{1,0:T(8,128)S(1)}, f32[80,128]{1,0:T(8,128)S(1)}, u32[]{:S(2)}, u32[]{:S(2)}) collective-permute-start(f32[80,128]{1,0:T(8,128)S(1)} %add_add_fusion.rest_0_), channel_id=1, source_target_pairs={{0,1},{1,0},{2,3},{3,2},{4,5},{5,4},{6,7},{7,6},{8,9},{9,8},{10,11... | collective-permute-start | bytes 122888 | tf_op jit(solution)/shard_map/ppermute | solution.py:678
  28.1 3.5 %collective-permute-start.10 = (bf16[80,128]{1,0:T(8,128)(2,1)S(1)}, bf16[80,128]{1,0:T(8,128)(2,1)S(1)}, u32[]{:S(2)}, u32[]{:S(2)}) collective-permute-start(bf16[80,128]{1,0:T(8,128)(2,1)S(1)} %get-tuple-element.81.rest_0_), channel_id=1, source_target_pairs={{0,12},{4,8},{8,4},{12,0},{1,13},{5,9},{9,5},{13,1},{2,14},{6,10},... | collective-permute-start | bytes 61448 | tf_op jit(solution)/shard_map/ppermute | solution.py:690
  28.2 4.0 %collective-permute-start.9 = (bf16[80,128]{1,0:T(8,128)(2,1)S(1)}, bf16[80,128]{1,0:T(8,128)(2,1)S(1)}, u32[]{:S(2)}, u32[]{:S(2)}) collective-permute-start(bf16[80,128]{1,0:T(8,128)(2,1)S(1)} %get-tuple-element.81.rest_0_), channel_id=1, source_target_pairs={{0,8},{4,12},{8,0},{12,4},{1,9},{5,13},{9,1},{13,5},{2,10},{6,14},... | collective-permute-start | bytes 61448 | tf_op jit(solution)/shard_map/ppermute | solution.py:690
  29.3 2.9 %collective-permute-start.8 = (bf16[80,128]{1,0:T(8,128)(2,1)S(1)}, bf16[80,128]{1,0:T(8,128)(2,1)S(1)}, u32[]{:S(2)}, u32[]{:S(2)}) collective-permute-start(bf16[80,128]{1,0:T(8,128)(2,1)S(1)} %get-tuple-element.81.rest_0_), channel_id=1, source_target_pairs={{0,4},{4,0},{8,12},{12,8},{1,5},{5,1},{9,13},{13,9},{2,6},{6,2},{1... | collective-permute-start | bytes 61448 | tf_op jit(solution)/shard_map/ppermute | solution.py:690

commit v9 on v8

--- a/solution.py
+++ b/solution.py
@@ -231,7 +231,8 @@
             gate_ref[gate_at + i] = nn(turn, pre[q * cols : (q + 1) * cols]).astype(BF16)
         corr = [strip[i, :, :, i // PER * LANES : (i // PER + POS) * LANES] for i in rows]
         corr = jnp.concatenate([c.reshape(cols, POS * LANES) for c in corr], axis=0)
-        grad = tn(pre, corr)
+        level = jnp.where(jnp.abs(slope - 1.0) < 2.0**-9, 1.0, 0.0).astype(BF16)
+        grad = tn(jnp.concatenate([pre, level], axis=1), corr)
         if r:
             grad = pltpu.roll(grad, POS * LANES - r * WIN, 1)
         total = grad if total is None else total + grad
@@ -323,19 +324,49 @@
     total = total + near_total_ref[...]
     head = head_ref[...]
     kout = head.shape[1]
-    share = stage.shape[0] // parts
+    share = stage.shape[1] // parts
     stage[...] = jnp.zeros(stage.shape, F32)
     scale = 1.0 / pixels
     turned = jnp.transpose(total) * scale
     for dy in range(SPAN):
-        put_rows(stage, share, dy * SPAN, turned[dy * WIN : dy * WIN + SPAN])
-    put_rows(stage, share, STAT, jnp.concatenate([head * slopes, hidden], axis=0) * scale)
+        for i in range(2):
+            block = turned[dy * WIN : dy * WIN + SPAN, i * kout : (i + 1) * kout]
+            put_rows(stage.at[i], share, dy * SPAN, block)
+    put_rows(stage.at[0], share, STAT, jnp.concatenate([head * slopes, hidden], axis=0) * scale)
     score = jnp.sum(hidden * head, axis=1, keepdims=True) * scale
+    for p in range(parts):
+        stage[0, (p + 1) * share - 1 : (p + 1) * share] = jnp.broadcast_to(score, (1, kout))
     me = lax.axis_index("space")
     for k in range(parts):
-        start = pl.multiple_of(partner(me, k, parts) * share, 8)
-        piece_refs[k][...] = stage[pl.ds(start, share), :]
-        piece_refs[k][share - 1 :] = jnp.broadcast_to(score, (1, kout))
+        at = pl.ds(pl.multiple_of(partner(me, k, parts) * share, 8), share)
+        encode(piece_refs[k], stage[0, at], stage[1, at])
+
+
+def encode(ref, value, level):
+    first = value.astype(BF16)
+    left = value - first.astype(F32)
+    second = left.astype(BF16)
+    third = left - second.astype(F32)
+    ref[0] = first
+    ref[1] = second
+    last = iota(value.shape, 0) == value.shape[0] - 1
+    ref[2] = jnp.where(last, third, level).astype(BF16)
+
+
+def decode(ref):
+    third = ref[2].astype(F32)
+    last = iota(third.shape, 0) == third.shape[0] - 1
+    value = ref[0].astype(F32) + ref[1].astype(F32) + jnp.where(last, third, 0.0)
+    return value, jnp.where(last, 0.0, third)
+
+
+def merge_kernel(*refs):
+    *came_refs, out_ref = refs
+    value, level = decode(came_refs[0])
+    for ref in came_refs[1:]:
+        more, flat = decode(ref)
+        value, level = value + more, level + flat
+    encode(out_ref, value, level)
 
 
 def back_chunks(gate_ref, wide_ref, r, rows, groups):
@@ -428,17 +459,20 @@
     return me ^ abs(step)
 
 
-def judge_kernel(pairs, first_ref, second_ref, win_ref, *rest):
+def judge_kernel(pairs, first_ref, second_ref, win_ref, head_ref, *rest):
     piece_refs = rest[:pairs]
     total_ref, grad_ref, loss_ref = rest[pairs:]
     share = total_ref.shape[0]
     me = lax.axis_index("pair")
     first, second, win = first_ref[...], second_ref[...], win_ref[...]
     hots, margin = [], jnp.zeros(first.shape, F32)
+    planes = [decode(ref) for ref in piece_refs]
+    head = head_ref[...]
+    held = head.astype(BF16).astype(F32)
     for k in range(pairs):
         pid = partner(me, -k, pairs)
         hot = (first == pid).astype(F32) - (second == pid).astype(F32)
-        score = piece_refs[k][share - 1 : share, 0:1]
+        score = planes[k][0][share - 1 : share, 0:1]
         margin = margin + hot * score
         hots.append(hot)
     sign = 2.0 * win.astype(F32) - 1.0
@@ -450,7 +484,8 @@
         grad = jnp.sum(margin_grad * hots[k], axis=1, keepdims=True)
         if k == 0:
             grad_ref[...] = jnp.broadcast_to(grad, grad_ref.shape)
-        total = total + grad * piece_refs[k][...]
+        extra = (grad * head).astype(BF16).astype(F32) - grad * held
+        total = total + grad * planes[k][0] + extra * planes[k][1]
     total_ref[...] = total.astype(total_ref.dtype)
 
 
@@ -612,7 +647,7 @@
         (
             shape((rows // 2, columns, kout), BF16),
             shape((2, kout)),
-            shape((kout, POS * LANES)),
+            shape((2 * kout, POS * LANES)),
         ),
         work,
         10**9,
@@ -641,8 +676,8 @@
     from_across = lax.ppermute(terms, "space", to_across)
     gate, *pieces = call(
         functools.partial(outer_kernel, inv_root, pixels, space),
-        (shape((rows, columns, kout), BF16),) + (shape((share, kout)),) * space,
-        work + [pltpu.VMEM((share * space, kout), F32)],
+        (shape((rows, columns, kout), BF16),) + (shape((3, share, kout), BF16),) * space,
+        work + [pltpu.VMEM((2, share * space, kout), F32)],
         2 * 10**9,
         turned,
         corr,
@@ -656,9 +691,10 @@
         near_total,
     )
     from_beyond = lax.ppermute(rim_terms(1, gate), ("groups", "space"), to_beyond)
-    quarter = pieces[0]
-    for k in reversed(range(1, space)):
-        quarter = quarter + lax.ppermute(pieces[k], "space", around("space", k))
+    came = [lax.ppermute(pieces[k], "space", around("space", k)) for k in reversed(range(1, space))]
+    (quarter,) = call(
+        merge_kernel, (shape((3, share, kout), BF16),), [], 10**4, pieces[0], *came
+    )
     source_sum, edit_sum = call(
         functools.partial(back_kernel, space),
         (shape((rows, groups, GROUP, chan)), shape((rows, columns, chan))),
@@ -685,6 +721,7 @@
         comp_first[None],
         comp_second[None],
         comp_win[None],
+        head_weight[None],
         *others,
     )
     gathered = [total] + [lax.ppermute(total, "space", around("space", k)) for k in range(1, space)]

time: 33 us -> 41.2 us (1.25)
  waiting for transfers between devices: 3.4 us -> 10.4 us
  Pallas kernels: 15.1 us -> 15.7 us
  starting transfers between devices: 13.5 us -> 14.1 us
    ppermute x3, waiting for transfers between devices: 0.49 us -> 7.39 us  [local(): lax.ppermute(pieces[k], 'space', around('space', k))]
    pallas_call x11 -> x12, Pallas kernels: 15.1 us -> 15.7 us  [call(): pl.pallas_call(kernel, out_shape=outs, in_specs=[pl.BlockSpec(memory_spac...]
    ppermute x3, waiting for transfers between devices: 1.1 us -> 1.63 us  [local(): lax.ppermute(quarter, 'pair', around('pair', k))]
  transfers between devices with their start and end apart: 13 -> 13, of which waited for: 4 -> 5; matrix products, arithmetic and copies ran while one was open for 0% -> 0% of each run, Pallas kernels for 35% -> 26%
where the time goes in v9:
time: 41.2 us; the launch traced here: 41.1 us
  Pallas kernels  15.7 us (38%)
  starting transfers between devices  14.1 us (34%)
  waiting for transfers between devices  10.4 us (25%)
  between operations  0.81 us (2%)
    pallas_call x12, Pallas kernels, call(): pl.pallas_call(kernel, out_shape=outs, in_specs=[pl.BlockSpec(memory_spac...  15.7 us
    ppermute x3, waiting for transfers between devices, local(): lax.ppermute(pieces[k], 'space', around('space', k))  7.39 us
    ppermute x3, starting transfers between devices, local(): lax.ppermute(quarter, 'pair', around('pair', k))  4.84 us
    ppermute x1, starting transfers between devices, local(): beyond = lax.ppermute(beyond, ('groups', 'space'), to_beyond)  2.56 us
    ppermute x3, starting transfers between devices, local(): lax.ppermute(pieces[k], 'space', around('space', k))  2.14 us
    ppermute x1, starting transfers between devices, local(): lax.ppermute(rim_terms(1, gate), ('groups', 'space'), to_beyond)  2.08 us
    ppermute x3, starting transfers between devices, local(): lax.ppermute(total, 'space', around('space', k))  1.92 us
    ppermute x3, waiting for transfers between devices, local(): lax.ppermute(quarter, 'pair', around('pair', k))  1.63 us
  transfers between devices with their start and end apart: 13, of which 5 were waited for; matrix products, arithmetic and copies ran while one was open for 0% of the time, Pallas kernels for 26%

profile of v9, /device:TPU:0, one launch (start us, length us, event | category | flops | bytes accessed | tf_op | source)
XLA Modules:
  0.0 41.1 jit_solution(13066779682376035536)
XLA Ops:
  0.6 1.2 %shard_map.129 = (bf16[8,128,256]{2,1,0:T(8,128)(2,1)S(1)}, bf16[8,128,256]{2,1,0:T(8,128)(2,1)S(1)}) custom-call(bf16[16,128,256]{2,1,0:T(8,128)(2,1)} %bitcast.25), custom_call_target="tpu_custom_call" | custom-call | flops 10000 | bytes 1048576 | tf_op jit(solution)/shard_map/pallas_call | solution.py:551
  1.9 0.5 %collective-permute-start = (bf16[8,128,256]{2,1,0:T(8,128)(2,1)S(1)}, bf16[8,128,256]{2,1,0:T(8,128)(2,1)S(1)}, u32[]{:S(2)}, u32[]{:S(2)}) collective-permute-start(bf16[8,128,256]{2,1,0:T(8,128)(2,1)S(1)} %get-tuple-element.53), channel_id=1, source_target_pairs={{0,4},{4,0},{8,12},{12,8},{1,5},{5,1},{9,13},{13,9},{2,6},{6,2},{1... | collective-permute-start | bytes 1572872 | tf_op jit(solution)/shard_map/ppermute | solution.py:610
  2.4 2.6 %collective-permute-start.1 = (bf16[8,128,256]{2,1,0:T(8,128)(2,1)S(1)}, bf16[8,128,256]{2,1,0:T(8,128)(2,1)S(1)}, u32[]{:S(2)}, u32[]{:S(2)}) collective-permute-start(bf16[8,128,256]{2,1,0:T(8,128)(2,1)S(1)} %get-tuple-element.57), channel_id=1, source_target_pairs={{0,16},{4,8},{8,4},{12,28},{16,0},{20,24},{24,20},{28,12},{1,17},{... | collective-permute-start | bytes 1572872 | tf_op jit(solution)/shard_map/ppermute | solution.py:611
  5.0 1.8 %shard_map.127 = (bf16[16,8,16,256]{3,2,1,0:T(8,128)(2,1)S(1)}, bf16[16,144,256]{2,1,0:T(8,128)(2,1)S(1)}, bf16[16,8,16,256]{3,2,1,0:T(8,128)(2,1)S(1)}, bf16[4,...) custom-call(bf16[16,8,16,256]{3,2,1,0:T(8,128)(2,1)} %bitcast.27, bf16[16,128,256]{2,1,0:T(8,128)(2,1)} %bitcast.26, ...), custom_call_target="tpu_custom_call" | custom-call | flops 10000 | bytes 2171136 | tf_op jit(solution)/shard_map/pallas_call | solution.py:551
  6.8 1.5 %shard_map.128 = (bf16[16,8,16,512]{3,2,1,0:T(8,128)(2,1)S(1)}, f32[16,128,128]{2,1,0:T(8,128)S(1)}) custom-call(bf16[16,8,16,256]{3,2,1,0:T(8,128)(2,1)S(1)} %get-tuple-element.48.turned_ref, bf16[16,144,256]{2,1,0:T(8,128)(2,1)S(1)} %get-tuple-element.49.pad.own_pad, bf16[4,896,128]{2,1,0:T(8,128)(2,1)S(1)} %get-tuple-element.50.tall_ref), custom_call_target="tpu_custom_call" | custom-call | flops 2000000000 | bytes 3145728 | tf_op jit(solution)/shard_map/pallas_call | solution.py:551
  8.3 2.0 %shard_map.130 = (bf16[8,128,128]{2,1,0:T(8,128)(2,1)S(1)}, f32[2,128]{1,0:T(2,128)S(1)}, f32[256,640]{1,0:T(8,128)S(1)}) custom-call(bf16[16,8,16,256]{3,2,1,0:T(8,128)(2,1)S(1)} %get-tuple-element.48.turned_ref, bf16[16,8,16,512]{3,2,1,0:T(8,128)(2,1)S(1)} %get-tuple-element.51.corr_ref, f32[16,128,128]{2,1,0:T(8,128)S(1)} %get-tuple-element.52.own_ref, ...), custom_call_target="tpu_custom_call" | custom-call | flops 1000000000 | bytes 5637120 | tf_op jit(solution)/shard_map/pallas_call | solution.py:551
  10.3 0.8 %shard_map.131 = bf16[8,128,256]{2,1,0:T(8,128)(2,1)S(1)} custom-call(bf16[8,128,128]{2,1,0:T(8,128)(2,1)S(1)} %get-tuple-element.54.gate_ref.near_gate_ref, bf16[4,128,896]{2,1,0:T(8,128)(2,1)S(1)} %get-tuple-element.55.wide_ref, bf16[16,8,16,256]{3,2,1,0:T(8,128)(2,1)S(1)} %get-tuple-element.56.source_ref), custom_call_target="tpu_custom_call" | custom-call | flops 1000000000 | bytes 2228224 | tf_op jit(solution)/shard_map/pallas_call | solution.py:551
  11.1 1.0 %collective-permute-done.1.halo_ref.beyond_ref = bf16[8,128,256]{2,1,0:T(8,128)(2,1)S(1)} collective-permute-done((bf16[8,128,256]{2,1,0:T(8,128)(2,1)S(1)}, bf16[8,128,256]{2,1,0:T(8,128)(2,1)S(1)}, u32[]{:S(2)}, u32[]{:S(2)}) %collective-permute-start.1) | collective-permute-done | bytes 524320 | tf_op jit(solution)/shard_map/ppermute | solution.py:611
  12.1 2.1 %shard_map.132 = (bf16[16,128,128]{2,1,0:T(8,128)(2,1)S(1)}, bf16[3,80,128]{2,1,0:T(8,128)(2,1)S(1)}, bf16[3,80,128]{2,1,0:T(8,128)(2,1)S(1)}, bf16[3,80,128]{2,1,0:T(8,128)(2,1)S(1)}, bf16[3,80,128]{2,1,0:T(8,128)(2,1)S(1)}) custom-call(bf16[16,8,16,256]{3,2,1,0:T(8,128)(2,1)S(1)} %get-tuple-element.48.turned_ref, ...), custom_call_target="tpu_custom_call" | custom-call | flops 2000000000 | bytes 6555648 | tf_op jit(solution)/shard_map/pallas_call | solution.py:551
  14.3 0.8 %shard_map.136 = bf16[8,128,256]{2,1,0:T(8,128)(2,1)S(1)} custom-call(bf16[16,128,128]{2,1,0:T(8,128)(2,1)S(1)} %get-tuple-element.65.gate_ref, bf16[4,128,896]{2,1,0:T(8,128)(2,1)S(1)} %get-tuple-element.55.wide_ref, bf16[16,8,16,256]{3,2,1,0:T(8,128)(2,1)S(1)} %get-tuple-element.56.source_ref), custom_call_target="tpu_custom_call" | custom-call | flops 1000000000 | bytes 2490368 | tf_op jit(solution)/shard_map/pallas_call | solution.py:551
  15.1 2.1 %collective-permute-start.12 = (bf16[8,128,256]{2,1,0:T(8,128)(2,1)S(1)}, bf16[8,128,256]{2,1,0:T(8,128)(2,1)S(1)}, u32[]{:S(2)}, u32[]{:S(2)}) collective-permute-start(bf16[8,128,256]{2,1,0:T(8,128)(2,1)S(1)} %shard_map.136), channel_id=1, source_target_pairs={{0,16},{4,8},{8,4},{12,28},{16,0},{20,24},{24,20},{28,12},{1,17},{... | collective-permute-start | bytes 1572872 | tf_op jit(solution)/shard_map/ppermute | solution.py:693
  17.2 0.4 collective-permute-start.2
  17.6 1.7 %collective-permute-start.3 = (bf16[3,80,128]{2,1,0:T(8,128)(2,1)S(1)}, bf16[3,80,128]{2,1,0:T(8,128)(2,1)S(1)}, u32[]{:S(2)}, u32[]{:S(2)}) collective-permute-start(bf16[3,80,128]{2,1,0:T(8,128)(2,1)S(1)} %get-tuple-element.63), channel_id=1, source_target_pairs={{0,8},{4,12},{8,0},{12,4},{1,9},{5,13},{9,1},{13,5},{2,10},{6,14},... | collective-permute-start | bytes 184328 | tf_op jit(solution)/shard_map/ppermute | solution.py:694
  19.3 2.2 %collective-permute-done.2.refs_1_ = bf16[3,80,128]{2,1,0:T(8,128)(2,1)S(1)} collective-permute-done((bf16[3,80,128]{2,1,0:T(8,128)(2,1)S(1)}, bf16[3,80,128]{2,1,0:T(8,128)(2,1)S(1)}, u32[]{:S(2)}, u32[]{:S(2)}) %collective-permute-start.2) | collective-permute-done | bytes 61472 | tf_op jit(solution)/shard_map/ppermute | solution.py:694
  21.5 5.2 %collective-permute-done.3.refs_2_ = bf16[3,80,128]{2,1,0:T(8,128)(2,1)S(1)} collective-permute-done((bf16[3,80,128]{2,1,0:T(8,128)(2,1)S(1)}, bf16[3,80,128]{2,1,0:T(8,128)(2,1)S(1)}, u32[]{:S(2)}, u32[]{:S(2)}) %collective-permute-start.3) | collective-permute-done | bytes 61472 | tf_op jit(solution)/shard_map/ppermute | solution.py:694
  26.8 4.2 %collective-permute-start.7 = (bf16[3,80,128]{2,1,0:T(8,128)(2,1)S(1)}, bf16[3,80,128]{2,1,0:T(8,128)(2,1)S(1)}, u32[]{:S(2)}, u32[]{:S(2)}) collective-permute-start(bf16[3,80,128]{2,1,0:T(8,128)(2,1)S(1)} %shard_map.133.rest_0_), channel_id=1, source_target_pairs={{0,3},{1,2},{2,1},{3,0},{4,7},{5,6},{6,5},{7,4},{8,11},{9,10},{10,... | collective-permute-start | bytes 184328 | tf_op jit(solution)/shard_map/ppermute | solution.py:714
  31.0 0.6 %collective-permute-start.5 = (bf16[3,80,128]{2,1,0:T(8,128)(2,1)S(1)}, bf16[3,80,128]{2,1,0:T(8,128)(2,1)S(1)}, u32[]{:S(2)}, u32[]{:S(2)}) collective-permute-start(bf16[3,80,128]{2,1,0:T(8,128)(2,1)S(1)} %shard_map.133.rest_0_), channel_id=1, source_target_pairs={{0,1},{1,0},{2,3},{3,2},{4,5},{5,4},{6,7},{7,6},{8,9},{9,8},{10,11... | collective-permute-start | bytes 184328 | tf_op jit(solution)/shard_map/ppermute | solution.py:714
  31.6 2.9 %shard_map.134 = (f32[16,8,16,256]{3,2,1,0:T(8,128)S(1)}, f32[16,128,256]{2,1,0:T(8,128)S(1)}) custom-call(bf16[16,128,128]{2,1,0:T(8,128)(2,1)S(1)} %get-tuple-element.65.gate_ref, bf16[4,128,896]{2,1,0:T(8,128)(2,1)S(1)} %get-tuple-element.55.wide_ref, bf16[16,8,16,256]{3,2,1,0:T(8,128)(2,1)S(1)} %get-tuple-element.56.source_ref, ...), custom_call_target="tpu_custom_call" | custom-call | flops 4000000000 | bytes 4718592 | tf_op jit(solution)/shard_map/pallas_call | solution.py:551
  34.6 1.6 %collective-permute-done.6.rest_2_ = bf16[3,80,128]{2,1,0:T(8,128)(2,1)S(1)} collective-permute-done((bf16[3,80,128]{2,1,0:T(8,128)(2,1)S(1)}, bf16[3,80,128]{2,1,0:T(8,128)(2,1)S(1)}, u32[]{:S(2)}, u32[]{:S(2)}) %collective-permute-start.6) | collective-permute-done | bytes 61472 | tf_op jit(solution)/shard_map/ppermute | solution.py:714
  36.5 0.6 %collective-permute-start.9 = (bf16[80,128]{1,0:T(8,128)(2,1)S(1)}, bf16[80,128]{1,0:T(8,128)(2,1)S(1)}, u32[]{:S(2)}, u32[]{:S(2)}) collective-permute-start(bf16[80,128]{1,0:T(8,128)(2,1)S(1)} %get-tuple-element.81.rest_0_), channel_id=1, source_target_pairs={{0,8},{4,12},{8,0},{12,4},{1,9},{5,13},{9,1},{13,5},{2,10},{6,14},... | collective-permute-start | bytes 61448 | tf_op jit(solution)/shard_map/ppermute | solution.py:727
  37.1 1.3 %collective-permute-start.8 = (bf16[80,128]{1,0:T(8,128)(2,1)S(1)}, bf16[80,128]{1,0:T(8,128)(2,1)S(1)}, u32[]{:S(2)}, u32[]{:S(2)}) collective-permute-start(bf16[80,128]{1,0:T(8,128)(2,1)S(1)} %get-tuple-element.81.rest_0_), channel_id=1, source_target_pairs={{0,4},{4,0},{8,12},{12,8},{1,5},{5,1},{9,13},{13,9},{2,6},{6,2},{1... | collective-permute-start | bytes 61448 | tf_op jit(solution)/shard_map/ppermute | solution.py:727
  38.4 1.6 %shard_map.137 = (bf16[16,128,256]{2,1,0:T(8,128)(2,1)}, bf16[16,128,256]{2,1,0:T(8,128)(2,1)}) custom-call(f32[8,128]{1,0:T(8,128)S(1)} %get-tuple-element.73.grad_ref, f32[16,128,256]{2,1,0:T(8,128)S(1)} %bitcast.16, f32[16,128,256]{2,1,0:T(8,128)S(1)} %get-tuple-element.75.edit_ref, bf16[8,128,256]{2,1,0:T(8,128)(2,1)S(1)} %collective-permute-done.11.across_ref, ...), custom_call_target="tpu_custom_call" | custom-call | flops 10000000 | bytes 5246976 | tf_op jit(solution)/shard_map/pallas_call | solution.py:551
  40.0 0.4 collective-permute-done.9.rest_2_
  40.4 0.7 %shard_map.138 = (f32[289,128]{1,0:T(8,128)}, f32[1,128]{1,0:T(1,128)}, f32[1,128]{1,0:T(1,128)}, f32[1,128]{1,0:T(1,128)}) custom-call(bf16[80,128]{1,0:T(8,128)(2,1)S(1)} %get-tuple-element.81.rest_0_, bf16[80,128]{1,0:T(8,128)(2,1)S(1)} %collective-permute-done.8.rest_1_, bf16[80,128]{1,0:T(8,128)(2,1)S(1)} %collective-permute-done.9.rest_2_, ...), custom_call_target="tpu_custom_call" | custom-call | flops 1000000 | bytes 82432 | tf_op jit(solution)/shard_map/pallas_call | solution.py:551
  (24 shorter events, 0.4 us)
Async XLA Ops:
  1.9 6.4 %collective-permute-start = (bf16[8,128,256]{2,1,0:T(8,128)(2,1)S(1)}, bf16[8,128,256]{2,1,0:T(8,128)(2,1)S(1)}, u32[]{:S(2)}, u32[]{:S(2)}) collective-permute-start(bf16[8,128,256]{2,1,0:T(8,128)(2,1)S(1)} %get-tuple-element.53), channel_id=1, source_target_pairs={{0,4},{4,0},{8,12},{12,8},{1,5},{5,1},{9,13},{13,9},{2,6},{6,2},{1... | collective-permute-start | bytes 1572872 | tf_op jit(solution)/shard_map/ppermute | solution.py:610
  2.4 9.7 %collective-permute-start.1 = (bf16[8,128,256]{2,1,0:T(8,128)(2,1)S(1)}, bf16[8,128,256]{2,1,0:T(8,128)(2,1)S(1)}, u32[]{:S(2)}, u32[]{:S(2)}) collective-permute-start(bf16[8,128,256]{2,1,0:T(8,128)(2,1)S(1)} %get-tuple-element.57), channel_id=1, source_target_pairs={{0,16},{4,8},{8,4},{12,28},{16,0},{20,24},{24,20},{28,12},{1,17},{... | collective-permute-start | bytes 1572872 | tf_op jit(solution)/shard_map/ppermute | solution.py:611
  6.8 1.5 %copy-start = (f32[128]{0:T(128)S(1)}, f32[128]{0:T(128)}, u32[]{:S(2)}) copy-start(f32[128]{0:T(128)} %param.12) | copy-start | bytes 1540
  6.8 1.5 %copy-start.1 = (f32[128]{0:T(128)S(1)}, f32[128]{0:T(128)}, u32[]{:S(2)}) copy-start(f32[128]{0:T(128)} %param.11) | copy-start | bytes 1540
  15.1 23.3 %collective-permute-start.12 = (bf16[8,128,256]{2,1,0:T(8,128)(2,1)S(1)}, bf16[8,128,256]{2,1,0:T(8,128)(2,1)S(1)}, u32[]{:S(2)}, u32[]{:S(2)}) collective-permute-start(bf16[8,128,256]{2,1,0:T(8,128)(2,1)S(1)} %shard_map.136), channel_id=1, source_target_pairs={{0,16},{4,8},{8,4},{12,28},{16,0},{20,24},{24,20},{28,12},{1,17},{... | collective-permute-start | bytes 1572872 | tf_op jit(solution)/shard_map/ppermute | solution.py:693
  17.2 21.2 %collective-permute-start.11 = (bf16[8,128,256]{2,1,0:T(8,128)(2,1)S(1)}, bf16[8,128,256]{2,1,0:T(8,128)(2,1)S(1)}, u32[]{:S(2)}, u32[]{:S(2)}) collective-permute-start(bf16[8,128,256]{2,1,0:T(8,128)(2,1)S(1)} %shard_map.131), channel_id=1, source_target_pairs={{0,4},{4,0},{8,12},{12,8},{1,5},{5,1},{9,13},{13,9},{2,6},{6,2},{1... | collective-permute-start | bytes 1572872 | tf_op jit(solution)/shard_map/ppermute | solution.py:676
  17.2 4.4 %collective-permute-start.2 = (bf16[3,80,128]{2,1,0:T(8,128)(2,1)S(1)}, bf16[3,80,128]{2,1,0:T(8,128)(2,1)S(1)}, u32[]{:S(2)}, u32[]{:S(2)}) collective-permute-start(bf16[3,80,128]{2,1,0:T(8,128)(2,1)S(1)} %get-tuple-element.62), channel_id=1, source_target_pairs={{0,12},{4,8},{8,4},{12,0},{1,13},{5,9},{9,5},{13,1},{2,14},{6,10},... | collective-permute-start | bytes 184328 | tf_op jit(solution)/shard_map/ppermute | solution.py:694
  17.6 9.1 %collective-permute-start.3 = (bf16[3,80,128]{2,1,0:T(8,128)(2,1)S(1)}, bf16[3,80,128]{2,1,0:T(8,128)(2,1)S(1)}, u32[]{:S(2)}, u32[]{:S(2)}) collective-permute-start(bf16[3,80,128]{2,1,0:T(8,128)(2,1)S(1)} %get-tuple-element.63), channel_id=1, source_target_pairs={{0,8},{4,12},{8,0},{12,4},{1,9},{5,13},{9,1},{13,5},{2,10},{6,14},... | collective-permute-start | bytes 184328 | tf_op jit(solution)/shard_map/ppermute | solution.py:694
  19.3 7.4 %collective-permute-start.4 = (bf16[3,80,128]{2,1,0:T(8,128)(2,1)S(1)}, bf16[3,80,128]{2,1,0:T(8,128)(2,1)S(1)}, u32[]{:S(2)}, u32[]{:S(2)}) collective-permute-start(bf16[3,80,128]{2,1,0:T(8,128)(2,1)S(1)} %get-tuple-element.64), channel_id=1, source_target_pairs={{0,4},{4,0},{8,12},{12,8},{1,5},{5,1},{9,13},{13,9},{2,6},{6,2},{1... | collective-permute-start | bytes 184328 | tf_op jit(solution)/shard_map/ppermute | solution.py:694
  26.7 9.5 %copy-start.2 = (s32[16]{0:T(128)S(1)}, s32[16]{0:T(128)}, u32[]{:S(2)}) copy-start(s32[16]{0:T(128)} %param.13) | copy-start | bytes 196
  26.8 9.5 %copy-start.3 = (s32[16]{0:T(128)S(1)}, s32[16]{0:T(128)}, u32[]{:S(2)}) copy-start(s32[16]{0:T(128)} %param.14) | copy-start | bytes 196
  26.8 9.4 %copy-start.4 = (s32[16]{0:T(128)S(1)}, s32[16]{0:T(128)}, u32[]{:S(2)}) copy-start(s32[16]{0:T(128)} %param.15) | copy-start | bytes 196
  26.8 7.8 %collective-permute-start.7 = (bf16[3,80,128]{2,1,0:T(8,128)(2,1)S(1)}, bf16[3,80,128]{2,1,0:T(8,128)(2,1)S(1)}, u32[]{:S(2)}, u32[]{:S(2)}) collective-permute-start(bf16[3,80,128]{2,1,0:T(8,128)(2,1)S(1)} %shard_map.133.rest_0_), channel_id=1, source_target_pairs={{0,3},{1,2},{2,1},{3,0},{4,7},{5,6},{6,5},{7,4},{8,11},{9,10},{10,... | collective-permute-start | bytes 184328 | tf_op jit(solution)/shard_map/ppermute | solution.py:714
  31.0 5.2 %collective-permute-start.6 = (bf16[3,80,128]{2,1,0:T(8,128)(2,1)S(1)}, bf16[3,80,128]{2,1,0:T(8,128)(2,1)S(1)}, u32[]{:S(2)}, u32[]{:S(2)}) collective-permute-start(bf16[3,80,128]{2,1,0:T(8,128)(2,1)S(1)} %shard_map.133.rest_0_), channel_id=1, source_target_pairs={{0,2},{1,3},{2,0},{3,1},{4,6},{5,7},{6,4},{7,5},{8,10},{9,11},{10,... | collective-permute-start | bytes 184328 | tf_op jit(solution)/shard_map/ppermute | solution.py:714
  31.0 5.2 %collective-permute-start.5 = (bf16[3,80,128]{2,1,0:T(8,128)(2,1)S(1)}, bf16[3,80,128]{2,1,0:T(8,128)(2,1)S(1)}, u32[]{:S(2)}, u32[]{:S(2)}) collective-permute-start(bf16[3,80,128]{2,1,0:T(8,128)(2,1)S(1)} %shard_map.133.rest_0_), channel_id=1, source_target_pairs={{0,1},{1,0},{2,3},{3,2},{4,5},{5,4},{6,7},{7,6},{8,9},{9,8},{10,11... | collective-permute-start | bytes 184328 | tf_op jit(solution)/shard_map/ppermute | solution.py:714
  36.4 3.5 %collective-permute-start.10 = (bf16[80,128]{1,0:T(8,128)(2,1)S(1)}, bf16[80,128]{1,0:T(8,128)(2,1)S(1)}, u32[]{:S(2)}, u32[]{:S(2)}) collective-permute-start(bf16[80,128]{1,0:T(8,128)(2,1)S(1)} %get-tuple-element.81.rest_0_), channel_id=1, source_target_pairs={{0,12},{4,8},{8,4},{12,0},{1,13},{5,9},{9,5},{13,1},{2,14},{6,10},... | collective-permute-start | bytes 61448 | tf_op jit(solution)/shard_map/ppermute | solution.py:727
  36.5 3.8 %collective-permute-start.9 = (bf16[80,128]{1,0:T(8,128)(2,1)S(1)}, bf16[80,128]{1,0:T(8,128)(2,1)S(1)}, u32[]{:S(2)}, u32[]{:S(2)}) collective-permute-start(bf16[80,128]{1,0:T(8,128)(2,1)S(1)} %get-tuple-element.81.rest_0_), channel_id=1, source_target_pairs={{0,8},{4,12},{8,0},{12,4},{1,9},{5,13},{9,1},{13,5},{2,10},{6,14},... | collective-permute-start | bytes 61448 | tf_op jit(solution)/shard_map/ppermute | solution.py:727
  37.1 3.3 %collective-permute-start.8 = (bf16[80,128]{1,0:T(8,128)(2,1)S(1)}, bf16[80,128]{1,0:T(8,128)(2,1)S(1)}, u32[]{:S(2)}, u32[]{:S(2)}) collective-permute-start(bf16[80,128]{1,0:T(8,128)(2,1)S(1)} %get-tuple-element.81.rest_0_), channel_id=1, source_target_pairs={{0,4},{4,0},{8,12},{12,8},{1,5},{5,1},{9,13},{13,9},{2,6},{6,2},{1... | collective-permute-start | bytes 61448 | tf_op jit(solution)/shard_map/ppermute | solution.py:727

commit v10 on v9

--- a/solution.py
+++ b/solution.py
@@ -690,8 +690,9 @@
         near_sums,
         near_total,
     )
-    from_beyond = lax.ppermute(rim_terms(1, gate), ("groups", "space"), to_beyond)
     came = [lax.ppermute(pieces[k], "space", around("space", k)) for k in reversed(range(1, space))]
+    far_terms, *came = lax.optimization_barrier((rim_terms(1, gate), *came))
+    from_beyond = lax.ppermute(far_terms, ("groups", "space"), to_beyond)
     (quarter,) = call(
         merge_kernel, (shape((3, share, kout), BF16),), [], 10**4, pieces[0], *came
     )

time: 41.2 us -> 35.9 us (0.87)
  waiting for transfers between devices: 10.4 us -> 5.37 us
    ppermute x3, waiting for transfers between devices: 7.39 us -> 2.53 us  [local(): lax.ppermute(pieces[k], 'space', around('space', k))]
    ppermute x1, starting transfers between devices: 0.01 us -> 0.43 us  [local(): from_across = lax.ppermute(terms, 'space', to_across)]
  transfers between devices with their start and end apart: 13 -> 13, of which waited for: 5 -> 5; matrix products, arithmetic and copies ran while one was open for 0% -> 0% of each run, Pallas kernels for 26% -> 33%
where the time goes in v10:
time: 35.9 us; the launch traced here: 35.7 us
  Pallas kernels  15.7 us (44%)
  starting transfers between devices  13.8 us (38%)
  waiting for transfers between devices  5.37 us (15%)
  between operations  0.81 us (2%)
    pallas_call x12, Pallas kernels, call(): pl.pallas_call(kernel, out_shape=outs, in_specs=[pl.BlockSpec(memory_spac...  15.7 us
    ppermute x3, starting transfers between devices, local(): lax.ppermute(quarter, 'pair', around('pair', k))  4.45 us
    ppermute x1, starting transfers between devices, local(): beyond = lax.ppermute(beyond, ('groups', 'space'), to_beyond)  2.56 us
    ppermute x3, waiting for transfers between devices, local(): lax.ppermute(pieces[k], 'space', around('space', k))  2.53 us
    ppermute x1, starting transfers between devices, local(): from_beyond = lax.ppermute(far_terms, ('groups', 'space'), to_beyond)  2.02 us
    ppermute x3, starting transfers between devices, local(): lax.ppermute(pieces[k], 'space', around('space', k))  1.93 us
    ppermute x3, starting transfers between devices, local(): lax.ppermute(total, 'space', around('space', k))  1.92 us
    ppermute x3, waiting for transfers between devices, local(): lax.ppermute(quarter, 'pair', around('pair', k))  1.43 us
  transfers between devices with their start and end apart: 13, of which 5 were waited for; matrix products, arithmetic and copies ran while one was open for 0% of the time, Pallas kernels for 33%

profile of v10, /device:TPU:0, one launch (start us, length us, event | category | flops | bytes accessed | tf_op | source)
XLA Modules:
  0.0 35.7 jit_solution(7505575472707836632)
XLA Ops:
  0.6 1.2 %shard_map.129 = (bf16[8,128,256]{2,1,0:T(8,128)(2,1)S(1)}, bf16[8,128,256]{2,1,0:T(8,128)(2,1)S(1)}) custom-call(bf16[16,128,256]{2,1,0:T(8,128)(2,1)} %bitcast.25), custom_call_target="tpu_custom_call" | custom-call | flops 10000 | bytes 1048576 | tf_op jit(solution)/shard_map/pallas_call | solution.py:551
  1.9 0.5 %collective-permute-start = (bf16[8,128,256]{2,1,0:T(8,128)(2,1)S(1)}, bf16[8,128,256]{2,1,0:T(8,128)(2,1)S(1)}, u32[]{:S(2)}, u32[]{:S(2)}) collective-permute-start(bf16[8,128,256]{2,1,0:T(8,128)(2,1)S(1)} %get-tuple-element.57), channel_id=1, source_target_pairs={{0,4},{4,0},{8,12},{12,8},{1,5},{5,1},{9,13},{13,9},{2,6},{6,2},{1... | collective-permute-start | bytes 1572872 | tf_op jit(solution)/shard_map/ppermute | solution.py:610
  2.4 2.6 %collective-permute-start.1 = (bf16[8,128,256]{2,1,0:T(8,128)(2,1)S(1)}, bf16[8,128,256]{2,1,0:T(8,128)(2,1)S(1)}, u32[]{:S(2)}, u32[]{:S(2)}) collective-permute-start(bf16[8,128,256]{2,1,0:T(8,128)(2,1)S(1)} %get-tuple-element.61), channel_id=1, source_target_pairs={{0,16},{4,8},{8,4},{12,28},{16,0},{20,24},{24,20},{28,12},{1,17},{... | collective-permute-start | bytes 1572872 | tf_op jit(solution)/shard_map/ppermute | solution.py:611
  5.0 1.8 %shard_map.127 = (bf16[16,8,16,256]{3,2,1,0:T(8,128)(2,1)S(1)}, bf16[16,144,256]{2,1,0:T(8,128)(2,1)S(1)}, bf16[16,8,16,256]{3,2,1,0:T(8,128)(2,1)S(1)}, bf16[4,...) custom-call(bf16[16,8,16,256]{3,2,1,0:T(8,128)(2,1)} %bitcast.27, bf16[16,128,256]{2,1,0:T(8,128)(2,1)} %bitcast.26, ...), custom_call_target="tpu_custom_call" | custom-call | flops 10000 | bytes 2171136 | tf_op jit(solution)/shard_map/pallas_call | solution.py:551
  6.8 1.5 %shard_map.128 = (bf16[16,8,16,512]{3,2,1,0:T(8,128)(2,1)S(1)}, f32[16,128,128]{2,1,0:T(8,128)S(1)}) custom-call(bf16[16,8,16,256]{3,2,1,0:T(8,128)(2,1)S(1)} %get-tuple-element.52.turned_ref, bf16[16,144,256]{2,1,0:T(8,128)(2,1)S(1)} %get-tuple-element.53.pad.own_pad, bf16[4,896,128]{2,1,0:T(8,128)(2,1)S(1)} %get-tuple-element.54.tall_ref), custom_call_target="tpu_custom_call" | custom-call | flops 2000000000 | bytes 3145728 | tf_op jit(solution)/shard_map/pallas_call | solution.py:551
  8.3 2.0 %shard_map.130 = (bf16[8,128,128]{2,1,0:T(8,128)(2,1)S(1)}, f32[2,128]{1,0:T(2,128)S(1)}, f32[256,640]{1,0:T(8,128)S(1)}) custom-call(bf16[16,8,16,256]{3,2,1,0:T(8,128)(2,1)S(1)} %get-tuple-element.52.turned_ref, bf16[16,8,16,512]{3,2,1,0:T(8,128)(2,1)S(1)} %get-tuple-element.55.corr_ref, f32[16,128,128]{2,1,0:T(8,128)S(1)} %get-tuple-element.56.own_ref, ...), custom_call_target="tpu_custom_call" | custom-call | flops 1000000000 | bytes 5637120 | tf_op jit(solution)/shard_map/pallas_call | solution.py:551
  10.3 0.8 %shard_map.131 = bf16[8,128,256]{2,1,0:T(8,128)(2,1)S(1)} custom-call(bf16[8,128,128]{2,1,0:T(8,128)(2,1)S(1)} %get-tuple-element.58.gate_ref.near_gate_ref, bf16[4,128,896]{2,1,0:T(8,128)(2,1)S(1)} %get-tuple-element.59.wide_ref, bf16[16,8,16,256]{3,2,1,0:T(8,128)(2,1)S(1)} %get-tuple-element.60.source_ref), custom_call_target="tpu_custom_call" | custom-call | flops 1000000000 | bytes 2228224 | tf_op jit(solution)/shard_map/pallas_call | solution.py:551
  11.1 1.0 %collective-permute-done.1.halo_ref.beyond_ref = bf16[8,128,256]{2,1,0:T(8,128)(2,1)S(1)} collective-permute-done((bf16[8,128,256]{2,1,0:T(8,128)(2,1)S(1)}, bf16[8,128,256]{2,1,0:T(8,128)(2,1)S(1)}, u32[]{:S(2)}, u32[]{:S(2)}) %collective-permute-start.1) | collective-permute-done | bytes 524320 | tf_op jit(solution)/shard_map/ppermute | solution.py:611
  12.1 2.1 %shard_map.132 = (bf16[16,128,128]{2,1,0:T(8,128)(2,1)S(1)}, bf16[3,80,128]{2,1,0:T(8,128)(2,1)S(1)}, bf16[3,80,128]{2,1,0:T(8,128)(2,1)S(1)}, bf16[3,80,128]{2,1,0:T(8,128)(2,1)S(1)}, bf16[3,80,128]{2,1,0:T(8,128)(2,1)S(1)}) custom-call(bf16[16,8,16,256]{3,2,1,0:T(8,128)(2,1)S(1)} %get-tuple-element.52.turned_ref, ...), custom_call_target="tpu_custom_call" | custom-call | flops 2000000000 | bytes 6555648 | tf_op jit(solution)/shard_map/pallas_call | solution.py:551
  14.3 1.3 %collective-permute-start.2 = (bf16[3,80,128]{2,1,0:T(8,128)(2,1)S(1)}, bf16[3,80,128]{2,1,0:T(8,128)(2,1)S(1)}, u32[]{:S(2)}, u32[]{:S(2)}) collective-permute-start(bf16[3,80,128]{2,1,0:T(8,128)(2,1)S(1)} %get-tuple-element.67), channel_id=1, source_target_pairs={{0,12},{4,8},{8,4},{12,0},{1,13},{5,9},{9,5},{13,1},{2,14},{6,10},... | collective-permute-start | bytes 184328 | tf_op jit(solution)/shard_map/ppermute | solution.py:693
  15.5 0.6 %collective-permute-start.3 = (bf16[3,80,128]{2,1,0:T(8,128)(2,1)S(1)}, bf16[3,80,128]{2,1,0:T(8,128)(2,1)S(1)}, u32[]{:S(2)}, u32[]{:S(2)}) collective-permute-start(bf16[3,80,128]{2,1,0:T(8,128)(2,1)S(1)} %get-tuple-element.68), channel_id=1, source_target_pairs={{0,8},{4,12},{8,0},{12,4},{1,9},{5,13},{9,1},{13,5},{2,10},{6,14},... | collective-permute-start | bytes 184328 | tf_op jit(solution)/shard_map/ppermute | solution.py:693
  16.2 0.4 %collective-permute-start.11 = (bf16[8,128,256]{2,1,0:T(8,128)(2,1)S(1)}, bf16[8,128,256]{2,1,0:T(8,128)(2,1)S(1)}, u32[]{:S(2)}, u32[]{:S(2)}) collective-permute-start(bf16[8,128,256]{2,1,0:T(8,128)(2,1)S(1)} %shard_map.131), channel_id=1, source_target_pairs={{0,4},{4,0},{8,12},{12,8},{1,5},{5,1},{9,13},{13,9},{2,6},{6,2},{1... | collective-permute-start | bytes 1572872 | tf_op jit(solution)/shard_map/ppermute | solution.py:676
  16.6 0.8 %shard_map.133 = bf16[8,128,256]{2,1,0:T(8,128)(2,1)S(1)} custom-call(bf16[16,128,128]{2,1,0:T(8,128)(2,1)S(1)} %get-tuple-element.66.gate_ref, bf16[4,128,896]{2,1,0:T(8,128)(2,1)S(1)} %get-tuple-element.59.wide_ref, bf16[16,8,16,256]{3,2,1,0:T(8,128)(2,1)S(1)} %get-tuple-element.60.source_ref), custom_call_target="tpu_custom_call" | custom-call | flops 1000000000 | bytes 2490368 | tf_op jit(solution)/shard_map/pallas_call | solution.py:551
  17.4 0.9 %collective-permute-done.2.refs_1_ = bf16[3,80,128]{2,1,0:T(8,128)(2,1)S(1)} collective-permute-done((bf16[3,80,128]{2,1,0:T(8,128)(2,1)S(1)}, bf16[3,80,128]{2,1,0:T(8,128)(2,1)S(1)}, u32[]{:S(2)}, u32[]{:S(2)}) %collective-permute-start.2) | collective-permute-done | bytes 61472 | tf_op jit(solution)/shard_map/ppermute | solution.py:693
  18.3 1.6 %collective-permute-done.3.refs_2_ = bf16[3,80,128]{2,1,0:T(8,128)(2,1)S(1)} collective-permute-done((bf16[3,80,128]{2,1,0:T(8,128)(2,1)S(1)}, bf16[3,80,128]{2,1,0:T(8,128)(2,1)S(1)}, u32[]{:S(2)}, u32[]{:S(2)}) %collective-permute-start.3) | collective-permute-done | bytes 61472 | tf_op jit(solution)/shard_map/ppermute | solution.py:693
  20.0 2.0 %collective-permute-start.12 = (bf16[8,128,256]{2,1,0:T(8,128)(2,1)S(1)}, bf16[8,128,256]{2,1,0:T(8,128)(2,1)S(1)}, u32[]{:S(2)}, u32[]{:S(2)}) collective-permute-start(bf16[8,128,256]{2,1,0:T(8,128)(2,1)S(1)} %shard_map.133), channel_id=1, source_target_pairs={{0,16},{4,8},{8,4},{12,28},{16,0},{20,24},{24,20},{28,12},{1,17},{... | collective-permute-start | bytes 1572872 | tf_op jit(solution)/shard_map/ppermute | solution.py:695
  22.1 3.7 %collective-permute-start.7 = (bf16[3,80,128]{2,1,0:T(8,128)(2,1)S(1)}, bf16[3,80,128]{2,1,0:T(8,128)(2,1)S(1)}, u32[]{:S(2)}, u32[]{:S(2)}) collective-permute-start(bf16[3,80,128]{2,1,0:T(8,128)(2,1)S(1)} %shard_map.134.rest_0_), channel_id=1, source_target_pairs={{0,3},{1,2},{2,1},{3,0},{4,7},{5,6},{6,5},{7,4},{8,11},{9,10},{10,... | collective-permute-start | bytes 184328 | tf_op jit(solution)/shard_map/ppermute | solution.py:715
  25.7 0.8 %collective-permute-start.5 = (bf16[3,80,128]{2,1,0:T(8,128)(2,1)S(1)}, bf16[3,80,128]{2,1,0:T(8,128)(2,1)S(1)}, u32[]{:S(2)}, u32[]{:S(2)}) collective-permute-start(bf16[3,80,128]{2,1,0:T(8,128)(2,1)S(1)} %shard_map.134.rest_0_), channel_id=1, source_target_pairs={{0,1},{1,0},{2,3},{3,2},{4,5},{5,4},{6,7},{7,6},{8,9},{9,8},{10,11... | collective-permute-start | bytes 184328 | tf_op jit(solution)/shard_map/ppermute | solution.py:715
  26.5 2.9 %shard_map.135 = (f32[16,8,16,256]{3,2,1,0:T(8,128)S(1)}, f32[16,128,256]{2,1,0:T(8,128)S(1)}) custom-call(bf16[16,128,128]{2,1,0:T(8,128)(2,1)S(1)} %get-tuple-element.66.gate_ref, bf16[4,128,896]{2,1,0:T(8,128)(2,1)S(1)} %get-tuple-element.59.wide_ref, bf16[16,8,16,256]{3,2,1,0:T(8,128)(2,1)S(1)} %get-tuple-element.60.source_ref, ...), custom_call_target="tpu_custom_call" | custom-call | flops 4000000000 | bytes 4718592 | tf_op jit(solution)/shard_map/pallas_call | solution.py:551
  29.5 1.4 %collective-permute-done.6.rest_2_ = bf16[3,80,128]{2,1,0:T(8,128)(2,1)S(1)} collective-permute-done((bf16[3,80,128]{2,1,0:T(8,128)(2,1)S(1)}, bf16[3,80,128]{2,1,0:T(8,128)(2,1)S(1)}, u32[]{:S(2)}, u32[]{:S(2)}) %collective-permute-start.6) | collective-permute-done | bytes 61472 | tf_op jit(solution)/shard_map/ppermute | solution.py:715
  31.2 0.7 %collective-permute-start.9 = (bf16[80,128]{1,0:T(8,128)(2,1)S(1)}, bf16[80,128]{1,0:T(8,128)(2,1)S(1)}, u32[]{:S(2)}, u32[]{:S(2)}) collective-permute-start(bf16[80,128]{1,0:T(8,128)(2,1)S(1)} %get-tuple-element.89.rest_0_), channel_id=1, source_target_pairs={{0,8},{4,12},{8,0},{12,4},{1,9},{5,13},{9,1},{13,5},{2,10},{6,14},... | collective-permute-start | bytes 61448 | tf_op jit(solution)/shard_map/ppermute | solution.py:728
  31.9 1.2 %collective-permute-start.8 = (bf16[80,128]{1,0:T(8,128)(2,1)S(1)}, bf16[80,128]{1,0:T(8,128)(2,1)S(1)}, u32[]{:S(2)}, u32[]{:S(2)}) collective-permute-start(bf16[80,128]{1,0:T(8,128)(2,1)S(1)} %get-tuple-element.89.rest_0_), channel_id=1, source_target_pairs={{0,4},{4,0},{8,12},{12,8},{1,5},{5,1},{9,13},{13,9},{2,6},{6,2},{1... | collective-permute-start | bytes 61448 | tf_op jit(solution)/shard_map/ppermute | solution.py:728
  33.0 1.6 %shard_map.137 = (bf16[16,128,256]{2,1,0:T(8,128)(2,1)}, bf16[16,128,256]{2,1,0:T(8,128)(2,1)}) custom-call(f32[8,128]{1,0:T(8,128)S(1)} %get-tuple-element.80.grad_ref, f32[16,128,256]{2,1,0:T(8,128)S(1)} %bitcast.16, f32[16,128,256]{2,1,0:T(8,128)S(1)} %get-tuple-element.82.edit_ref, bf16[8,128,256]{2,1,0:T(8,128)(2,1)S(1)} %collective-permute-done.11.across_ref, ...), custom_call_target="tpu_custom_call" | custom-call | flops 10000000 | bytes 5246976 | tf_op jit(solution)/shard_map/pallas_call | solution.py:551
  35.0 0.7 %shard_map.138 = (f32[289,128]{1,0:T(8,128)}, f32[1,128]{1,0:T(1,128)}, f32[1,128]{1,0:T(1,128)}, f32[1,128]{1,0:T(1,128)}) custom-call(bf16[80,128]{1,0:T(8,128)(2,1)S(1)} %get-tuple-element.89.rest_0_, bf16[80,128]{1,0:T(8,128)(2,1)S(1)} %collective-permute-done.8.rest_1_, bf16[80,128]{1,0:T(8,128)(2,1)S(1)} %collective-permute-done.9.rest_2_, ...), custom_call_target="tpu_custom_call" | custom-call | flops 1000000 | bytes 82432 | tf_op jit(solution)/shard_map/pallas_call | solution.py:551
  (24 shorter events, 0.8 us)
Async XLA Ops:
  1.9 6.4 %collective-permute-start = (bf16[8,128,256]{2,1,0:T(8,128)(2,1)S(1)}, bf16[8,128,256]{2,1,0:T(8,128)(2,1)S(1)}, u32[]{:S(2)}, u32[]{:S(2)}) collective-permute-start(bf16[8,128,256]{2,1,0:T(8,128)(2,1)S(1)} %get-tuple-element.57), channel_id=1, source_target_pairs={{0,4},{4,0},{8,12},{12,8},{1,5},{5,1},{9,13},{13,9},{2,6},{6,2},{1... | collective-permute-start | bytes 1572872 | tf_op jit(solution)/shard_map/ppermute | solution.py:610
  2.4 9.7 %collective-permute-start.1 = (bf16[8,128,256]{2,1,0:T(8,128)(2,1)S(1)}, bf16[8,128,256]{2,1,0:T(8,128)(2,1)S(1)}, u32[]{:S(2)}, u32[]{:S(2)}) collective-permute-start(bf16[8,128,256]{2,1,0:T(8,128)(2,1)S(1)} %get-tuple-element.61), channel_id=1, source_target_pairs={{0,16},{4,8},{8,4},{12,28},{16,0},{20,24},{24,20},{28,12},{1,17},{... | collective-permute-start | bytes 1572872 | tf_op jit(solution)/shard_map/ppermute | solution.py:611
  6.8 1.5 %copy-start = (f32[128]{0:T(128)S(1)}, f32[128]{0:T(128)}, u32[]{:S(2)}) copy-start(f32[128]{0:T(128)} %param.12) | copy-start | bytes 1540
  6.8 1.5 %copy-start.1 = (f32[128]{0:T(128)S(1)}, f32[128]{0:T(128)}, u32[]{:S(2)}) copy-start(f32[128]{0:T(128)} %param.11) | copy-start | bytes 1540
  14.3 4.1 %collective-permute-start.2 = (bf16[3,80,128]{2,1,0:T(8,128)(2,1)S(1)}, bf16[3,80,128]{2,1,0:T(8,128)(2,1)S(1)}, u32[]{:S(2)}, u32[]{:S(2)}) collective-permute-start(bf16[3,80,128]{2,1,0:T(8,128)(2,1)S(1)} %get-tuple-element.67), channel_id=1, source_target_pairs={{0,12},{4,8},{8,4},{12,0},{1,13},{5,9},{9,5},{13,1},{2,14},{6,10},... | collective-permute-start | bytes 184328 | tf_op jit(solution)/shard_map/ppermute | solution.py:693
  15.5 4.4 %collective-permute-start.3 = (bf16[3,80,128]{2,1,0:T(8,128)(2,1)S(1)}, bf16[3,80,128]{2,1,0:T(8,128)(2,1)S(1)}, u32[]{:S(2)}, u32[]{:S(2)}) collective-permute-start(bf16[3,80,128]{2,1,0:T(8,128)(2,1)S(1)} %get-tuple-element.68), channel_id=1, source_target_pairs={{0,8},{4,12},{8,0},{12,4},{1,9},{5,13},{9,1},{13,5},{2,10},{6,14},... | collective-permute-start | bytes 184328 | tf_op jit(solution)/shard_map/ppermute | solution.py:693
  16.1 3.8 %collective-permute-start.4 = (bf16[3,80,128]{2,1,0:T(8,128)(2,1)S(1)}, bf16[3,80,128]{2,1,0:T(8,128)(2,1)S(1)}, u32[]{:S(2)}, u32[]{:S(2)}) collective-permute-start(bf16[3,80,128]{2,1,0:T(8,128)(2,1)S(1)} %get-tuple-element.69), channel_id=1, source_target_pairs={{0,4},{4,0},{8,12},{12,8},{1,5},{5,1},{9,13},{13,9},{2,6},{6,2},{1... | collective-permute-start | bytes 184328 | tf_op jit(solution)/shard_map/ppermute | solution.py:693
  16.2 16.9 %collective-permute-start.11 = (bf16[8,128,256]{2,1,0:T(8,128)(2,1)S(1)}, bf16[8,128,256]{2,1,0:T(8,128)(2,1)S(1)}, u32[]{:S(2)}, u32[]{:S(2)}) collective-permute-start(bf16[8,128,256]{2,1,0:T(8,128)(2,1)S(1)} %shard_map.131), channel_id=1, source_target_pairs={{0,4},{4,0},{8,12},{12,8},{1,5},{5,1},{9,13},{13,9},{2,6},{6,2},{1... | collective-permute-start | bytes 1572872 | tf_op jit(solution)/shard_map/ppermute | solution.py:676
  20.0 13.1 %collective-permute-start.12 = (bf16[8,128,256]{2,1,0:T(8,128)(2,1)S(1)}, bf16[8,128,256]{2,1,0:T(8,128)(2,1)S(1)}, u32[]{:S(2)}, u32[]{:S(2)}) collective-permute-start(bf16[8,128,256]{2,1,0:T(8,128)(2,1)S(1)} %shard_map.133), channel_id=1, source_target_pairs={{0,16},{4,8},{8,4},{12,28},{16,0},{20,24},{24,20},{28,12},{1,17},{... | collective-permute-start | bytes 1572872 | tf_op jit(solution)/shard_map/ppermute | solution.py:695
  22.0 8.9 %copy-start.2 = (s32[16]{0:T(128)S(1)}, s32[16]{0:T(128)}, u32[]{:S(2)}) copy-start(s32[16]{0:T(128)} %param.13) | copy-start | bytes 196
  22.0 8.9 %copy-start.3 = (s32[16]{0:T(128)S(1)}, s32[16]{0:T(128)}, u32[]{:S(2)}) copy-start(s32[16]{0:T(128)} %param.14) | copy-start | bytes 196
  22.0 8.9 %copy-start.4 = (s32[16]{0:T(128)S(1)}, s32[16]{0:T(128)}, u32[]{:S(2)}) copy-start(s32[16]{0:T(128)} %param.15) | copy-start | bytes 196
  22.1 7.4 %collective-permute-start.7 = (bf16[3,80,128]{2,1,0:T(8,128)(2,1)S(1)}, bf16[3,80,128]{2,1,0:T(8,128)(2,1)S(1)}, u32[]{:S(2)}, u32[]{:S(2)}) collective-permute-start(bf16[3,80,128]{2,1,0:T(8,128)(2,1)S(1)} %shard_map.134.rest_0_), channel_id=1, source_target_pairs={{0,3},{1,2},{2,1},{3,0},{4,7},{5,6},{6,5},{7,4},{8,11},{9,10},{10,... | collective-permute-start | bytes 184328 | tf_op jit(solution)/shard_map/ppermute | solution.py:715
  25.7 5.2 %collective-permute-start.6 = (bf16[3,80,128]{2,1,0:T(8,128)(2,1)S(1)}, bf16[3,80,128]{2,1,0:T(8,128)(2,1)S(1)}, u32[]{:S(2)}, u32[]{:S(2)}) collective-permute-start(bf16[3,80,128]{2,1,0:T(8,128)(2,1)S(1)} %shard_map.134.rest_0_), channel_id=1, source_target_pairs={{0,2},{1,3},{2,0},{3,1},{4,6},{5,7},{6,4},{7,5},{8,10},{9,11},{10,... | collective-permute-start | bytes 184328 | tf_op jit(solution)/shard_map/ppermute | solution.py:715
  25.7 5.2 %collective-permute-start.5 = (bf16[3,80,128]{2,1,0:T(8,128)(2,1)S(1)}, bf16[3,80,128]{2,1,0:T(8,128)(2,1)S(1)}, u32[]{:S(2)}, u32[]{:S(2)}) collective-permute-start(bf16[3,80,128]{2,1,0:T(8,128)(2,1)S(1)} %shard_map.134.rest_0_), channel_id=1, source_target_pairs={{0,1},{1,0},{2,3},{3,2},{4,5},{5,4},{6,7},{7,6},{8,9},{9,8},{10,11... | collective-permute-start | bytes 184328 | tf_op jit(solution)/shard_map/ppermute | solution.py:715
  31.1 3.5 %collective-permute-start.10 = (bf16[80,128]{1,0:T(8,128)(2,1)S(1)}, bf16[80,128]{1,0:T(8,128)(2,1)S(1)}, u32[]{:S(2)}, u32[]{:S(2)}) collective-permute-start(bf16[80,128]{1,0:T(8,128)(2,1)S(1)} %get-tuple-element.89.rest_0_), channel_id=1, source_target_pairs={{0,12},{4,8},{8,4},{12,0},{1,13},{5,9},{9,5},{13,1},{2,14},{6,10},... | collective-permute-start | bytes 61448 | tf_op jit(solution)/shard_map/ppermute | solution.py:728
  31.2 3.8 %collective-permute-start.9 = (bf16[80,128]{1,0:T(8,128)(2,1)S(1)}, bf16[80,128]{1,0:T(8,128)(2,1)S(1)}, u32[]{:S(2)}, u32[]{:S(2)}) collective-permute-start(bf16[80,128]{1,0:T(8,128)(2,1)S(1)} %get-tuple-element.89.rest_0_), channel_id=1, source_target_pairs={{0,8},{4,12},{8,0},{12,4},{1,9},{5,13},{9,1},{13,5},{2,10},{6,14},... | collective-permute-start | bytes 61448 | tf_op jit(solution)/shard_map/ppermute | solution.py:728
  31.9 3.2 %collective-permute-start.8 = (bf16[80,128]{1,0:T(8,128)(2,1)S(1)}, bf16[80,128]{1,0:T(8,128)(2,1)S(1)}, u32[]{:S(2)}, u32[]{:S(2)}) collective-permute-start(bf16[80,128]{1,0:T(8,128)(2,1)S(1)} %get-tuple-element.89.rest_0_), channel_id=1, source_target_pairs={{0,4},{4,0},{8,12},{12,8},{1,5},{5,1},{9,13},{13,9},{2,6},{6,2},{1... | collective-permute-start | bytes 61448 | tf_op jit(solution)/shard_map/ppermute | solution.py:728
